TPU v7x, 32 devices: a whole 2x2x4 slice. The times are simulated.
32 devices in a mesh: groups: 2 (over y), ctx: 4 (over z), tp: 4 (over x, core).
Axes of the slice: x: 2, y: 2, z: 4, core: 2. Of those that a mesh axis runs over, the one named last changes fastest.
Arguments:
- hidden: bfloat16 [1024, 8192], P(('groups', 'ctx'), 'tp'), parts along dimension 0, may hold values from -6 to 6
- base_query_rows: bfloat16 [1024, 8192], P(('groups', 'ctx'), 'tp'), parts along dimension 0, may hold values from -60 to 60
- base_key_rows: bfloat16 [1024, 1024], P(('groups', 'ctx'), 'tp'), parts along dimension 0, may hold values from -60 to 60
- base_value_rows: bfloat16 [1024, 1024], P(('groups', 'ctx'), 'tp'), parts along dimension 0, may hold values from -6 to 6
- stored_block_order: int32 [16], P('groups'), parts along dimension 0, may hold values from 0 to 7, each once
- version: int32 [8], P('groups'), parts along dimension 0, may hold values from 0 to 3
- publisher: int32 [2], P('groups'), parts along dimension 0, may hold values from 0 to 3
- adapter_down_weight: bfloat16 [4, 4, 192, 8192], P('ctx', None, None, 'tp'), may hold values from -0.0625 to 0.0625
- adapter_up_query: bfloat16 [4, 4, 64, 8192], P('ctx', None, None, 'tp'), may hold values from -0.75 to 0.75
- adapter_up_key_value: bfloat16 [4, 4, 2, 64, 1024], P('ctx', None, None, None, 'tp'), may hold values from -0.75 to 0.75
- output_down_weight: bfloat16 [4, 4, 64, 8192], P('ctx', None, None, 'tp'), may hold values from -0.1875 to 0.1875
- output_up_weight: bfloat16 [4, 4, 64, 8192], P('ctx', None, None, 'tp'), may hold values from -0.75 to 0.75
Outputs:
- attended: bfloat16 [1024, 8192], P(('groups', 'ctx'), 'tp'), parts along dimension 0
- adapted: bfloat16 [1024, 8192], P(('groups', 'ctx'), 'tp'), parts along dimension 0
There are 2 independent parts, one for each index of `groups`. A program takes and returns all parts, laid end to end along the dimension named above; an argument that names none is the same for every part. Nothing has to cross between parts.
Inputs may be any that keep to these rules, and one draw needn't show every extreme that they name: `stored_block_order`: each half-block of the prompt is stored exactly once.
All inputs are finite; a program needn't handle non-finite values.
Results may differ from a plain program's by a relative error of at most 0.015.
The roundings to bfloat16 on the way count: a program that leaves them out, or rounds other values in their place, can miss the bound.
Values may be sent and summed in bfloat16 or wider, within the bound.
No kernel may reach another device: no remote copies, remote signals or barrier semaphores. Data moves between devices by JAX's collectives and lax.ppermute only.
A program may use at most 64 MiB of HBM per device.

v0:
```python
import functools

import jax
import jax.numpy as jnp
from jax import lax
from jax.experimental import pallas as pl
from jax.experimental.pallas import tpu as pltpu
from jax.sharding import PartitionSpec as P


HEAD_SIZE = 128
ADAPTER_RANK = 64
NEG_BIG = -1e30
CHUNK_ROWS = 32
LAG = 2
PIECES = 2
KERNEL_VMEM = 8 << 20


def after(value, *earlier):
    return lax.optimization_barrier((value,) + earlier)[0]


def ring_order(count):
    return [0] + list(range(1, count, 2)) + list(range(2, count, 2))[::-1]


def ring_place(index, count):
    table = [0] * count
    for place, member in enumerate(ring_order(count)):
        table[member] = place
    place = jnp.int32(0)
    for member in range(count):
        place = jnp.where(index == member, table[member], place)
    return place


def ring_member(place, count):
    member = jnp.int32(0)
    for at, who in enumerate(ring_order(count)):
        member = jnp.where(place == at, who, member)
    return member


def ring_pairs(count, back=False):
    order = ring_order(count)
    pairs = [(order[i], order[(i + 1) % count]) for i in range(count)]
    return [(b, a) for a, b in pairs] if back else pairs


def doubling_sums(value, axis, wire):
    count = lax.axis_size(axis)
    if count & (count - 1):
        return [lax.psum(value, axis)]
    sums = []
    step = 1
    while step < count:
        pairs = [(i, i ^ step) for i in range(count)]
        sent = value.astype(wire)
        other = lax.ppermute(sent, axis, pairs)
        value = sent.astype(jnp.float32) + other.astype(jnp.float32)
        sums.append(value)
        step *= 2
    return sums


def rotation_tables(token_index_list):
    half_dim = HEAD_SIZE // 2
    frequency = 500000.0 ** (-(jnp.arange(half_dim, dtype=jnp.float32) * 2.0) / HEAD_SIZE)
    angles = token_index_list.astype(jnp.float32)[:, None] * frequency[None, :]
    cosine, sine = jnp.cos(angles), jnp.sin(angles)
    return jnp.concatenate([cosine, cosine, -sine, sine], axis=1)


def rotate(values, tables):
    swapped = pltpu.roll(values, HEAD_SIZE // 2, axis=1)
    return values * tables[:, :HEAD_SIZE] + swapped * tables[:, HEAD_SIZE:]


CONTRACT_LAST = (((1,), (1,)), ((), ()))
VMEM = pl.BlockSpec(memory_space=pltpu.VMEM)
SMEM = pl.BlockSpec(memory_space=pltpu.SMEM)


def chunk_call(kernel, behind, candidates, chunks, operands, out_shape):
    names = sorted(chunks)
    rows, width = chunks[names[0]].shape
    number = len(candidates[0])

    def body(behind_ref, *refs):
        chunk_refs = dict(zip(names, refs))
        weight_ref = refs[-1]
        for distance, held in enumerate(candidates):

            @pl.when(behind_ref[0] == distance)
            def _(held=held):
                for i, name in enumerate(held):
                    weight_ref[i * rows : (i + 1) * rows, :] = chunk_refs[name][...]

        kernel(weight_ref, *refs[len(names) : -1])

    return pl.pallas_call(
        body,
        out_shape=pltpu.VMEM(out_shape.shape, out_shape.dtype),
        in_specs=[SMEM] + [VMEM] * (len(names) + len(operands)),
        out_specs=VMEM,
        scratch_shapes=[pltpu.VMEM((number * rows, width), jnp.bfloat16)],
        compiler_params=pltpu.CompilerParams(vmem_limit_bytes=KERNEL_VMEM),
    )(
        behind,
        *[
            pltpu.with_memory_space_constraint(x, pltpu.VMEM)
            for x in [chunks[name] for name in names] + operands
        ],
    )


def low_kernel(weight_ref, *refs):
    out_ref = refs[-1]
    total, lane = None, 0
    for rows_ref in refs[:-1]:
        ends = lane + rows_ref.shape[1]
        part = lax.dot_general(
            rows_ref[...],
            weight_ref[:, lane:ends],
            CONTRACT_LAST,
            preferred_element_type=jnp.float32,
        )
        total = part if total is None else total + part
        lane = ends
    out_ref[...] = total


def up_kernel(weight_ref, low_ref, out_ref):
    out_ref[...] = jnp.dot(
        low_ref[...].astype(jnp.bfloat16), weight_ref[...], preferred_element_type=jnp.float32
    ).astype(out_ref.dtype)


def pair_kernel(weight_ref, low_ref, keys_ref, values_ref, tables_ref, out_ref):
    width = keys_ref.shape[1]
    rank = ADAPTER_RANK
    fold = weight_ref.shape[1] // width
    rows = 2 * rank // fold
    up = jnp.concatenate(
        [weight_ref[:rows, i * width : (i + 1) * width] for i in range(fold)], axis=0
    )
    low = low_ref[...].astype(jnp.bfloat16)
    keys = keys_ref[...].astype(jnp.float32) + jnp.dot(
        low[:, :rank], up[:rank], preferred_element_type=jnp.float32
    )
    values = values_ref[...].astype(jnp.float32) + jnp.dot(
        low[:, rank:], up[rank:], preferred_element_type=jnp.float32
    )
    for head in range(0, width, HEAD_SIZE):
        out_ref[:, head : head + HEAD_SIZE] = rotate(
            keys[:, head : head + HEAD_SIZE], tables_ref[...]
        ).astype(jnp.bfloat16)
    out_ref[:, width:] = values.astype(jnp.bfloat16)


def attend_kernel(
    first_head, group_size, block_count, weight_ref, low_ref, base_ref, tables_ref, query_pos_ref, key_pos_ref, *refs
):
    key_refs = refs[:block_count]
    value_refs = refs[block_count : 2 * block_count]
    out_ref = refs[-1]
    low = low_ref[...].astype(jnp.bfloat16)
    visible = key_pos_ref[...] <= query_pos_ref[...]
    group = None
    for lane in range(0, out_ref.shape[1], HEAD_SIZE):
        head = first_head + lane // HEAD_SIZE
        if head // group_size != group:
            group = head // group_size
            lanes = slice(group * HEAD_SIZE, (group + 1) * HEAD_SIZE)
            keys = jnp.concatenate([ref[:, lanes] for ref in key_refs], axis=0)
            values = jnp.concatenate([ref[:, lanes] for ref in value_refs], axis=0)
        at = slice(head * HEAD_SIZE, (head + 1) * HEAD_SIZE)
        queries = base_ref[:, at].astype(jnp.float32) + jnp.dot(
            low, weight_ref[:, at], preferred_element_type=jnp.float32
        )
        queries = rotate(queries, tables_ref[...]).astype(jnp.bfloat16)
        scores = lax.dot_general(
            queries, keys, CONTRACT_LAST, preferred_element_type=jnp.float32
        ) * HEAD_SIZE ** (-0.5)
        scores = jnp.where(visible, scores, NEG_BIG)
        raw = jnp.exp(scores - jnp.max(scores, axis=1, keepdims=True))
        totals = jnp.sum(raw, axis=1, keepdims=True)
        mixed = jnp.dot(raw.astype(jnp.bfloat16), values, preferred_element_type=jnp.float32)
        out_ref[:, lane : lane + HEAD_SIZE] = (mixed / totals).astype(jnp.bfloat16)


def token_positions(stored_block_order, first_row, row_count, half_rows):
    flat_index = first_row + jnp.arange(row_count, dtype=jnp.int32)
    block_index = flat_index // half_rows
    matches = (
        block_index[:, None] == jnp.arange(stored_block_order.shape[0], dtype=jnp.int32)[None, :]
    )
    stored_block = jnp.sum(jnp.where(matches, stored_block_order[None, :], 0), axis=1)
    return stored_block * half_rows + flat_index % half_rows


def shards(
    hidden,
    base_query_rows,
    base_key_rows,
    base_value_rows,
    stored_block_order,
    version,
    publisher,
    adapter_down_weight,
    adapter_up_query,
    adapter_up_key_value,
    output_down_weight,
    output_up_weight,
):
    rank = ADAPTER_RANK
    width = hidden.shape[1]
    source = publisher[0]
    slots = jnp.arange(version.shape[0], dtype=jnp.int32)
    chosen = jnp.sum(jnp.where(slots == source, version, 0))
    count = lax.axis_size("ctx")
    own_index = lax.axis_index("ctx")
    place = ring_place(own_index, count)
    behind = (place - ring_place(source, count)) % count
    is_source = behind == 0

    def pick(stored, first, rows):
        return lax.dynamic_slice(
            stored, (0, chosen, first, 0), (1, 1, rows, stored.shape[-1])
        ).reshape(rows, stored.shape[-1])

    pair_width = adapter_up_key_value.shape[-1]
    fold = width // pair_width
    pair_rows = 2 * rank // fold
    own_pair = lax.dynamic_index_in_dim(adapter_up_key_value[0], chosen, 0, keepdims=False)
    own_pair = own_pair.reshape(fold, pair_rows, pair_width).transpose(1, 0, 2)
    own_pair = own_pair.reshape(pair_rows, width)

    def pieces(stored, first, rows):
        return [pick(stored, first + i, CHUNK_ROWS) for i in range(0, rows, CHUNK_ROWS)]

    own = (
        pieces(adapter_down_weight, rank, 2 * rank)
        + pieces(adapter_down_weight, 0, rank)
        + [jnp.pad(own_pair, ((0, CHUNK_ROWS - pair_rows), (0, 0)))]
        + pieces(adapter_up_query, 0, rank)
        + pieces(output_down_weight, 0, rank)
        + pieces(output_up_weight, 0, rank)
    )
    per = rank // CHUNK_ROWS

    pairs = ring_pairs(count)
    arrived, sent = [], []
    own[LAG:] = lax.optimization_barrier(own[LAG:])

    def stream_to(last):
        for turn in range(len(sent), last):
            if turn < LAG:
                moving = own[turn]
            else:
                moving = after(arrived[turn - LAG], sent[-1])
                if turn < len(own):
                    moving = jnp.where(is_source, own[turn], moving)
            sent.append(moving)
            arrived.append(lax.ppermute(moving, "ctx", pairs))

    drain = LAG * (count - 2)

    distance = jnp.full((1,), behind, jnp.int32)

    def on_chunks(kernel, first, number, operands, shape, dtype):
        chunks = {("own", first + i): own[first + i] for i in range(number)}
        candidates = [[("own", first + i) for i in range(number)]]
        for hop in range(count - 1):
            turns = [first + i + LAG * hop for i in range(number)]
            candidates.append([("ring", turn) for turn in turns])
            chunks.update({("ring", turn): arrived[turn] for turn in turns})
        return chunk_call(
            kernel, distance, candidates, chunks, operands, jax.ShapeDtypeStruct(shape, dtype)
        )

    local_rows = hidden.shape[0]
    half_rows = local_rows // 2
    query_pos = token_positions(stored_block_order, own_index * local_rows, local_rows, half_rows)
    tables = rotation_tables(query_pos)

    stream_to(len(own) + drain)
    part = on_chunks(low_kernel, 0, 2 * per, [hidden], (local_rows, 2 * rank), jnp.float32)
    pair_sums = doubling_sums(part, "tp", jnp.float32)
    part = on_chunks(low_kernel, 2 * per, per, [hidden], (local_rows, rank), jnp.float32)
    query_sums = doubling_sums(part, "tp", jnp.float32)
    both = on_chunks(
        pair_kernel,
        3 * per,
        1,
        [pair_sums[-1], base_key_rows, base_value_rows, tables],
        (local_rows, 2 * pair_width),
        jnp.bfloat16,
    )

    forward, backward = ring_pairs(count), ring_pairs(count, back=True)
    key_blocks, value_blocks = {0: both[:, :pair_width]}, {0: both[:, pair_width:]}
    ahead, back = both, both
    for hop in range(1, (count - 1) // 2 + 1):
        ahead = lax.ppermute(ahead, "ctx", forward)
        back = lax.ppermute(back, "ctx", backward)
        for offset, block in ((-hop, ahead), (hop, back)):
            key_blocks[offset] = block[:, :pair_width]
            value_blocks[offset] = block[:, pair_width:]
    if count % 2 == 0:
        far = lax.ppermute(ahead[:, :pair_width], "ctx", forward)
        key_blocks[count // 2] = far
        far = lax.ppermute(back[:, pair_width:], "ctx", backward)
        value_blocks[count // 2] = far
    offsets = sorted(key_blocks)
    key_pos = jnp.concatenate(
        [
            token_positions(
                stored_block_order,
                ring_member((place + o) % count, count) * local_rows,
                local_rows,
                half_rows,
            )
            for o in offsets
        ]
    )
    local_heads = base_query_rows.shape[1] // HEAD_SIZE
    group_size = local_heads // (pair_width // HEAD_SIZE)
    piece_heads = local_heads // PIECES
    pieces_out = [
        on_chunks(
            functools.partial(attend_kernel, piece * piece_heads, group_size, len(offsets)),
            3 * per + 1,
            per,
            [query_sums[-1], base_query_rows, tables, query_pos[:, None], key_pos[None, :]]
            + [key_blocks[o] for o in offsets]
            + [value_blocks[o] for o in offsets],
            (local_rows, piece_heads * HEAD_SIZE),
            jnp.bfloat16,
        )
        for piece in range(PIECES)
    ]
    attended = jnp.concatenate(pieces_out, axis=1)
    late = 4 * per + 1
    part = on_chunks(low_kernel, late, per, pieces_out, (local_rows, rank), jnp.float32)
    out_low = doubling_sums(part, "tp", jnp.float32)[-1]
    adapted = on_chunks(up_kernel, late + per, per, [out_low], attended.shape, jnp.bfloat16)
    return (attended, adapted)


def solution(mesh):
    placed = (
        P(("groups", "ctx"), "tp"),
        P(("groups", "ctx"), "tp"),
        P(("groups", "ctx"), "tp"),
        P(("groups", "ctx"), "tp"),
        P("groups"),
        P("groups"),
        P("groups"),
        P("ctx", None, None, "tp"),
        P("ctx", None, None, "tp"),
        P("ctx", None, None, None, "tp"),
        P("ctx", None, None, "tp"),
        P("ctx", None, None, "tp"),
    )
    return jax.shard_map(
        shards,
        mesh=mesh,
        in_specs=placed,
        out_specs=(P(("groups", "ctx"), "tp"), P(("groups", "ctx"), "tp")),
        check_vma=False,
    )
```

profile of v0, /device:TPU:0, one launch (start us, length us, event | category | flops | bytes accessed | tf_op | source)
XLA Modules:
  0.0 91.1 jit_solution(4928493911799677579)
XLA Ops:
  1.3 1.3 %fusion.11 = s32[]{:T(128)} fusion(s32[4]{0:T(128)} %param.17, s32[]{:T(128)} %bitcast.37), kind=kLoop, calls=%fused_computation.79 | loop fusion | flops 11 | bytes 24 | tf_op jit(solution)/shard_map/reduce_sum | solution.py:221
  4.6 1.3 %dynamic-slice_bitcast_fusion = (bf16[32,2048]{1,0:T(8,128)(2,1)S(1)}, bf16[32,2048]{1,0:T(8,128)(2,1)S(1)}, bf16[32,2048]{1,0:T(8,128)(2,1)S(1)}, bf16[32,2048]...) fusion(bf16[1,4,192,2048]{3,2,1,0:T(8,128)(2,1)} %param.19, s32[]{:T(128)S(6)} %select_n.247), kind=kLoop, calls=%fused_computation.2 | loop fusion | bytes 1572868 | tf_op jit(solution)/shard_map/reshape | solution.py:231
  5.9 3.1 %collective-permute-start.1 = (bf16[32,2048]{1,0:T(8,128)(2,1)S(1)}, bf16[32,2048]{1,0:T(8,128)(2,1)S(1)}, u32[]{:S(2)}, u32[]{:S(2)}) collective-permute-start(bf16[32,2048]{1,0:T(8,128)(2,1)S(1)} %get-tuple-element.59.refs_0_), channel_id=1, source_target_pairs={{0,4},{4,12},{12,8},{8,0},{1,5},{5,13},{13,9},{9,1},{2,6},{6,14},{... | collective-permute-start | bytes 393224 | tf_op jit(solution)/shard_map/ppermute | solution.py:266
  9.0 2.6 %collective-permute-start = (bf16[32,2048]{1,0:T(8,128)(2,1)S(1)}, bf16[32,2048]{1,0:T(8,128)(2,1)S(1)}, u32[]{:S(2)}, u32[]{:S(2)}) collective-permute-start(bf16[32,2048]{1,0:T(8,128)(2,1)S(1)} %get-tuple-element.64.refs_1_), channel_id=1, source_target_pairs={{0,4},{4,12},{12,8},{8,0},{1,5},{5,13},{13,9},{9,1},{2,6},{6,14},{... | collective-permute-start | bytes 393224 | tf_op jit(solution)/shard_map/ppermute | solution.py:266
  11.7 0.7 select_reduce_fusion.3
  12.7 1.0 %dynamic-slice_bitcast_fusion.6 = (bf16[32,2048]{1,0:T(8,128)(2,1)S(1)}, bf16[32,2048]{1,0:T(8,128)(2,1)S(1)}) fusion(bf16[1,4,64,2048]{3,2,1,0:T(8,128)(2,1)} %param.20, s32[]{:T(128)S(6)} %select_n.247), kind=kLoop, calls=%fused_computation.8 | loop fusion | bytes 524292 | tf_op jit(solution)/shard_map/reshape | solution.py:231
  13.7 1.1 %dynamic-slice_bitcast_fusion.2 = (bf16[32,2048]{1,0:T(8,128)(2,1)S(1)}, bf16[32,2048]{1,0:T(8,128)(2,1)S(1)}, bf16[32,2048]{1,0:T(8,128)(2,1)S(1)}, bf16[32,2048]{1,0:T(8,128)(2,1)S(1)}) fusion(bf16[1,4,64,2048]{3,2,1,0:T(8,128)(2,1)} %param.23, s32[]{:T(128)S(6)} %select_n.247, bf16[1,4,64,2048]{3,2,1,0:T(8,128)(2,1)} %param.22), kind=kLoop, calls=%fused_computation.4 | loop fusion | bytes 1048580 | tf_op jit(solution)/shard_map/reshape | solution.py:231
  15.2 0.5 collective-permute-start.3
  15.7 0.6 collective-permute-done.refs_5_
  16.4 2.7 %collective-permute-start.2 = (bf16[32,2048]{1,0:T(8,128)(2,1)S(1)}, bf16[32,2048]{1,0:T(8,128)(2,1)S(1)}, u32[]{:S(2)}, u32[]{:S(2)}) collective-permute-start(bf16[32,2048]{1,0:T(8,128)(2,1)S(1)} %broadcast_select_fusion.9), channel_id=1, source_target_pairs={{0,4},{4,12},{12,8},{8,0},{1,5},{5,13},{13,9},{9,1},{2,6},{6,14},{... | collective-permute-start | bytes 393224 | tf_op jit(solution)/shard_map/ppermute | solution.py:266
  19.0 3.2 %collective-permute-done.3.refs_6_ = bf16[32,2048]{1,0:T(8,128)(2,1)S(1)} collective-permute-done((bf16[32,2048]{1,0:T(8,128)(2,1)S(1)}, bf16[32,2048]{1,0:T(8,128)(2,1)S(1)}, u32[]{:S(2)}, u32[]{:S(2)}) %collective-permute-start.3) | collective-permute-done | bytes 131104 | tf_op jit(solution)/shard_map/ppermute | solution.py:266
  22.3 0.6 collective-permute-start.5
  22.9 1.6 %collective-permute-done.2.refs_7_ = bf16[32,2048]{1,0:T(8,128)(2,1)S(1)} collective-permute-done((bf16[32,2048]{1,0:T(8,128)(2,1)S(1)}, bf16[32,2048]{1,0:T(8,128)(2,1)S(1)}, u32[]{:S(2)}, u32[]{:S(2)}) %collective-permute-start.2) | collective-permute-done | bytes 131104 | tf_op jit(solution)/shard_map/ppermute | solution.py:266
  24.5 1.9 %collective-permute-start.4 = (bf16[32,2048]{1,0:T(8,128)(2,1)S(1)}, bf16[32,2048]{1,0:T(8,128)(2,1)S(1)}, u32[]{:S(2)}, u32[]{:S(2)}) collective-permute-start(bf16[32,2048]{1,0:T(8,128)(2,1)S(1)} %broadcast_select_fusion.7), channel_id=1, source_target_pairs={{0,4},{4,12},{12,8},{8,0},{1,5},{5,13},{13,9},{9,1},{2,6},{6,14},{... | collective-permute-start | bytes 393224 | tf_op jit(solution)/shard_map/ppermute | solution.py:266
  26.4 2.1 %collective-permute-done.5.refs_2_.refs_8_ = bf16[32,2048]{1,0:T(8,128)(2,1)S(1)} collective-permute-done((bf16[32,2048]{1,0:T(8,128)(2,1)S(1)}, bf16[32,2048]{1,0:T(8,128)(2,1)S(1)}, u32[]{:S(2)}, u32[]{:S(2)}) %collective-permute-start.5) | collective-permute-done | bytes 131104 | tf_op jit(solution)/shard_map/ppermute | solution.py:266
  28.5 0.4 collective-permute-start.7
  28.9 2.6 %collective-permute-done.4.refs_3_.refs_9_ = bf16[32,2048]{1,0:T(8,128)(2,1)S(1)} collective-permute-done((bf16[32,2048]{1,0:T(8,128)(2,1)S(1)}, bf16[32,2048]{1,0:T(8,128)(2,1)S(1)}, u32[]{:S(2)}, u32[]{:S(2)}) %collective-permute-start.4) | collective-permute-done | bytes 131104 | tf_op jit(solution)/shard_map/ppermute | solution.py:266
  31.5 1.0 %collective-permute-start.6 = (bf16[32,2048]{1,0:T(8,128)(2,1)S(1)}, bf16[32,2048]{1,0:T(8,128)(2,1)S(1)}, u32[]{:S(2)}, u32[]{:S(2)}) collective-permute-start(bf16[32,2048]{1,0:T(8,128)(2,1)S(1)} %broadcast_select_fusion.5), channel_id=1, source_target_pairs={{0,4},{4,12},{12,8},{8,0},{1,5},{5,13},{13,9},{9,1},{2,6},{6,14},{... | collective-permute-start | bytes 393224 | tf_op jit(solution)/shard_map/ppermute | solution.py:266
  32.5 1.8 %collective-permute-done.7.refs_4_.refs_10_.refs_1_ = bf16[32,2048]{1,0:T(8,128)(2,1)S(1)} collective-permute-done((bf16[32,2048]{1,0:T(8,128)(2,1)S(1)}, bf16[32,2048]{1,0:T(8,128)(2,1)S(1)}, u32[]{:S(2)}, u32[]{:S(2)}) %collective-permute-start.7) | collective-permute-done | bytes 131104 | tf_op jit(solution)/shard_map/ppermute | solution.py:266
  34.4 1.6 %collective-permute-start.8 = (bf16[32,2048]{1,0:T(8,128)(2,1)S(1)}, bf16[32,2048]{1,0:T(8,128)(2,1)S(1)}, u32[]{:S(2)}, u32[]{:S(2)}) collective-permute-start(bf16[32,2048]{1,0:T(8,128)(2,1)S(1)} %broadcast_select_fusion.4), channel_id=1, source_target_pairs={{0,4},{4,12},{12,8},{8,0},{1,5},{5,13},{13,9},{9,1},{2,6},{6,14},{... | collective-permute-start | bytes 393224 | tf_op jit(solution)/shard_map/ppermute | solution.py:266
  36.0 1.4 %collective-permute-done.6.refs_5_.refs_11_.refs_2_ = bf16[32,2048]{1,0:T(8,128)(2,1)S(1)} collective-permute-done((bf16[32,2048]{1,0:T(8,128)(2,1)S(1)}, bf16[32,2048]{1,0:T(8,128)(2,1)S(1)}, u32[]{:S(2)}, u32[]{:S(2)}) %collective-permute-start.6) | collective-permute-done | bytes 131104 | tf_op jit(solution)/shard_map/ppermute | solution.py:266
  37.9 1.4 %collective-permute-start.9 = (bf16[32,2048]{1,0:T(8,128)(2,1)S(1)}, bf16[32,2048]{1,0:T(8,128)(2,1)S(1)}, u32[]{:S(2)}, u32[]{:S(2)}) collective-permute-start(bf16[32,2048]{1,0:T(8,128)(2,1)S(1)} %broadcast_select_fusion.3), channel_id=1, source_target_pairs={{0,4},{4,12},{12,8},{8,0},{1,5},{5,13},{13,9},{9,1},{2,6},{6,14},{... | collective-permute-start | bytes 393224 | tf_op jit(solution)/shard_map/ppermute | solution.py:266
  39.5 1.6 %collective-permute-start.16 = (f32[128,128]{1,0:T(8,128)S(1)}, f32[128,128]{1,0:T(8,128)S(1)}, u32[]{:S(2)}, u32[]{:S(2)}) collective-permute-start(f32[128,128]{1,0:T(8,128)S(1)} %add.245), channel_id=1, source_target_pairs={{0,2},{1,3},{2,0},{3,1},{4,6},{5,7},{6,4},{7,5},{8,10},{9,11},{10,... | collective-permute-start | bytes 196616 | tf_op jit(solution)/shard_map/ppermute | solution.py:60
  41.1 2.8 %collective-permute-done.16 = f32[128,128]{1,0:T(8,128)S(1)} collective-permute-done((f32[128,128]{1,0:T(8,128)S(1)}, f32[128,128]{1,0:T(8,128)S(1)}, u32[]{:S(2)}, u32[]{:S(2)}) %collective-permute-start.16) | collective-permute-done | bytes 65568 | tf_op jit(solution)/shard_map/ppermute | solution.py:60
  43.9 0.9 collective-permute-done.9.refs_7_.refs_4_.refs_2_
  45.2 2.1 %collective-permute-start.10 = (bf16[32,2048]{1,0:T(8,128)(2,1)S(1)}, bf16[32,2048]{1,0:T(8,128)(2,1)S(1)}, u32[]{:S(2)}, u32[]{:S(2)}) collective-permute-start(bf16[32,2048]{1,0:T(8,128)(2,1)S(1)} %broadcast_select_fusion.2), channel_id=1, source_target_pairs={{0,4},{4,12},{12,8},{8,0},{1,5},{5,13},{13,9},{9,1},{2,6},{6,14},{... | collective-permute-start | bytes 393224 | tf_op jit(solution)/shard_map/ppermute | solution.py:266
  47.3 1.6 %collective-permute-start.14 = (f32[128,64]{1,0:T(8,128)S(1)}, f32[128,64]{1,0:T(8,128)S(1)}, u32[]{:S(2)}, u32[]{:S(2)}) collective-permute-start(f32[128,64]{1,0:T(8,128)S(1)} %add.212), channel_id=1, source_target_pairs={{0,2},{1,3},{2,0},{3,1},{4,6},{5,7},{6,4},{7,5},{8,10},{9,11},{10,... | collective-permute-start | bytes 98312 | tf_op jit(solution)/shard_map/ppermute | solution.py:60
  48.9 2.3 %collective-permute-start.11 = (bf16[32,2048]{1,0:T(8,128)(2,1)S(1)}, bf16[32,2048]{1,0:T(8,128)(2,1)S(1)}, u32[]{:S(2)}, u32[]{:S(2)}) collective-permute-start(bf16[32,2048]{1,0:T(8,128)(2,1)S(1)} %broadcast_select_fusion.1), channel_id=1, source_target_pairs={{0,4},{4,12},{12,8},{8,0},{1,5},{5,13},{13,9},{9,1},{2,6},{6,14},{... | collective-permute-start | bytes 393224 | tf_op jit(solution)/shard_map/ppermute | solution.py:266
  51.2 0.5 collective-permute-done.14
  51.7 0.4 collective-permute-done.10.refs_3_.refs_5_
  52.3 1.9 %collective-permute-start.18 = (bf16[128,512]{1,0:T(8,128)(2,1)S(1)}, bf16[128,512]{1,0:T(8,128)(2,1)S(1)}, u32[]{:S(2)}, u32[]{:S(2)}) collective-permute-start(bf16[128,512]{1,0:T(8,128)(2,1)S(1)} %shard_map.133), channel_id=1, source_target_pairs={{4,0},{12,4},{8,12},{0,8},{5,1},{13,5},{9,13},{1,9},{6,2},{14,6},{... | collective-permute-start | bytes 393224 | tf_op jit(solution)/shard_map/ppermute | solution.py:307
  54.4 2.9 %collective-permute-start.12 = (bf16[32,2048]{1,0:T(8,128)(2,1)S(1)}, bf16[32,2048]{1,0:T(8,128)(2,1)S(1)}, u32[]{:S(2)}, u32[]{:S(2)}) collective-permute-start(bf16[32,2048]{1,0:T(8,128)(2,1)S(1)} %broadcast_select_fusion), channel_id=1, source_target_pairs={{0,4},{4,12},{12,8},{8,0},{1,5},{5,13},{13,9},{9,1},{2,6},{6,14},{... | collective-permute-start | bytes 393224 | tf_op jit(solution)/shard_map/ppermute | solution.py:266
  57.3 2.0 %collective-permute-start.21 = (bf16[32,2048]{1,0:T(8,128)(2,1)S(1)}, bf16[32,2048]{1,0:T(8,128)(2,1)S(1)}, u32[]{:S(2)}, u32[]{:S(2)}) collective-permute-start(bf16[32,2048]{1,0:T(8,128)(2,1)S(1)} %collective-permute-done.11.refs_6_.refs_4_.refs_2_), channel_id=1, source_target_pairs={{0,4},{4,12},{12,8},{8,0},{1,5},{5,13},{13,9},{9,1},{2,6},{6,14},{... | collective-permute-start | bytes 393224 | tf_op jit(solution)/shard_map/ppermute | solution.py:266
  59.3 2.3 %collective-permute-start.20 = (bf16[128,256]{1,0:T(8,128)(2,1)S(1)}, bf16[128,256]{1,0:T(8,128)(2,1)S(1)}, u32[]{:S(2)}, u32[]{:S(2)}) collective-permute-start(bf16[128,256]{1,0:T(8,128)(2,1)S(1)} %get-tuple-element.71.refs_19_), channel_id=1, source_target_pairs={{4,0},{12,4},{8,12},{0,8},{5,1},{13,5},{9,13},{1,9},{6,2},{14,6},{... | collective-permute-start | bytes 196616 | tf_op jit(solution)/shard_map/ppermute | solution.py:314
  61.6 1.1 %collective-permute-done.17 = bf16[128,512]{1,0:T(8,128)(2,1)S(1)} collective-permute-done((bf16[128,512]{1,0:T(8,128)(2,1)S(1)}, bf16[128,512]{1,0:T(8,128)(2,1)S(1)}, u32[]{:S(2)}, u32[]{:S(2)}) %collective-permute-start.17) | collective-permute-done | bytes 131104 | tf_op jit(solution)/shard_map/ppermute | solution.py:306
  62.7 0.8 collective-permute-start.19
  63.5 2.0 %collective-permute-done.12.refs_7_.refs_5_.refs_3_ = bf16[32,2048]{1,0:T(8,128)(2,1)S(1)} collective-permute-done((bf16[32,2048]{1,0:T(8,128)(2,1)S(1)}, bf16[32,2048]{1,0:T(8,128)(2,1)S(1)}, u32[]{:S(2)}, u32[]{:S(2)}) %collective-permute-start.12) | collective-permute-done | bytes 131104 | tf_op jit(solution)/shard_map/ppermute | solution.py:266
  65.5 4.5 %collective-permute-start.22 = (bf16[32,2048]{1,0:T(8,128)(2,1)S(1)}, bf16[32,2048]{1,0:T(8,128)(2,1)S(1)}, u32[]{:S(2)}, u32[]{:S(2)}) collective-permute-start(bf16[32,2048]{1,0:T(8,128)(2,1)S(1)} %collective-permute-done.12.refs_7_.refs_5_.refs_3_), channel_id=1, source_target_pairs={{0,4},{4,12},{12,8},{8,0},{1,5},{5,13},{13,9},{9,1},{2,6},{6,14},{... | collective-permute-start | bytes 393224 | tf_op jit(solution)/shard_map/ppermute | solution.py:266
  69.9 0.9 %collective-permute-done.20.refs_20_ = bf16[128,256]{1,0:T(8,128)(2,1)S(1)} collective-permute-done((bf16[128,256]{1,0:T(8,128)(2,1)S(1)}, bf16[128,256]{1,0:T(8,128)(2,1)S(1)}, u32[]{:S(2)}, u32[]{:S(2)}) %collective-permute-start.20) | collective-permute-done | bytes 65568 | tf_op jit(solution)/shard_map/ppermute | solution.py:314
  70.9 1.3 %collective-permute-done.19.refs_16_ = bf16[128,256]{1,0:T(8,128)(2,1)S(1)} collective-permute-done((bf16[128,256]{1,0:T(8,128)(2,1)S(1)}, bf16[128,256]{1,0:T(8,128)(2,1)S(1)}, u32[]{:S(2)}, u32[]{:S(2)}) %collective-permute-start.19) | collective-permute-done | bytes 65568 | tf_op jit(solution)/shard_map/ppermute | solution.py:312
  72.2 3.8 %shard_map.135.refs_9_ = bf16[128,1024]{1,0:T(8,128)(2,1)S(1)} custom-call(s32[1]{0:T(128)} %bitcast.1.behind_ref, bf16[32,2048]{1,0:T(8,128)(2,1)S(1)} %get-tuple-element.28.refs_0_, bf16[32,2048]{1,0:T(8,128)(2,1)S(1)} %get-tuple-element.29.refs_1_, bf16[32,2048]{1,0:T(8,128)(2,1)S(1)} %collective-permute-done.6.refs_5_.refs_11_.refs_2_, ...), custom_call_target="tpu_custom_call" | custom-call | tf_op jit(solution)/shard_map/pallas_call | solution.py:102
  76.1 3.9 %shard_map.134.refs_8_ = bf16[128,1024]{1,0:T(8,128)(2,1)S(1)} custom-call(s32[1]{0:T(128)} %bitcast.1.behind_ref, bf16[32,2048]{1,0:T(8,128)(2,1)S(1)} %get-tuple-element.28.refs_0_, bf16[32,2048]{1,0:T(8,128)(2,1)S(1)} %get-tuple-element.29.refs_1_, bf16[32,2048]{1,0:T(8,128)(2,1)S(1)} %collective-permute-done.6.refs_5_.refs_11_.refs_2_, ...), custom_call_target="tpu_custom_call" | custom-call | tf_op jit(solution)/shard_map/pallas_call | solution.py:102
  80.4 3.1 %collective-permute-start.24 = (bf16[32,2048]{1,0:T(8,128)(2,1)S(1)}, bf16[32,2048]{1,0:T(8,128)(2,1)S(1)}, u32[]{:S(2)}, u32[]{:S(2)}) collective-permute-start(bf16[32,2048]{1,0:T(8,128)(2,1)S(1)} %collective-permute-done.22.refs_7_.refs_5_), channel_id=1, source_target_pairs={{0,4},{4,12},{12,8},{8,0},{1,5},{5,13},{13,9},{9,1},{2,6},{6,14},{... | collective-permute-start | bytes 393224 | tf_op jit(solution)/shard_map/ppermute | solution.py:266
  83.6 1.6 %collective-permute-start.26 = (f32[128,64]{1,0:T(8,128)S(1)}, f32[128,64]{1,0:T(8,128)S(1)}, u32[]{:S(2)}, u32[]{:S(2)}) collective-permute-start(f32[128,64]{1,0:T(8,128)S(1)} %add.247), channel_id=1, source_target_pairs={{0,2},{1,3},{2,0},{3,1},{4,6},{5,7},{6,4},{7,5},{8,10},{9,11},{10,... | collective-permute-start | bytes 98312 | tf_op jit(solution)/shard_map/ppermute | solution.py:60
  85.2 0.8 pad_maximum_fusion
  86.0 1.9 %collective-permute-done.26 = f32[128,64]{1,0:T(8,128)S(1)} collective-permute-done((f32[128,64]{1,0:T(8,128)S(1)}, f32[128,64]{1,0:T(8,128)S(1)}, u32[]{:S(2)}, u32[]{:S(2)}) %collective-permute-start.26) | collective-permute-done | bytes 32800 | tf_op jit(solution)/shard_map/ppermute | solution.py:60
  87.9 2.0 %collective-permute-done.24.refs_7_ = bf16[32,2048]{1,0:T(8,128)(2,1)S(1)} collective-permute-done((bf16[32,2048]{1,0:T(8,128)(2,1)S(1)}, bf16[32,2048]{1,0:T(8,128)(2,1)S(1)}, u32[]{:S(2)}, u32[]{:S(2)}) %collective-permute-start.24) | collective-permute-done | bytes 131104 | tf_op jit(solution)/shard_map/ppermute | solution.py:266
  90.3 0.8 copy.23
  (67 shorter events, 3.0 us)
Async XLA Ops:
  0.6 12.0 %copy-start = (bf16[1,4,2,64,256]{4,3,2,1,0:T(8,128)(2,1)S(1)}, bf16[1,4,2,64,256]{4,3,2,1,0:T(8,128)(2,1)}, u32[]{:S(2)}) copy-start(bf16[1,4,2,64,256]{4,3,2,1,0:T(8,128)(2,1)} %param.21) | copy-start | bytes 786436
  4.6 32.9 %copy-start.2 = (bf16[128,2048]{1,0:T(8,128)(2,1)S(1)}, bf16[128,2048]{1,0:T(8,128)(2,1)}, u32[]{:S(2)}) copy-start(bf16[128,2048]{1,0:T(8,128)(2,1)} %refs_12_.1) | copy-start | bytes 1572868
  5.9 9.3 %collective-permute-start.1 = (bf16[32,2048]{1,0:T(8,128)(2,1)S(1)}, bf16[32,2048]{1,0:T(8,128)(2,1)S(1)}, u32[]{:S(2)}, u32[]{:S(2)}) collective-permute-start(bf16[32,2048]{1,0:T(8,128)(2,1)S(1)} %get-tuple-element.59.refs_0_), channel_id=1, source_target_pairs={{0,4},{4,12},{12,8},{8,0},{1,5},{5,13},{13,9},{9,1},{2,6},{6,14},{... | collective-permute-start | bytes 393224 | tf_op jit(solution)/shard_map/ppermute | solution.py:266
  9.0 7.3 %collective-permute-start = (bf16[32,2048]{1,0:T(8,128)(2,1)S(1)}, bf16[32,2048]{1,0:T(8,128)(2,1)S(1)}, u32[]{:S(2)}, u32[]{:S(2)}) collective-permute-start(bf16[32,2048]{1,0:T(8,128)(2,1)S(1)} %get-tuple-element.64.refs_1_), channel_id=1, source_target_pairs={{0,4},{4,12},{12,8},{8,0},{1,5},{5,13},{13,9},{9,1},{2,6},{6,14},{... | collective-permute-start | bytes 393224 | tf_op jit(solution)/shard_map/ppermute | solution.py:266
  15.2 7.0 %collective-permute-start.3 = (bf16[32,2048]{1,0:T(8,128)(2,1)S(1)}, bf16[32,2048]{1,0:T(8,128)(2,1)S(1)}, u32[]{:S(2)}, u32[]{:S(2)}) collective-permute-start(bf16[32,2048]{1,0:T(8,128)(2,1)S(1)} %broadcast_select_fusion.10), channel_id=1, source_target_pairs={{0,4},{4,12},{12,8},{8,0},{1,5},{5,13},{13,9},{9,1},{2,6},{6,14},{... | collective-permute-start | bytes 393224 | tf_op jit(solution)/shard_map/ppermute | solution.py:266
  16.4 8.1 %collective-permute-start.2 = (bf16[32,2048]{1,0:T(8,128)(2,1)S(1)}, bf16[32,2048]{1,0:T(8,128)(2,1)S(1)}, u32[]{:S(2)}, u32[]{:S(2)}) collective-permute-start(bf16[32,2048]{1,0:T(8,128)(2,1)S(1)} %broadcast_select_fusion.9), channel_id=1, source_target_pairs={{0,4},{4,12},{12,8},{8,0},{1,5},{5,13},{13,9},{9,1},{2,6},{6,14},{... | collective-permute-start | bytes 393224 | tf_op jit(solution)/shard_map/ppermute | solution.py:266
  22.3 6.2 %collective-permute-start.5 = (bf16[32,2048]{1,0:T(8,128)(2,1)S(1)}, bf16[32,2048]{1,0:T(8,128)(2,1)S(1)}, u32[]{:S(2)}, u32[]{:S(2)}) collective-permute-start(bf16[32,2048]{1,0:T(8,128)(2,1)S(1)} %broadcast_select_fusion.8), channel_id=1, source_target_pairs={{0,4},{4,12},{12,8},{8,0},{1,5},{5,13},{13,9},{9,1},{2,6},{6,14},{... | collective-permute-start | bytes 393224 | tf_op jit(solution)/shard_map/ppermute | solution.py:266
  24.5 7.0 %collective-permute-start.4 = (bf16[32,2048]{1,0:T(8,128)(2,1)S(1)}, bf16[32,2048]{1,0:T(8,128)(2,1)S(1)}, u32[]{:S(2)}, u32[]{:S(2)}) collective-permute-start(bf16[32,2048]{1,0:T(8,128)(2,1)S(1)} %broadcast_select_fusion.7), channel_id=1, source_target_pairs={{0,4},{4,12},{12,8},{8,0},{1,5},{5,13},{13,9},{9,1},{2,6},{6,14},{... | collective-permute-start | bytes 393224 | tf_op jit(solution)/shard_map/ppermute | solution.py:266
  28.5 5.9 %collective-permute-start.7 = (bf16[32,2048]{1,0:T(8,128)(2,1)S(1)}, bf16[32,2048]{1,0:T(8,128)(2,1)S(1)}, u32[]{:S(2)}, u32[]{:S(2)}) collective-permute-start(bf16[32,2048]{1,0:T(8,128)(2,1)S(1)} %broadcast_select_fusion.6), channel_id=1, source_target_pairs={{0,4},{4,12},{12,8},{8,0},{1,5},{5,13},{13,9},{9,1},{2,6},{6,14},{... | collective-permute-start | bytes 393224 | tf_op jit(solution)/shard_map/ppermute | solution.py:266
  31.5 5.9 %collective-permute-start.6 = (bf16[32,2048]{1,0:T(8,128)(2,1)S(1)}, bf16[32,2048]{1,0:T(8,128)(2,1)S(1)}, u32[]{:S(2)}, u32[]{:S(2)}) collective-permute-start(bf16[32,2048]{1,0:T(8,128)(2,1)S(1)} %broadcast_select_fusion.5), channel_id=1, source_target_pairs={{0,4},{4,12},{12,8},{8,0},{1,5},{5,13},{13,9},{9,1},{2,6},{6,14},{... | collective-permute-start | bytes 393224 | tf_op jit(solution)/shard_map/ppermute | solution.py:266
  34.4 17.7 %copy-start.3 = (bf16[128,256]{1,0:T(8,128)(2,1)S(1)}, bf16[128,256]{1,0:T(8,128)(2,1)}, u32[]{:S(2)}) copy-start(bf16[128,256]{1,0:T(8,128)(2,1)} %refs_5_.1) | copy-start | bytes 196612
  34.4 17.6 %copy-start.4 = (bf16[128,256]{1,0:T(8,128)(2,1)S(1)}, bf16[128,256]{1,0:T(8,128)(2,1)}, u32[]{:S(2)}) copy-start(bf16[128,256]{1,0:T(8,128)(2,1)} %refs_6_.1) | copy-start | bytes 196612
  34.4 9.4 %collective-permute-start.8 = (bf16[32,2048]{1,0:T(8,128)(2,1)S(1)}, bf16[32,2048]{1,0:T(8,128)(2,1)S(1)}, u32[]{:S(2)}, u32[]{:S(2)}) collective-permute-start(bf16[32,2048]{1,0:T(8,128)(2,1)S(1)} %broadcast_select_fusion.4), channel_id=1, source_target_pairs={{0,4},{4,12},{12,8},{8,0},{1,5},{5,13},{13,9},{9,1},{2,6},{6,14},{... | collective-permute-start | bytes 393224 | tf_op jit(solution)/shard_map/ppermute | solution.py:266
  37.8 34.4 %copy-start.1 = (bf16[128,2048]{1,0:T(8,128)(2,1)S(1)}, bf16[128,2048]{1,0:T(8,128)(2,1)}, u32[]{:S(2)}) copy-start(bf16[128,2048]{1,0:T(8,128)(2,1)} %refs_9_.3) | copy-start | bytes 1572868
  37.8 1.7 %collective-permute-start.15 = (f32[128,128]{1,0:T(8,128)S(1)}, f32[128,128]{1,0:T(8,128)S(1)}, u32[]{:S(2)}, u32[]{:S(2)}) collective-permute-start(f32[128,128]{1,0:T(8,128)S(1)} %shard_map.132), channel_id=1, source_target_pairs={{0,1},{1,0},{2,3},{3,2},{4,5},{5,4},{6,7},{7,6},{8,9},{9,8},{10,11... | collective-permute-start | bytes 196616 | tf_op jit(solution)/shard_map/ppermute | solution.py:60
  37.9 6.8 %collective-permute-start.9 = (bf16[32,2048]{1,0:T(8,128)(2,1)S(1)}, bf16[32,2048]{1,0:T(8,128)(2,1)S(1)}, u32[]{:S(2)}, u32[]{:S(2)}) collective-permute-start(bf16[32,2048]{1,0:T(8,128)(2,1)S(1)} %broadcast_select_fusion.3), channel_id=1, source_target_pairs={{0,4},{4,12},{12,8},{8,0},{1,5},{5,13},{13,9},{9,1},{2,6},{6,14},{... | collective-permute-start | bytes 393224 | tf_op jit(solution)/shard_map/ppermute | solution.py:266
  39.5 4.3 %collective-permute-start.16 = (f32[128,128]{1,0:T(8,128)S(1)}, f32[128,128]{1,0:T(8,128)S(1)}, u32[]{:S(2)}, u32[]{:S(2)}) collective-permute-start(f32[128,128]{1,0:T(8,128)S(1)} %add.245), channel_id=1, source_target_pairs={{0,2},{1,3},{2,0},{3,1},{4,6},{5,7},{6,4},{7,5},{8,10},{9,11},{10,... | collective-permute-start | bytes 196616 | tf_op jit(solution)/shard_map/ppermute | solution.py:60
  45.1 2.2 %collective-permute-start.13 = (f32[128,64]{1,0:T(8,128)S(1)}, f32[128,64]{1,0:T(8,128)S(1)}, u32[]{:S(2)}, u32[]{:S(2)}) collective-permute-start(f32[128,64]{1,0:T(8,128)S(1)} %shard_map.131), channel_id=1, source_target_pairs={{0,1},{1,0},{2,3},{3,2},{4,5},{5,4},{6,7},{7,6},{8,9},{9,8},{10,11... | collective-permute-start | bytes 98312 | tf_op jit(solution)/shard_map/ppermute | solution.py:60
  45.2 6.8 %collective-permute-start.10 = (bf16[32,2048]{1,0:T(8,128)(2,1)S(1)}, bf16[32,2048]{1,0:T(8,128)(2,1)S(1)}, u32[]{:S(2)}, u32[]{:S(2)}) collective-permute-start(bf16[32,2048]{1,0:T(8,128)(2,1)S(1)} %broadcast_select_fusion.2), channel_id=1, source_target_pairs={{0,4},{4,12},{12,8},{8,0},{1,5},{5,13},{13,9},{9,1},{2,6},{6,14},{... | collective-permute-start | bytes 393224 | tf_op jit(solution)/shard_map/ppermute | solution.py:266
  47.3 4.3 %collective-permute-start.14 = (f32[128,64]{1,0:T(8,128)S(1)}, f32[128,64]{1,0:T(8,128)S(1)}, u32[]{:S(2)}, u32[]{:S(2)}) collective-permute-start(f32[128,64]{1,0:T(8,128)S(1)} %add.212), channel_id=1, source_target_pairs={{0,2},{1,3},{2,0},{3,1},{4,6},{5,7},{6,4},{7,5},{8,10},{9,11},{10,... | collective-permute-start | bytes 98312 | tf_op jit(solution)/shard_map/ppermute | solution.py:60
  48.9 8.4 %collective-permute-start.11 = (bf16[32,2048]{1,0:T(8,128)(2,1)S(1)}, bf16[32,2048]{1,0:T(8,128)(2,1)S(1)}, u32[]{:S(2)}, u32[]{:S(2)}) collective-permute-start(bf16[32,2048]{1,0:T(8,128)(2,1)S(1)} %broadcast_select_fusion.1), channel_id=1, source_target_pairs={{0,4},{4,12},{12,8},{8,0},{1,5},{5,13},{13,9},{9,1},{2,6},{6,14},{... | collective-permute-start | bytes 393224 | tf_op jit(solution)/shard_map/ppermute | solution.py:266
  52.3 6.9 %collective-permute-start.18 = (bf16[128,512]{1,0:T(8,128)(2,1)S(1)}, bf16[128,512]{1,0:T(8,128)(2,1)S(1)}, u32[]{:S(2)}, u32[]{:S(2)}) collective-permute-start(bf16[128,512]{1,0:T(8,128)(2,1)S(1)} %shard_map.133), channel_id=1, source_target_pairs={{4,0},{12,4},{8,12},{0,8},{5,1},{13,5},{9,13},{1,9},{6,2},{14,6},{... | collective-permute-start | bytes 393224 | tf_op jit(solution)/shard_map/ppermute | solution.py:307
  54.2 8.4 %collective-permute-start.17 = (bf16[128,512]{1,0:T(8,128)(2,1)S(1)}, bf16[128,512]{1,0:T(8,128)(2,1)S(1)}, u32[]{:S(2)}, u32[]{:S(2)}) collective-permute-start(bf16[128,512]{1,0:T(8,128)(2,1)S(1)} %shard_map.133), channel_id=1, source_target_pairs={{0,4},{4,12},{12,8},{8,0},{1,5},{5,13},{13,9},{9,1},{2,6},{6,14},{... | collective-permute-start | bytes 393224 | tf_op jit(solution)/shard_map/ppermute | solution.py:306
  54.4 11.1 %collective-permute-start.12 = (bf16[32,2048]{1,0:T(8,128)(2,1)S(1)}, bf16[32,2048]{1,0:T(8,128)(2,1)S(1)}, u32[]{:S(2)}, u32[]{:S(2)}) collective-permute-start(bf16[32,2048]{1,0:T(8,128)(2,1)S(1)} %broadcast_select_fusion), channel_id=1, source_target_pairs={{0,4},{4,12},{12,8},{8,0},{1,5},{5,13},{13,9},{9,1},{2,6},{6,14},{... | collective-permute-start | bytes 393224 | tf_op jit(solution)/shard_map/ppermute | solution.py:266
  57.3 22.7 %collective-permute-start.21 = (bf16[32,2048]{1,0:T(8,128)(2,1)S(1)}, bf16[32,2048]{1,0:T(8,128)(2,1)S(1)}, u32[]{:S(2)}, u32[]{:S(2)}) collective-permute-start(bf16[32,2048]{1,0:T(8,128)(2,1)S(1)} %collective-permute-done.11.refs_6_.refs_4_.refs_2_), channel_id=1, source_target_pairs={{0,4},{4,12},{12,8},{8,0},{1,5},{5,13},{13,9},{9,1},{2,6},{6,14},{... | collective-permute-start | bytes 393224 | tf_op jit(solution)/shard_map/ppermute | solution.py:266
  59.3 11.6 %collective-permute-start.20 = (bf16[128,256]{1,0:T(8,128)(2,1)S(1)}, bf16[128,256]{1,0:T(8,128)(2,1)S(1)}, u32[]{:S(2)}, u32[]{:S(2)}) collective-permute-start(bf16[128,256]{1,0:T(8,128)(2,1)S(1)} %get-tuple-element.71.refs_19_), channel_id=1, source_target_pairs={{4,0},{12,4},{8,12},{0,8},{5,1},{13,5},{9,13},{1,9},{6,2},{14,6},{... | collective-permute-start | bytes 196616 | tf_op jit(solution)/shard_map/ppermute | solution.py:314
  62.7 9.6 %collective-permute-start.19 = (bf16[128,256]{1,0:T(8,128)(2,1)S(1)}, bf16[128,256]{1,0:T(8,128)(2,1)S(1)}, u32[]{:S(2)}, u32[]{:S(2)}) collective-permute-start(bf16[128,256]{1,0:T(8,128)(2,1)S(1)} %get-tuple-element.76.refs_13_), channel_id=1, source_target_pairs={{0,4},{4,12},{12,8},{8,0},{1,5},{5,13},{13,9},{9,1},{2,6},{6,14},{... | collective-permute-start | bytes 196616 | tf_op jit(solution)/shard_map/ppermute | solution.py:312
  65.5 14.5 %collective-permute-start.22 = (bf16[32,2048]{1,0:T(8,128)(2,1)S(1)}, bf16[32,2048]{1,0:T(8,128)(2,1)S(1)}, u32[]{:S(2)}, u32[]{:S(2)}) collective-permute-start(bf16[32,2048]{1,0:T(8,128)(2,1)S(1)} %collective-permute-done.12.refs_7_.refs_5_.refs_3_), channel_id=1, source_target_pairs={{0,4},{4,12},{12,8},{8,0},{1,5},{5,13},{13,9},{9,1},{2,6},{6,14},{... | collective-permute-start | bytes 393224 | tf_op jit(solution)/shard_map/ppermute | solution.py:266
  80.3 3.3 %collective-permute-start.25 = (f32[128,64]{1,0:T(8,128)S(1)}, f32[128,64]{1,0:T(8,128)S(1)}, u32[]{:S(2)}, u32[]{:S(2)}) collective-permute-start(f32[128,64]{1,0:T(8,128)S(1)} %shard_map.136), channel_id=1, source_target_pairs={{0,1},{1,0},{2,3},{3,2},{4,5},{5,4},{6,7},{7,6},{8,9},{9,8},{10,11... | collective-permute-start | bytes 98312 | tf_op jit(solution)/shard_map/ppermute | solution.py:60
  80.4 7.6 %collective-permute-start.23 = (bf16[32,2048]{1,0:T(8,128)(2,1)S(1)}, bf16[32,2048]{1,0:T(8,128)(2,1)S(1)}, u32[]{:S(2)}, u32[]{:S(2)}) collective-permute-start(bf16[32,2048]{1,0:T(8,128)(2,1)S(1)} %collective-permute-done.21.refs_6_.refs_4_), channel_id=1, source_target_pairs={{0,4},{4,12},{12,8},{8,0},{1,5},{5,13},{13,9},{9,1},{2,6},{6,14},{... | collective-permute-start | bytes 393224 | tf_op jit(solution)/shard_map/ppermute | solution.py:266
  80.4 9.5 %collective-permute-start.24 = (bf16[32,2048]{1,0:T(8,128)(2,1)S(1)}, bf16[32,2048]{1,0:T(8,128)(2,1)S(1)}, u32[]{:S(2)}, u32[]{:S(2)}) collective-permute-start(bf16[32,2048]{1,0:T(8,128)(2,1)S(1)} %collective-permute-done.22.refs_7_.refs_5_), channel_id=1, source_target_pairs={{0,4},{4,12},{12,8},{8,0},{1,5},{5,13},{13,9},{9,1},{2,6},{6,14},{... | collective-permute-start | bytes 393224 | tf_op jit(solution)/shard_map/ppermute | solution.py:266
  83.6 4.3 %collective-permute-start.26 = (f32[128,64]{1,0:T(8,128)S(1)}, f32[128,64]{1,0:T(8,128)S(1)}, u32[]{:S(2)}, u32[]{:S(2)}) collective-permute-start(f32[128,64]{1,0:T(8,128)S(1)} %add.247), channel_id=1, source_target_pairs={{0,2},{1,3},{2,0},{3,1},{4,6},{5,7},{6,4},{7,5},{8,10},{9,11},{10,... | collective-permute-start | bytes 98312 | tf_op jit(solution)/shard_map/ppermute | solution.py:60
where the time goes:
time: 91.3 us; the launch traced here: 91.1 us
  starting transfers between devices  42.9 us (47%)
  waiting for transfers between devices  27.2 us (30%)
  Pallas kernels  9.25 us (10%)
  local copies, waits for them, and re-layouts  4.45 us (5%)
  other arithmetic  3.71 us (4%)
  between operations  3.64 us (4%)
    ppermute x17, starting transfers between devices, stream_to(): arrived.append(lax.ppermute(moving, 'ctx', pairs))  32.8 us
    ppermute x17, waiting for transfers between devices, stream_to(): arrived.append(lax.ppermute(moving, 'ctx', pairs))  18.7 us
    pallas_call x7, Pallas kernels, chunk_call(): pl.pallas_call(body, out_shape=pltpu.VMEM(out_shape.shape, out_shape.dtyp...  9.25 us
    ppermute x6, waiting for transfers between devices, doubling_sums(): other = lax.ppermute(sent, axis, pairs)  5.17 us
    ppermute x6, starting transfers between devices, doubling_sums(): other = lax.ppermute(sent, axis, pairs)  4.89 us
    reshape x3, local copies, waits for them, and re-layouts, pick(): return lax.dynamic_slice(stored, (0, chosen, first, 0), (1, 1, rows, stor...  3.45 us
    ppermute x1, starting transfers between devices, shards(): far = lax.ppermute(back[:, pair_width:], 'ctx', backward)  2.32 us
    ppermute x1, starting transfers between devices, shards(): back = lax.ppermute(back, 'ctx', backward)  1.93 us
  transfers between devices with their start and end apart: 27, of which 17 were waited for; matrix products, arithmetic and copies ran while one was open for 5% of the time, Pallas kernels for 9%

commit v1 on v0

--- a/solution.py
+++ b/solution.py
@@ -1,4 +1,5 @@
 import functools
+import math
 
 import jax
 import jax.numpy as jnp
@@ -11,9 +12,10 @@
 HEAD_SIZE = 128
 ADAPTER_RANK = 64
 NEG_BIG = -1e30
-CHUNK_ROWS = 32
-LAG = 2
-PIECES = 2
+EXPONENT_SCALE = HEAD_SIZE ** (-0.5) * math.log2(math.e)
+CHUNK_ROWS = 16
+LAG = 4
+PIECES = 4
 KERNEL_VMEM = 8 << 20
 
 
@@ -84,7 +86,7 @@
 
 def chunk_call(kernel, behind, candidates, chunks, operands, out_shape):
     names = sorted(chunks)
-    rows, width = chunks[names[0]].shape
+    rows, width = CHUNK_ROWS, chunks[names[0]].shape[1]
     number = len(candidates[0])
 
     def body(behind_ref, *refs):
@@ -94,8 +96,8 @@
 
             @pl.when(behind_ref[0] == distance)
             def _(held=held):
-                for i, name in enumerate(held):
-                    weight_ref[i * rows : (i + 1) * rows, :] = chunk_refs[name][...]
+                for i, (name, row) in enumerate(held):
+                    weight_ref[i * rows : (i + 1) * rows, :] = chunk_refs[name][row : row + rows]
 
         kernel(weight_ref, *refs[len(names) : -1])
 
@@ -111,6 +113,58 @@
         *[
             pltpu.with_memory_space_constraint(x, pltpu.VMEM)
             for x in [chunks[name] for name in names] + operands
+        ],
+    )
+
+
+def own_chunks(chunk_range, publisher, version, down, up_query, up_pair, out_down, out_up):
+    rank = ADAPTER_RANK
+    width = down.shape[-1]
+    pair_width = up_pair.shape[-1]
+    fold = width // pair_width
+    pair_rows = 2 * rank // fold
+    plan = [(0, rank + first) for first in range(0, 2 * rank, CHUNK_ROWS)] + [(2, 0)]
+    plan += [(0, first) for first in range(0, rank, CHUNK_ROWS)]
+    for weight in (1, 3, 4):
+        plan += [(weight, first) for first in range(0, rank, CHUNK_ROWS)]
+    plan = plan[chunk_range]
+
+    def body(publisher_ref, version_ref, *refs):
+        weights, outs, sem = refs[:5], refs[5:-1], refs[-1]
+        chosen = version_ref[publisher_ref[0]]
+        copies = []
+        for (which, first), out in zip(plan, outs):
+            if which != 2:
+                rows = weights[which].at[0, chosen, pl.ds(first, CHUNK_ROWS)]
+                copies.append((rows, out))
+                continue
+            for i in range(fold):
+                half, row = divmod(i * pair_rows, rank)
+                rows = weights[which].at[0, chosen, half, pl.ds(row, pair_rows)]
+                lanes = pl.ds(i * pair_width, pair_width)
+                copies.append((rows, out.at[pl.ds(0, pair_rows), lanes]))
+        copies = [
+            pltpu.make_async_copy(rows, out, sem.at[i]) for i, (rows, out) in enumerate(copies)
+        ]
+        for copy in copies:
+            copy.start()
+        for copy in copies:
+            copy.wait()
+
+    in_place = pl.BlockSpec(memory_space=pltpu.HBM)
+    return pl.pallas_call(
+        body,
+        out_shape=[pltpu.VMEM((CHUNK_ROWS, width), jnp.bfloat16)] * len(plan),
+        in_specs=[SMEM, SMEM] + [in_place] * 5,
+        out_specs=[VMEM] * len(plan),
+        scratch_shapes=[pltpu.SemaphoreType.DMA((len(plan) + fold - 1,))],
+        compiler_params=pltpu.CompilerParams(vmem_limit_bytes=KERNEL_VMEM),
+    )(
+        publisher,
+        version,
+        *[
+            pltpu.with_memory_space_constraint(x, pltpu.HBM)
+            for x in (down, up_query, up_pair, out_down, out_up)
         ],
     )
 
@@ -160,13 +214,12 @@
 
 
 def attend_kernel(
-    first_head, group_size, block_count, weight_ref, low_ref, base_ref, tables_ref, query_pos_ref, key_pos_ref, *refs
+    first_head, group_size, block_count, weight_ref, low_ref, base_ref, tables_ref, hidden_ref, *refs
 ):
     key_refs = refs[:block_count]
     value_refs = refs[block_count : 2 * block_count]
     out_ref = refs[-1]
     low = low_ref[...].astype(jnp.bfloat16)
-    visible = key_pos_ref[...] <= query_pos_ref[...]
     group = None
     for lane in range(0, out_ref.shape[1], HEAD_SIZE):
         head = first_head + lane // HEAD_SIZE
@@ -182,9 +235,9 @@
         queries = rotate(queries, tables_ref[...]).astype(jnp.bfloat16)
         scores = lax.dot_general(
             queries, keys, CONTRACT_LAST, preferred_element_type=jnp.float32
-        ) * HEAD_SIZE ** (-0.5)
-        scores = jnp.where(visible, scores, NEG_BIG)
-        raw = jnp.exp(scores - jnp.max(scores, axis=1, keepdims=True))
+        )
+        scores = scores + hidden_ref[...]
+        raw = jnp.exp2((scores - jnp.max(scores, axis=1, keepdims=True)) * EXPONENT_SCALE)
         totals = jnp.sum(raw, axis=1, keepdims=True)
         mixed = jnp.dot(raw.astype(jnp.bfloat16), values, preferred_element_type=jnp.float32)
         out_ref[:, lane : lane + HEAD_SIZE] = (mixed / totals).astype(jnp.bfloat16)
@@ -215,67 +268,59 @@
     output_up_weight,
 ):
     rank = ADAPTER_RANK
-    width = hidden.shape[1]
-    source = publisher[0]
-    slots = jnp.arange(version.shape[0], dtype=jnp.int32)
-    chosen = jnp.sum(jnp.where(slots == source, version, 0))
     count = lax.axis_size("ctx")
     own_index = lax.axis_index("ctx")
     place = ring_place(own_index, count)
+    pair_width = adapter_up_key_value.shape[-1]
+    weights = (
+        adapter_down_weight,
+        adapter_up_query,
+        adapter_up_key_value,
+        output_down_weight,
+        output_up_weight,
+    )
+    own = []
+    for chunk_range in (slice(0, LAG), slice(LAG, None)):
+        own += own_chunks(chunk_range, publisher, version, *weights)
+    per = rank // CHUNK_ROWS
+
+    pairs = ring_pairs(count)
+    arrived, sent = [], []
+    for turn in range(LAG):
+        sent.append(own[turn])
+        arrived.append(lax.ppermute(own[turn], "ctx", pairs))
+    source = after(publisher, *sent)[0]
     behind = (place - ring_place(source, count)) % count
     is_source = behind == 0
-
-    def pick(stored, first, rows):
-        return lax.dynamic_slice(
-            stored, (0, chosen, first, 0), (1, 1, rows, stored.shape[-1])
-        ).reshape(rows, stored.shape[-1])
-
-    pair_width = adapter_up_key_value.shape[-1]
-    fold = width // pair_width
-    pair_rows = 2 * rank // fold
-    own_pair = lax.dynamic_index_in_dim(adapter_up_key_value[0], chosen, 0, keepdims=False)
-    own_pair = own_pair.reshape(fold, pair_rows, pair_width).transpose(1, 0, 2)
-    own_pair = own_pair.reshape(pair_rows, width)
-
-    def pieces(stored, first, rows):
-        return [pick(stored, first + i, CHUNK_ROWS) for i in range(0, rows, CHUNK_ROWS)]
-
-    own = (
-        pieces(adapter_down_weight, rank, 2 * rank)
-        + pieces(adapter_down_weight, 0, rank)
-        + [jnp.pad(own_pair, ((0, CHUNK_ROWS - pair_rows), (0, 0)))]
-        + pieces(adapter_up_query, 0, rank)
-        + pieces(output_down_weight, 0, rank)
-        + pieces(output_up_weight, 0, rank)
-    )
-    per = rank // CHUNK_ROWS
-
-    pairs = ring_pairs(count)
-    arrived, sent = [], []
-    own[LAG:] = lax.optimization_barrier(own[LAG:])
-
-    def stream_to(last):
-        for turn in range(len(sent), last):
-            if turn < LAG:
-                moving = own[turn]
-            else:
-                moving = after(arrived[turn - LAG], sent[-1])
-                if turn < len(own):
-                    moving = jnp.where(is_source, own[turn], moving)
-            sent.append(moving)
-            arrived.append(lax.ppermute(moving, "ctx", pairs))
-
-    drain = LAG * (count - 2)
+    for turn in range(LAG, len(own)):
+        moving = after(arrived[turn - LAG], sent[-1])
+        moving = jnp.where(is_source, own[turn], moving)
+        sent.append(moving)
+        arrived.append(lax.ppermute(moving, "ctx", pairs))
+    late = []
+    for _ in range(count - 2):
+        moving = late[-1] if late else jnp.concatenate(arrived[-LAG:], axis=0)
+        late.append(lax.ppermute(moving, "ctx", pairs))
+    stored_block_order = after(stored_block_order, sent[3 * LAG])
 
     distance = jnp.full((1,), behind, jnp.int32)
 
     def on_chunks(kernel, first, number, operands, shape, dtype):
-        chunks = {("own", first + i): own[first + i] for i in range(number)}
-        candidates = [[("own", first + i) for i in range(number)]]
-        for hop in range(count - 1):
-            turns = [first + i + LAG * hop for i in range(number)]
-            candidates.append([("ring", turn) for turn in turns])
-            chunks.update({("ring", turn): arrived[turn] for turn in turns})
+        chunks, candidates = {}, []
+        for hop in range(-1, count - 1):
+            held = []
+            for k in range(first, first + number):
+                turn = k + LAG * hop
+                if hop < 0:
+                    key, row, array = ("own", k), 0, own[k]
+                elif turn < len(own):
+                    key, row, array = ("ring", turn), 0, arrived[turn]
+                else:
+                    group, row = divmod(turn - len(own), LAG)
+                    key, row, array = ("late", group), row * CHUNK_ROWS, late[group]
+                chunks[key] = array
+                held.append((key, row))
+            candidates.append(held)
         return chunk_call(
             kernel, distance, candidates, chunks, operands, jax.ShapeDtypeStruct(shape, dtype)
         )
@@ -285,14 +330,13 @@
     query_pos = token_positions(stored_block_order, own_index * local_rows, local_rows, half_rows)
     tables = rotation_tables(query_pos)
 
-    stream_to(len(own) + drain)
     part = on_chunks(low_kernel, 0, 2 * per, [hidden], (local_rows, 2 * rank), jnp.float32)
     pair_sums = doubling_sums(part, "tp", jnp.float32)
-    part = on_chunks(low_kernel, 2 * per, per, [hidden], (local_rows, rank), jnp.float32)
+    part = on_chunks(low_kernel, 2 * per + 1, per, [hidden], (local_rows, rank), jnp.float32)
     query_sums = doubling_sums(part, "tp", jnp.float32)
     both = on_chunks(
         pair_kernel,
-        3 * per,
+        2 * per,
         1,
         [pair_sums[-1], base_key_rows, base_value_rows, tables],
         (local_rows, 2 * pair_width),
@@ -325,6 +369,7 @@
             for o in offsets
         ]
     )
+    hide = jnp.where(key_pos[None, :] <= query_pos[:, None], 0.0, NEG_BIG)
     local_heads = base_query_rows.shape[1] // HEAD_SIZE
     group_size = local_heads // (pair_width // HEAD_SIZE)
     piece_heads = local_heads // PIECES
@@ -333,7 +378,7 @@
             functools.partial(attend_kernel, piece * piece_heads, group_size, len(offsets)),
             3 * per + 1,
             per,
-            [query_sums[-1], base_query_rows, tables, query_pos[:, None], key_pos[None, :]]
+            [query_sums[-1], base_query_rows, tables, hide]
             + [key_blocks[o] for o in offsets]
             + [value_blocks[o] for o in offsets],
             (local_rows, piece_heads * HEAD_SIZE),
@@ -342,10 +387,9 @@
         for piece in range(PIECES)
     ]
     attended = jnp.concatenate(pieces_out, axis=1)
-    late = 4 * per + 1
-    part = on_chunks(low_kernel, late, per, pieces_out, (local_rows, rank), jnp.float32)
+    part = on_chunks(low_kernel, 4 * per + 1, per, pieces_out, (local_rows, rank), jnp.float32)
     out_low = doubling_sums(part, "tp", jnp.float32)[-1]
-    adapted = on_chunks(up_kernel, late + per, per, [out_low], attended.shape, jnp.bfloat16)
+    adapted = on_chunks(up_kernel, 5 * per + 1, per, [out_low], attended.shape, jnp.bfloat16)
     return (attended, adapted)
 
 

time: 91.3 us -> 86.2 us (0.944)
  waiting for transfers between devices: 27.2 us -> 19.3 us
  starting transfers between devices: 42.9 us -> 48.1 us
  Pallas kernels: 9.25 us -> 13.3 us
  local copies, waits for them, and re-layouts: 4.45 us -> 1.51 us
  other arithmetic: 3.71 us -> 1.85 us
  between operations: 3.64 us -> 1.8 us
    ppermute x17 -> x27, waiting for transfers between devices: 18.7 us -> 5.47 us  [the longest x2 4.01 us: shards(): late.append(lax.ppermute(moving, 'ctx', pairs))]
    ppermute x1, waiting for transfers between devices: 0.92 us -> 6.87 us  [shards(): far = lax.ppermute(back[:, pair_width:], 'ctx', backward)]
    ppermute x17 -> x27, starting transfers between devices: 32.8 us -> 37.6 us  [the longest x21 29 us: shards(): arrived.append(lax.ppermute(moving, 'ctx', pairs))]
    pallas_call x0 -> x2, Pallas kernels: none -> 3.78 us  [own_chunks(): pl.pallas_call(body, out_shape=[pltpu.VMEM((CHUNK_ROWS, width), jnp.bfloa...]
    reshape x4 -> x0, local copies, waits for them, and re-layouts: 3.46 us -> none  [the longest x3 3.45 us: pick(): return lax.dynamic_slice(stored, (0, chosen, first, 0), (1, 1, rows, stor...]
    reduce_sum x1 -> x0, other arithmetic: 1.29 us -> none  [shards(): chosen = jnp.sum(jnp.where(slots == source, version, 0))]
    pallas_call x7 -> x9, Pallas kernels: 9.25 us -> 9.56 us  [chunk_call(): pl.pallas_call(body, out_shape=pltpu.VMEM(out_shape.shape, out_shape.dtyp...]
  transfers between devices with their start and end apart: 27 -> 37, of which waited for: 17 -> 12; matrix products, arithmetic and copies ran while one was open for 5% -> 2% of each run, Pallas kernels for 9% -> 13%
where the time goes in v1:
time: 86.2 us; the launch traced here: 85.9 us
  starting transfers between devices  48.1 us (56%)
  waiting for transfers between devices  19.3 us (22%)
  Pallas kernels  13.3 us (15%)
  other arithmetic  1.85 us (2%)
  between operations  1.8 us (2%)
  local copies, waits for them, and re-layouts  1.51 us (2%)
    ppermute x21, starting transfers between devices, shards(): arrived.append(lax.ppermute(moving, 'ctx', pairs))  29 us
    pallas_call x9, Pallas kernels, chunk_call(): pl.pallas_call(body, out_shape=pltpu.VMEM(out_shape.shape, out_shape.dtyp...  9.56 us
    ppermute x1, waiting for transfers between devices, shards(): far = lax.ppermute(back[:, pair_width:], 'ctx', backward)  6.87 us
    ppermute x4, starting transfers between devices, shards(): arrived.append(lax.ppermute(own[turn], 'ctx', pairs))  6.21 us
    ppermute x6, waiting for transfers between devices, doubling_sums(): other = lax.ppermute(sent, axis, pairs)  4.99 us
    ppermute x6, starting transfers between devices, doubling_sums(): other = lax.ppermute(sent, axis, pairs)  4.76 us
    ppermute x2, waiting for transfers between devices, shards(): late.append(lax.ppermute(moving, 'ctx', pairs))  4.01 us
    pallas_call x2, Pallas kernels, own_chunks(): pl.pallas_call(body, out_shape=[pltpu.VMEM((CHUNK_ROWS, width), jnp.bfloa...  3.78 us
  transfers between devices with their start and end apart: 37, of which 12 were waited for; matrix products, arithmetic and copies ran while one was open for 2% of the time, Pallas kernels for 13%

profile of v1, /device:TPU:0, one launch (start us, length us, event | category | flops | bytes accessed | tf_op | source)
XLA Modules:
  0.0 85.9 jit_solution(3143117584421723666)
XLA Ops:
  1.3 0.6 copy-done.4
  1.9 1.6 %shard_map.131 = (bf16[16,2048]{1,0:T(8,128)(2,1)S(1)}, bf16[16,2048]{1,0:T(8,128)(2,1)S(1)}, bf16[16,2048]{1,0:T(8,128)(2,1)S(1)}, bf16[16,2048]{1,0:T(8,128)(2,1)S(1)}) custom-call(s32[1]{0:T(128)S(6)} %copy.16.publisher_ref, s32[4]{0:T(128)S(1)} %copy-done.4, bf16[1,4,192,2048]{3,2,1,0:T(8,128)(2,1)} %refs_0_.3, bf16[1,4,64,2048]{3,2,1,0:T(8,128)(2,1)} %refs_1_.3, ...), custom_call_target="tpu_custom_call" | custom-call | tf_op jit(solution)/shard_map/pallas_call | solution.py:155
  3.5 3.1 %collective-permute-start.1 = (bf16[16,2048]{1,0:T(8,128)(2,1)S(1)}, bf16[16,2048]{1,0:T(8,128)(2,1)S(1)}, u32[]{:S(2)}, u32[]{:S(2)}) collective-permute-start(bf16[16,2048]{1,0:T(8,128)(2,1)S(1)} %get-tuple-element.50.refs_0_), channel_id=1, source_target_pairs={{0,4},{4,12},{12,8},{8,0},{1,5},{5,13},{13,9},{9,1},{2,6},{6,14},{... | collective-permute-start | bytes 196616 | tf_op jit(solution)/shard_map/ppermute | solution.py:291
  6.6 2.6 %collective-permute-start = (bf16[16,2048]{1,0:T(8,128)(2,1)S(1)}, bf16[16,2048]{1,0:T(8,128)(2,1)S(1)}, u32[]{:S(2)}, u32[]{:S(2)}) collective-permute-start(bf16[16,2048]{1,0:T(8,128)(2,1)S(1)} %get-tuple-element.51.refs_1_), channel_id=1, source_target_pairs={{0,4},{4,12},{12,8},{8,0},{1,5},{5,13},{13,9},{9,1},{2,6},{6,14},{... | collective-permute-start | bytes 196616 | tf_op jit(solution)/shard_map/ppermute | solution.py:291
  9.2 0.4 collective-permute-start.5
  9.8 2.2 %shard_map.132 = (bf16[16,2048]{1,0:T(8,128)(2,1)S(1)}, bf16[16,2048]{1,0:T(8,128)(2,1)S(1)}, bf16[16,2048]{1,0:T(8,128)(2,1)S(1)}, bf16[16,2048]{1,0:T(8,128)(2...) custom-call(s32[1]{0:T(128)S(6)} %copy.16.publisher_ref, ...), custom_call_target="tpu_custom_call" | custom-call | tf_op jit(solution)/shard_map/pallas_call | solution.py:155
  12.2 1.9 %collective-permute-start.3 = (bf16[16,2048]{1,0:T(8,128)(2,1)S(1)}, bf16[16,2048]{1,0:T(8,128)(2,1)S(1)}, u32[]{:S(2)}, u32[]{:S(2)}) collective-permute-start(bf16[16,2048]{1,0:T(8,128)(2,1)S(1)} %broadcast_select_fusion.20), channel_id=1, source_target_pairs={{0,4},{4,12},{12,8},{8,0},{1,5},{5,13},{13,9},{9,1},{2,6},{6,14},{... | collective-permute-start | bytes 196616 | tf_op jit(solution)/shard_map/ppermute | solution.py:299
  14.1 2.6 %collective-permute-start.2 = (bf16[16,2048]{1,0:T(8,128)(2,1)S(1)}, bf16[16,2048]{1,0:T(8,128)(2,1)S(1)}, u32[]{:S(2)}, u32[]{:S(2)}) collective-permute-start(bf16[16,2048]{1,0:T(8,128)(2,1)S(1)} %broadcast_select_fusion.19), channel_id=1, source_target_pairs={{0,4},{4,12},{12,8},{8,0},{1,5},{5,13},{13,9},{9,1},{2,6},{6,14},{... | collective-permute-start | bytes 196616 | tf_op jit(solution)/shard_map/ppermute | solution.py:299
  16.7 0.5 collective-permute-start.9
  17.6 1.7 %collective-permute-start.7 = (bf16[16,2048]{1,0:T(8,128)(2,1)S(1)}, bf16[16,2048]{1,0:T(8,128)(2,1)S(1)}, u32[]{:S(2)}, u32[]{:S(2)}) collective-permute-start(bf16[16,2048]{1,0:T(8,128)(2,1)S(1)} %broadcast_select_fusion.16), channel_id=1, source_target_pairs={{0,4},{4,12},{12,8},{8,0},{1,5},{5,13},{13,9},{9,1},{2,6},{6,14},{... | collective-permute-start | bytes 196616 | tf_op jit(solution)/shard_map/ppermute | solution.py:299
  19.3 0.7 collective-permute-done.2.refs_13_
  20.0 2.5 %collective-permute-start.6 = (bf16[16,2048]{1,0:T(8,128)(2,1)S(1)}, bf16[16,2048]{1,0:T(8,128)(2,1)S(1)}, u32[]{:S(2)}, u32[]{:S(2)}) collective-permute-start(bf16[16,2048]{1,0:T(8,128)(2,1)S(1)} %broadcast_select_fusion.15), channel_id=1, source_target_pairs={{0,4},{4,12},{12,8},{8,0},{1,5},{5,13},{13,9},{9,1},{2,6},{6,14},{... | collective-permute-start | bytes 196616 | tf_op jit(solution)/shard_map/ppermute | solution.py:299
  22.7 0.6 collective-permute-start.11
  23.4 1.3 %collective-permute-start.13 = (bf16[16,2048]{1,0:T(8,128)(2,1)S(1)}, bf16[16,2048]{1,0:T(8,128)(2,1)S(1)}, u32[]{:S(2)}, u32[]{:S(2)}) collective-permute-start(bf16[16,2048]{1,0:T(8,128)(2,1)S(1)} %broadcast_select_fusion.13), channel_id=1, source_target_pairs={{0,4},{4,12},{12,8},{8,0},{1,5},{5,13},{13,9},{9,1},{2,6},{6,14},{... | collective-permute-start | bytes 196616 | tf_op jit(solution)/shard_map/ppermute | solution.py:299
  24.8 1.3 %collective-permute-start.15 = (bf16[16,2048]{1,0:T(8,128)(2,1)S(1)}, bf16[16,2048]{1,0:T(8,128)(2,1)S(1)}, u32[]{:S(2)}, u32[]{:S(2)}) collective-permute-start(bf16[16,2048]{1,0:T(8,128)(2,1)S(1)} %broadcast_select_fusion.12), channel_id=1, source_target_pairs={{0,4},{4,12},{12,8},{8,0},{1,5},{5,13},{13,9},{9,1},{2,6},{6,14},{... | collective-permute-start | bytes 196616 | tf_op jit(solution)/shard_map/ppermute | solution.py:299
  26.2 2.0 %collective-permute-start.10 = (bf16[16,2048]{1,0:T(8,128)(2,1)S(1)}, bf16[16,2048]{1,0:T(8,128)(2,1)S(1)}, u32[]{:S(2)}, u32[]{:S(2)}) collective-permute-start(bf16[16,2048]{1,0:T(8,128)(2,1)S(1)} %broadcast_select_fusion.11), channel_id=1, source_target_pairs={{0,4},{4,12},{12,8},{8,0},{1,5},{5,13},{13,9},{9,1},{2,6},{6,14},{... | collective-permute-start | bytes 196616 | tf_op jit(solution)/shard_map/ppermute | solution.py:299
  28.4 1.2 %collective-permute-start.12 = (bf16[16,2048]{1,0:T(8,128)(2,1)S(1)}, bf16[16,2048]{1,0:T(8,128)(2,1)S(1)}, u32[]{:S(2)}, u32[]{:S(2)}) collective-permute-start(bf16[16,2048]{1,0:T(8,128)(2,1)S(1)} %broadcast_select_fusion.10), channel_id=1, source_target_pairs={{0,4},{4,12},{12,8},{8,0},{1,5},{5,13},{13,9},{9,1},{2,6},{6,14},{... | collective-permute-start | bytes 196616 | tf_op jit(solution)/shard_map/ppermute | solution.py:299
  29.6 1.4 %collective-permute-start.14 = (bf16[16,2048]{1,0:T(8,128)(2,1)S(1)}, bf16[16,2048]{1,0:T(8,128)(2,1)S(1)}, u32[]{:S(2)}, u32[]{:S(2)}) collective-permute-start(bf16[16,2048]{1,0:T(8,128)(2,1)S(1)} %broadcast_select_fusion.9), channel_id=1, source_target_pairs={{0,4},{4,12},{12,8},{8,0},{1,5},{5,13},{13,9},{9,1},{2,6},{6,14},{... | collective-permute-start | bytes 196616 | tf_op jit(solution)/shard_map/ppermute | solution.py:299
  31.5 1.3 %collective-permute-start.16 = (bf16[16,2048]{1,0:T(8,128)(2,1)S(1)}, bf16[16,2048]{1,0:T(8,128)(2,1)S(1)}, u32[]{:S(2)}, u32[]{:S(2)}) collective-permute-start(bf16[16,2048]{1,0:T(8,128)(2,1)S(1)} %broadcast_select_fusion.8), channel_id=1, source_target_pairs={{0,4},{4,12},{12,8},{8,0},{1,5},{5,13},{13,9},{9,1},{2,6},{6,14},{... | collective-permute-start | bytes 196616 | tf_op jit(solution)/shard_map/ppermute | solution.py:299
  32.8 1.3 %collective-permute-start.17 = (bf16[16,2048]{1,0:T(8,128)(2,1)S(1)}, bf16[16,2048]{1,0:T(8,128)(2,1)S(1)}, u32[]{:S(2)}, u32[]{:S(2)}) collective-permute-start(bf16[16,2048]{1,0:T(8,128)(2,1)S(1)} %broadcast_select_fusion.7), channel_id=1, source_target_pairs={{0,4},{4,12},{12,8},{8,0},{1,5},{5,13},{13,9},{9,1},{2,6},{6,14},{... | collective-permute-start | bytes 196616 | tf_op jit(solution)/shard_map/ppermute | solution.py:299
  34.2 1.1 %collective-permute-start.18 = (bf16[16,2048]{1,0:T(8,128)(2,1)S(1)}, bf16[16,2048]{1,0:T(8,128)(2,1)S(1)}, u32[]{:S(2)}, u32[]{:S(2)}) collective-permute-start(bf16[16,2048]{1,0:T(8,128)(2,1)S(1)} %broadcast_select_fusion.6), channel_id=1, source_target_pairs={{0,4},{4,12},{12,8},{8,0},{1,5},{5,13},{13,9},{9,1},{2,6},{6,14},{... | collective-permute-start | bytes 196616 | tf_op jit(solution)/shard_map/ppermute | solution.py:299
  35.6 1.3 %collective-permute-start.19 = (bf16[16,2048]{1,0:T(8,128)(2,1)S(1)}, bf16[16,2048]{1,0:T(8,128)(2,1)S(1)}, u32[]{:S(2)}, u32[]{:S(2)}) collective-permute-start(bf16[16,2048]{1,0:T(8,128)(2,1)S(1)} %broadcast_select_fusion.5), channel_id=1, source_target_pairs={{0,4},{4,12},{12,8},{8,0},{1,5},{5,13},{13,9},{9,1},{2,6},{6,14},{... | collective-permute-start | bytes 196616 | tf_op jit(solution)/shard_map/ppermute | solution.py:299
  37.4 1.4 %collective-permute-start.20 = (bf16[16,2048]{1,0:T(8,128)(2,1)S(1)}, bf16[16,2048]{1,0:T(8,128)(2,1)S(1)}, u32[]{:S(2)}, u32[]{:S(2)}) collective-permute-start(bf16[16,2048]{1,0:T(8,128)(2,1)S(1)} %broadcast_select_fusion.4), channel_id=1, source_target_pairs={{0,4},{4,12},{12,8},{8,0},{1,5},{5,13},{13,9},{9,1},{2,6},{6,14},{... | collective-permute-start | bytes 196616 | tf_op jit(solution)/shard_map/ppermute | solution.py:299
  38.8 1.0 %collective-permute-start.21 = (bf16[16,2048]{1,0:T(8,128)(2,1)S(1)}, bf16[16,2048]{1,0:T(8,128)(2,1)S(1)}, u32[]{:S(2)}, u32[]{:S(2)}) collective-permute-start(bf16[16,2048]{1,0:T(8,128)(2,1)S(1)} %broadcast_select_fusion.3), channel_id=1, source_target_pairs={{0,4},{4,12},{12,8},{8,0},{1,5},{5,13},{13,9},{9,1},{2,6},{6,14},{... | collective-permute-start | bytes 196616 | tf_op jit(solution)/shard_map/ppermute | solution.py:299
  39.8 1.4 %collective-permute-start.22 = (bf16[16,2048]{1,0:T(8,128)(2,1)S(1)}, bf16[16,2048]{1,0:T(8,128)(2,1)S(1)}, u32[]{:S(2)}, u32[]{:S(2)}) collective-permute-start(bf16[16,2048]{1,0:T(8,128)(2,1)S(1)} %broadcast_select_fusion.2), channel_id=1, source_target_pairs={{0,4},{4,12},{12,8},{8,0},{1,5},{5,13},{13,9},{9,1},{2,6},{6,14},{... | collective-permute-start | bytes 196616 | tf_op jit(solution)/shard_map/ppermute | solution.py:299
  41.3 1.3 %collective-permute-start.23 = (bf16[16,2048]{1,0:T(8,128)(2,1)S(1)}, bf16[16,2048]{1,0:T(8,128)(2,1)S(1)}, u32[]{:S(2)}, u32[]{:S(2)}) collective-permute-start(bf16[16,2048]{1,0:T(8,128)(2,1)S(1)} %broadcast_select_fusion.1), channel_id=1, source_target_pairs={{0,4},{4,12},{12,8},{8,0},{1,5},{5,13},{13,9},{9,1},{2,6},{6,14},{... | collective-permute-start | bytes 196616 | tf_op jit(solution)/shard_map/ppermute | solution.py:299
  42.6 1.6 %collective-permute-start.28 = (f32[128,128]{1,0:T(8,128)S(1)}, f32[128,128]{1,0:T(8,128)S(1)}, u32[]{:S(2)}, u32[]{:S(2)}) collective-permute-start(f32[128,128]{1,0:T(8,128)S(1)} %add.205), channel_id=1, source_target_pairs={{0,2},{1,3},{2,0},{3,1},{4,6},{5,7},{6,4},{7,5},{8,10},{9,11},{10,... | collective-permute-start | bytes 196616 | tf_op jit(solution)/shard_map/ppermute | solution.py:62
  44.2 1.4 %collective-permute-start.24 = (bf16[16,2048]{1,0:T(8,128)(2,1)S(1)}, bf16[16,2048]{1,0:T(8,128)(2,1)S(1)}, u32[]{:S(2)}, u32[]{:S(2)}) collective-permute-start(bf16[16,2048]{1,0:T(8,128)(2,1)S(1)} %broadcast_select_fusion), channel_id=1, source_target_pairs={{0,4},{4,12},{12,8},{8,0},{1,5},{5,13},{13,9},{9,1},{2,6},{6,14},{... | collective-permute-start | bytes 196616 | tf_op jit(solution)/shard_map/ppermute | solution.py:299
  45.9 1.1 %collective-permute-done.28 = f32[128,128]{1,0:T(8,128)S(1)} collective-permute-done((f32[128,128]{1,0:T(8,128)S(1)}, f32[128,128]{1,0:T(8,128)S(1)}, u32[]{:S(2)}, u32[]{:S(2)}) %collective-permute-start.28) | collective-permute-done | bytes 65568 | tf_op jit(solution)/shard_map/ppermute | solution.py:62
  47.4 0.8 collective-permute-done.25
  48.2 1.6 %collective-permute-start.30 = (bf16[128,512]{1,0:T(8,128)(2,1)S(1)}, bf16[128,512]{1,0:T(8,128)(2,1)S(1)}, u32[]{:S(2)}, u32[]{:S(2)}) collective-permute-start(bf16[128,512]{1,0:T(8,128)(2,1)S(1)} %shard_map.135), channel_id=1, source_target_pairs={{4,0},{12,4},{8,12},{0,8},{5,1},{13,5},{9,13},{1,9},{6,2},{14,6},{... | collective-permute-start | bytes 393224 | tf_op jit(solution)/shard_map/ppermute | solution.py:351
  50.3 1.5 %collective-permute-start.26 = (f32[128,64]{1,0:T(8,128)S(1)}, f32[128,64]{1,0:T(8,128)S(1)}, u32[]{:S(2)}, u32[]{:S(2)}) collective-permute-start(f32[128,64]{1,0:T(8,128)S(1)} %add.176), channel_id=1, source_target_pairs={{0,2},{1,3},{2,0},{3,1},{4,6},{5,7},{6,4},{7,5},{8,10},{9,11},{10,... | collective-permute-start | bytes 98312 | tf_op jit(solution)/shard_map/ppermute | solution.py:62
  51.8 2.3 %collective-permute-start.33 = (bf16[64,2048]{1,0:T(8,128)(2,1)S(1)}, bf16[64,2048]{1,0:T(8,128)(2,1)S(1)}, u32[]{:S(2)}, u32[]{:S(2)}) collective-permute-start(bf16[64,2048]{1,0:T(8,128)(2,1)S(1)} %pad_maximum_fusion.1), channel_id=1, source_target_pairs={{0,4},{4,12},{12,8},{8,0},{1,5},{5,13},{13,9},{9,1},{2,6},{6,14},{... | collective-permute-start | bytes 786440 | tf_op jit(solution)/shard_map/ppermute | solution.py:303
  54.1 3.1 %collective-permute-start.32 = (bf16[128,256]{1,0:T(8,128)(2,1)S(1)}, bf16[128,256]{1,0:T(8,128)(2,1)S(1)}, u32[]{:S(2)}, u32[]{:S(2)}) collective-permute-start(bf16[128,256]{1,0:T(8,128)(2,1)S(1)} %get-tuple-element.105.refs_26_), channel_id=1, source_target_pairs={{4,0},{12,4},{8,12},{0,8},{5,1},{13,5},{9,13},{1,9},{6,2},{14,6},{... | collective-permute-start | bytes 196616 | tf_op jit(solution)/shard_map/ppermute | solution.py:358
  57.2 1.2 %collective-permute-done.29 = bf16[128,512]{1,0:T(8,128)(2,1)S(1)} collective-permute-done((bf16[128,512]{1,0:T(8,128)(2,1)S(1)}, bf16[128,512]{1,0:T(8,128)(2,1)S(1)}, u32[]{:S(2)}, u32[]{:S(2)}) %collective-permute-start.29) | collective-permute-done | bytes 131104 | tf_op jit(solution)/shard_map/ppermute | solution.py:350
  58.5 0.6 collective-permute-start.31
  59.1 6.9 %collective-permute-done.32.refs_27_ = bf16[128,256]{1,0:T(8,128)(2,1)S(1)} collective-permute-done((bf16[128,256]{1,0:T(8,128)(2,1)S(1)}, bf16[128,256]{1,0:T(8,128)(2,1)S(1)}, u32[]{:S(2)}, u32[]{:S(2)}) %collective-permute-start.32) | collective-permute-done | bytes 65568 | tf_op jit(solution)/shard_map/ppermute | solution.py:358
  66.0 0.7 collective-permute-done.31.refs_23_
  66.7 2.0 %shard_map.139.refs_16_ = bf16[128,512]{1,0:T(8,128)(2,1)S(1)} custom-call(s32[1]{0:T(128)} %bitcast.1.behind_ref, bf16[16,2048]{1,0:T(8,128)(2,1)S(1)} %get-tuple-element.55.refs_0_, bf16[16,2048]{1,0:T(8,128)(2,1)S(1)} %get-tuple-element.56.refs_1_, bf16[16,2048]{1,0:T(8,128)(2,1)S(1)} %get-tuple-element.57.refs_2_, ...), custom_call_target="tpu_custom_call" | custom-call | tf_op jit(solution)/shard_map/pallas_call | solution.py:104
  68.7 2.0 %shard_map.138.refs_15_ = bf16[128,512]{1,0:T(8,128)(2,1)S(1)} custom-call(s32[1]{0:T(128)} %bitcast.1.behind_ref, bf16[16,2048]{1,0:T(8,128)(2,1)S(1)} %get-tuple-element.55.refs_0_, bf16[16,2048]{1,0:T(8,128)(2,1)S(1)} %get-tuple-element.56.refs_1_, bf16[16,2048]{1,0:T(8,128)(2,1)S(1)} %get-tuple-element.57.refs_2_, ...), custom_call_target="tpu_custom_call" | custom-call | tf_op jit(solution)/shard_map/pallas_call | solution.py:104
  70.7 2.0 %shard_map.137.refs_14_ = bf16[128,512]{1,0:T(8,128)(2,1)S(1)} custom-call(s32[1]{0:T(128)} %bitcast.1.behind_ref, bf16[16,2048]{1,0:T(8,128)(2,1)S(1)} %get-tuple-element.55.refs_0_, bf16[16,2048]{1,0:T(8,128)(2,1)S(1)} %get-tuple-element.56.refs_1_, bf16[16,2048]{1,0:T(8,128)(2,1)S(1)} %get-tuple-element.57.refs_2_, ...), custom_call_target="tpu_custom_call" | custom-call | tf_op jit(solution)/shard_map/pallas_call | solution.py:104
  72.7 2.0 %shard_map.136.refs_13_ = bf16[128,512]{1,0:T(8,128)(2,1)S(1)} custom-call(s32[1]{0:T(128)} %bitcast.1.behind_ref, bf16[16,2048]{1,0:T(8,128)(2,1)S(1)} %get-tuple-element.55.refs_0_, bf16[16,2048]{1,0:T(8,128)(2,1)S(1)} %get-tuple-element.56.refs_1_, bf16[16,2048]{1,0:T(8,128)(2,1)S(1)} %get-tuple-element.57.refs_2_, ...), custom_call_target="tpu_custom_call" | custom-call | tf_op jit(solution)/shard_map/pallas_call | solution.py:104
  75.3 1.2 %collective-permute-done.35 = f32[128,64]{1,0:T(8,128)S(1)} collective-permute-done((f32[128,64]{1,0:T(8,128)S(1)}, f32[128,64]{1,0:T(8,128)S(1)}, u32[]{:S(2)}, u32[]{:S(2)}) %collective-permute-start.35) | collective-permute-done | bytes 32800 | tf_op jit(solution)/shard_map/ppermute | solution.py:62
  76.4 1.6 %collective-permute-start.36 = (f32[128,64]{1,0:T(8,128)S(1)}, f32[128,64]{1,0:T(8,128)S(1)}, u32[]{:S(2)}, u32[]{:S(2)}) collective-permute-start(f32[128,64]{1,0:T(8,128)S(1)} %add.207), channel_id=1, source_target_pairs={{0,2},{1,3},{2,0},{3,1},{4,6},{5,7},{6,4},{7,5},{8,10},{9,11},{10,... | collective-permute-start | bytes 98312 | tf_op jit(solution)/shard_map/ppermute | solution.py:62
  78.0 0.8 pad_maximum_fusion
  78.8 1.9 %collective-permute-done.36 = f32[128,64]{1,0:T(8,128)S(1)} collective-permute-done((f32[128,64]{1,0:T(8,128)S(1)}, f32[128,64]{1,0:T(8,128)S(1)}, u32[]{:S(2)}, u32[]{:S(2)}) %collective-permute-start.36) | collective-permute-done | bytes 32800 | tf_op jit(solution)/shard_map/ppermute | solution.py:62
  80.8 4.0 %collective-permute-done.34.refs_1_ = bf16[64,2048]{1,0:T(8,128)(2,1)S(1)} collective-permute-done((bf16[64,2048]{1,0:T(8,128)(2,1)S(1)}, bf16[64,2048]{1,0:T(8,128)(2,1)S(1)}, u32[]{:S(2)}, u32[]{:S(2)}) %collective-permute-start.34) | collective-permute-done | bytes 262176 | tf_op jit(solution)/shard_map/ppermute | solution.py:303
  85.1 0.8 copy.15
  (98 shorter events, 4.4 us)
Async XLA Ops:
  1.3 0.7 copy-start.4
  1.9 7.8 %copy-start.5 = (s32[4]{0:T(128)S(1)}, s32[4]{0:T(128)}, u32[]{:S(2)}) copy-start(s32[4]{0:T(128)} %version_ref.3) | copy-start | bytes 52
  3.5 8.6 %collective-permute-start.1 = (bf16[16,2048]{1,0:T(8,128)(2,1)S(1)}, bf16[16,2048]{1,0:T(8,128)(2,1)S(1)}, u32[]{:S(2)}, u32[]{:S(2)}) collective-permute-start(bf16[16,2048]{1,0:T(8,128)(2,1)S(1)} %get-tuple-element.50.refs_0_), channel_id=1, source_target_pairs={{0,4},{4,12},{12,8},{8,0},{1,5},{5,13},{13,9},{9,1},{2,6},{6,14},{... | collective-permute-start | bytes 196616 | tf_op jit(solution)/shard_map/ppermute | solution.py:291
  6.6 7.5 %collective-permute-start = (bf16[16,2048]{1,0:T(8,128)(2,1)S(1)}, bf16[16,2048]{1,0:T(8,128)(2,1)S(1)}, u32[]{:S(2)}, u32[]{:S(2)}) collective-permute-start(bf16[16,2048]{1,0:T(8,128)(2,1)S(1)} %get-tuple-element.51.refs_1_), channel_id=1, source_target_pairs={{0,4},{4,12},{12,8},{8,0},{1,5},{5,13},{13,9},{9,1},{2,6},{6,14},{... | collective-permute-start | bytes 196616 | tf_op jit(solution)/shard_map/ppermute | solution.py:291
  9.2 7.5 %collective-permute-start.5 = (bf16[16,2048]{1,0:T(8,128)(2,1)S(1)}, bf16[16,2048]{1,0:T(8,128)(2,1)S(1)}, u32[]{:S(2)}, u32[]{:S(2)}) collective-permute-start(bf16[16,2048]{1,0:T(8,128)(2,1)S(1)} %get-tuple-element.52.refs_2_), channel_id=1, source_target_pairs={{0,4},{4,12},{12,8},{8,0},{1,5},{5,13},{13,9},{9,1},{2,6},{6,14},{... | collective-permute-start | bytes 196616 | tf_op jit(solution)/shard_map/ppermute | solution.py:291
  9.7 7.6 %collective-permute-start.4 = (bf16[16,2048]{1,0:T(8,128)(2,1)S(1)}, bf16[16,2048]{1,0:T(8,128)(2,1)S(1)}, u32[]{:S(2)}, u32[]{:S(2)}) collective-permute-start(bf16[16,2048]{1,0:T(8,128)(2,1)S(1)} %get-tuple-element.53.refs_3_), channel_id=1, source_target_pairs={{0,4},{4,12},{12,8},{8,0},{1,5},{5,13},{13,9},{9,1},{2,6},{6,14},{... | collective-permute-start | bytes 196616 | tf_op jit(solution)/shard_map/ppermute | solution.py:291
  9.7 18.5 %copy-start.6 = (s32[8]{0:T(128)S(1)}, s32[8]{0:T(128)}, u32[]{:S(2)}) copy-start(s32[8]{0:T(128)} %param.16) | copy-start | bytes 100
  12.0 25.0 %copy-start.1 = (bf16[128,2048]{1,0:T(8,128)(2,1)S(1)}, bf16[128,2048]{1,0:T(8,128)(2,1)}, u32[]{:S(2)}) copy-start(bf16[128,2048]{1,0:T(8,128)(2,1)} %refs_24_.1) | copy-start | bytes 1572868
  12.2 5.4 %collective-permute-start.3 = (bf16[16,2048]{1,0:T(8,128)(2,1)S(1)}, bf16[16,2048]{1,0:T(8,128)(2,1)S(1)}, u32[]{:S(2)}, u32[]{:S(2)}) collective-permute-start(bf16[16,2048]{1,0:T(8,128)(2,1)S(1)} %broadcast_select_fusion.20), channel_id=1, source_target_pairs={{0,4},{4,12},{12,8},{8,0},{1,5},{5,13},{13,9},{9,1},{2,6},{6,14},{... | collective-permute-start | bytes 196616 | tf_op jit(solution)/shard_map/ppermute | solution.py:299
  14.1 5.9 %collective-permute-start.2 = (bf16[16,2048]{1,0:T(8,128)(2,1)S(1)}, bf16[16,2048]{1,0:T(8,128)(2,1)S(1)}, u32[]{:S(2)}, u32[]{:S(2)}) collective-permute-start(bf16[16,2048]{1,0:T(8,128)(2,1)S(1)} %broadcast_select_fusion.19), channel_id=1, source_target_pairs={{0,4},{4,12},{12,8},{8,0},{1,5},{5,13},{13,9},{9,1},{2,6},{6,14},{... | collective-permute-start | bytes 196616 | tf_op jit(solution)/shard_map/ppermute | solution.py:299
  16.7 5.9 %collective-permute-start.9 = (bf16[16,2048]{1,0:T(8,128)(2,1)S(1)}, bf16[16,2048]{1,0:T(8,128)(2,1)S(1)}, u32[]{:S(2)}, u32[]{:S(2)}) collective-permute-start(bf16[16,2048]{1,0:T(8,128)(2,1)S(1)} %broadcast_select_fusion.18), channel_id=1, source_target_pairs={{0,4},{4,12},{12,8},{8,0},{1,5},{5,13},{13,9},{9,1},{2,6},{6,14},{... | collective-permute-start | bytes 196616 | tf_op jit(solution)/shard_map/ppermute | solution.py:299
  17.3 6.1 %collective-permute-start.8 = (bf16[16,2048]{1,0:T(8,128)(2,1)S(1)}, bf16[16,2048]{1,0:T(8,128)(2,1)S(1)}, u32[]{:S(2)}, u32[]{:S(2)}) collective-permute-start(bf16[16,2048]{1,0:T(8,128)(2,1)S(1)} %broadcast_select_fusion.17), channel_id=1, source_target_pairs={{0,4},{4,12},{12,8},{8,0},{1,5},{5,13},{13,9},{9,1},{2,6},{6,14},{... | collective-permute-start | bytes 196616 | tf_op jit(solution)/shard_map/ppermute | solution.py:299
  17.6 7.2 %collective-permute-start.7 = (bf16[16,2048]{1,0:T(8,128)(2,1)S(1)}, bf16[16,2048]{1,0:T(8,128)(2,1)S(1)}, u32[]{:S(2)}, u32[]{:S(2)}) collective-permute-start(bf16[16,2048]{1,0:T(8,128)(2,1)S(1)} %broadcast_select_fusion.16), channel_id=1, source_target_pairs={{0,4},{4,12},{12,8},{8,0},{1,5},{5,13},{13,9},{9,1},{2,6},{6,14},{... | collective-permute-start | bytes 196616 | tf_op jit(solution)/shard_map/ppermute | solution.py:299
  20.0 6.1 %collective-permute-start.6 = (bf16[16,2048]{1,0:T(8,128)(2,1)S(1)}, bf16[16,2048]{1,0:T(8,128)(2,1)S(1)}, u32[]{:S(2)}, u32[]{:S(2)}) collective-permute-start(bf16[16,2048]{1,0:T(8,128)(2,1)S(1)} %broadcast_select_fusion.15), channel_id=1, source_target_pairs={{0,4},{4,12},{12,8},{8,0},{1,5},{5,13},{13,9},{9,1},{2,6},{6,14},{... | collective-permute-start | bytes 196616 | tf_op jit(solution)/shard_map/ppermute | solution.py:299
  22.7 5.6 %collective-permute-start.11 = (bf16[16,2048]{1,0:T(8,128)(2,1)S(1)}, bf16[16,2048]{1,0:T(8,128)(2,1)S(1)}, u32[]{:S(2)}, u32[]{:S(2)}) collective-permute-start(bf16[16,2048]{1,0:T(8,128)(2,1)S(1)} %broadcast_select_fusion.14), channel_id=1, source_target_pairs={{0,4},{4,12},{12,8},{8,0},{1,5},{5,13},{13,9},{9,1},{2,6},{6,14},{... | collective-permute-start | bytes 196616 | tf_op jit(solution)/shard_map/ppermute | solution.py:299
  23.4 6.2 %collective-permute-start.13 = (bf16[16,2048]{1,0:T(8,128)(2,1)S(1)}, bf16[16,2048]{1,0:T(8,128)(2,1)S(1)}, u32[]{:S(2)}, u32[]{:S(2)}) collective-permute-start(bf16[16,2048]{1,0:T(8,128)(2,1)S(1)} %broadcast_select_fusion.13), channel_id=1, source_target_pairs={{0,4},{4,12},{12,8},{8,0},{1,5},{5,13},{13,9},{9,1},{2,6},{6,14},{... | collective-permute-start | bytes 196616 | tf_op jit(solution)/shard_map/ppermute | solution.py:299
  24.8 6.7 %collective-permute-start.15 = (bf16[16,2048]{1,0:T(8,128)(2,1)S(1)}, bf16[16,2048]{1,0:T(8,128)(2,1)S(1)}, u32[]{:S(2)}, u32[]{:S(2)}) collective-permute-start(bf16[16,2048]{1,0:T(8,128)(2,1)S(1)} %broadcast_select_fusion.12), channel_id=1, source_target_pairs={{0,4},{4,12},{12,8},{8,0},{1,5},{5,13},{13,9},{9,1},{2,6},{6,14},{... | collective-permute-start | bytes 196616 | tf_op jit(solution)/shard_map/ppermute | solution.py:299
  26.2 6.6 %collective-permute-start.10 = (bf16[16,2048]{1,0:T(8,128)(2,1)S(1)}, bf16[16,2048]{1,0:T(8,128)(2,1)S(1)}, u32[]{:S(2)}, u32[]{:S(2)}) collective-permute-start(bf16[16,2048]{1,0:T(8,128)(2,1)S(1)} %broadcast_select_fusion.11), channel_id=1, source_target_pairs={{0,4},{4,12},{12,8},{8,0},{1,5},{5,13},{13,9},{9,1},{2,6},{6,14},{... | collective-permute-start | bytes 196616 | tf_op jit(solution)/shard_map/ppermute | solution.py:299
  28.4 5.8 %collective-permute-start.12 = (bf16[16,2048]{1,0:T(8,128)(2,1)S(1)}, bf16[16,2048]{1,0:T(8,128)(2,1)S(1)}, u32[]{:S(2)}, u32[]{:S(2)}) collective-permute-start(bf16[16,2048]{1,0:T(8,128)(2,1)S(1)} %broadcast_select_fusion.10), channel_id=1, source_target_pairs={{0,4},{4,12},{12,8},{8,0},{1,5},{5,13},{13,9},{9,1},{2,6},{6,14},{... | collective-permute-start | bytes 196616 | tf_op jit(solution)/shard_map/ppermute | solution.py:299
  29.6 6.0 %collective-permute-start.14 = (bf16[16,2048]{1,0:T(8,128)(2,1)S(1)}, bf16[16,2048]{1,0:T(8,128)(2,1)S(1)}, u32[]{:S(2)}, u32[]{:S(2)}) collective-permute-start(bf16[16,2048]{1,0:T(8,128)(2,1)S(1)} %broadcast_select_fusion.9), channel_id=1, source_target_pairs={{0,4},{4,12},{12,8},{8,0},{1,5},{5,13},{13,9},{9,1},{2,6},{6,14},{... | collective-permute-start | bytes 196616 | tf_op jit(solution)/shard_map/ppermute | solution.py:299
  31.5 15.6 %copy-start.2 = (bf16[128,256]{1,0:T(8,128)(2,1)S(1)}, bf16[128,256]{1,0:T(8,128)(2,1)}, u32[]{:S(2)}) copy-start(bf16[128,256]{1,0:T(8,128)(2,1)} %refs_5_.1) | copy-start | bytes 196612
  31.5 15.6 %copy-start.3 = (bf16[128,256]{1,0:T(8,128)(2,1)S(1)}, bf16[128,256]{1,0:T(8,128)(2,1)}, u32[]{:S(2)}) copy-start(bf16[128,256]{1,0:T(8,128)(2,1)} %refs_6_.1) | copy-start | bytes 196612
  31.5 5.9 %collective-permute-start.16 = (bf16[16,2048]{1,0:T(8,128)(2,1)S(1)}, bf16[16,2048]{1,0:T(8,128)(2,1)S(1)}, u32[]{:S(2)}, u32[]{:S(2)}) collective-permute-start(bf16[16,2048]{1,0:T(8,128)(2,1)S(1)} %broadcast_select_fusion.8), channel_id=1, source_target_pairs={{0,4},{4,12},{12,8},{8,0},{1,5},{5,13},{13,9},{9,1},{2,6},{6,14},{... | collective-permute-start | bytes 196616 | tf_op jit(solution)/shard_map/ppermute | solution.py:299
  32.8 6.0 %collective-permute-start.17 = (bf16[16,2048]{1,0:T(8,128)(2,1)S(1)}, bf16[16,2048]{1,0:T(8,128)(2,1)S(1)}, u32[]{:S(2)}, u32[]{:S(2)}) collective-permute-start(bf16[16,2048]{1,0:T(8,128)(2,1)S(1)} %broadcast_select_fusion.7), channel_id=1, source_target_pairs={{0,4},{4,12},{12,8},{8,0},{1,5},{5,13},{13,9},{9,1},{2,6},{6,14},{... | collective-permute-start | bytes 196616 | tf_op jit(solution)/shard_map/ppermute | solution.py:299
  34.2 5.7 %collective-permute-start.18 = (bf16[16,2048]{1,0:T(8,128)(2,1)S(1)}, bf16[16,2048]{1,0:T(8,128)(2,1)S(1)}, u32[]{:S(2)}, u32[]{:S(2)}) collective-permute-start(bf16[16,2048]{1,0:T(8,128)(2,1)S(1)} %broadcast_select_fusion.6), channel_id=1, source_target_pairs={{0,4},{4,12},{12,8},{8,0},{1,5},{5,13},{13,9},{9,1},{2,6},{6,14},{... | collective-permute-start | bytes 196616 | tf_op jit(solution)/shard_map/ppermute | solution.py:299
  35.6 5.7 %collective-permute-start.19 = (bf16[16,2048]{1,0:T(8,128)(2,1)S(1)}, bf16[16,2048]{1,0:T(8,128)(2,1)S(1)}, u32[]{:S(2)}, u32[]{:S(2)}) collective-permute-start(bf16[16,2048]{1,0:T(8,128)(2,1)S(1)} %broadcast_select_fusion.5), channel_id=1, source_target_pairs={{0,4},{4,12},{12,8},{8,0},{1,5},{5,13},{13,9},{9,1},{2,6},{6,14},{... | collective-permute-start | bytes 196616 | tf_op jit(solution)/shard_map/ppermute | solution.py:299
  37.3 29.4 %copy-start = (bf16[128,2048]{1,0:T(8,128)(2,1)S(1)}, bf16[128,2048]{1,0:T(8,128)(2,1)}, u32[]{:S(2)}) copy-start(bf16[128,2048]{1,0:T(8,128)(2,1)} %refs_17_.7) | copy-start | bytes 1572868
  37.3 5.3 %collective-permute-start.27 = (f32[128,128]{1,0:T(8,128)S(1)}, f32[128,128]{1,0:T(8,128)S(1)}, u32[]{:S(2)}, u32[]{:S(2)}) collective-permute-start(f32[128,128]{1,0:T(8,128)S(1)} %shard_map.134), channel_id=1, source_target_pairs={{0,1},{1,0},{2,3},{3,2},{4,5},{5,4},{6,7},{7,6},{8,9},{9,8},{10,11... | collective-permute-start | bytes 196616 | tf_op jit(solution)/shard_map/ppermute | solution.py:62
  37.4 6.8 %collective-permute-start.20 = (bf16[16,2048]{1,0:T(8,128)(2,1)S(1)}, bf16[16,2048]{1,0:T(8,128)(2,1)S(1)}, u32[]{:S(2)}, u32[]{:S(2)}) collective-permute-start(bf16[16,2048]{1,0:T(8,128)(2,1)S(1)} %broadcast_select_fusion.4), channel_id=1, source_target_pairs={{0,4},{4,12},{12,8},{8,0},{1,5},{5,13},{13,9},{9,1},{2,6},{6,14},{... | collective-permute-start | bytes 196616 | tf_op jit(solution)/shard_map/ppermute | solution.py:299
  38.8 13.0 %collective-permute-start.21 = (bf16[16,2048]{1,0:T(8,128)(2,1)S(1)}, bf16[16,2048]{1,0:T(8,128)(2,1)S(1)}, u32[]{:S(2)}, u32[]{:S(2)}) collective-permute-start(bf16[16,2048]{1,0:T(8,128)(2,1)S(1)} %broadcast_select_fusion.3), channel_id=1, source_target_pairs={{0,4},{4,12},{12,8},{8,0},{1,5},{5,13},{13,9},{9,1},{2,6},{6,14},{... | collective-permute-start | bytes 196616 | tf_op jit(solution)/shard_map/ppermute | solution.py:299
  39.8 10.5 %collective-permute-start.22 = (bf16[16,2048]{1,0:T(8,128)(2,1)S(1)}, bf16[16,2048]{1,0:T(8,128)(2,1)S(1)}, u32[]{:S(2)}, u32[]{:S(2)}) collective-permute-start(bf16[16,2048]{1,0:T(8,128)(2,1)S(1)} %broadcast_select_fusion.2), channel_id=1, source_target_pairs={{0,4},{4,12},{12,8},{8,0},{1,5},{5,13},{13,9},{9,1},{2,6},{6,14},{... | collective-permute-start | bytes 196616 | tf_op jit(solution)/shard_map/ppermute | solution.py:299
  41.3 8.6 %collective-permute-start.23 = (bf16[16,2048]{1,0:T(8,128)(2,1)S(1)}, bf16[16,2048]{1,0:T(8,128)(2,1)S(1)}, u32[]{:S(2)}, u32[]{:S(2)}) collective-permute-start(bf16[16,2048]{1,0:T(8,128)(2,1)S(1)} %broadcast_select_fusion.1), channel_id=1, source_target_pairs={{0,4},{4,12},{12,8},{8,0},{1,5},{5,13},{13,9},{9,1},{2,6},{6,14},{... | collective-permute-start | bytes 196616 | tf_op jit(solution)/shard_map/ppermute | solution.py:299
  42.6 4.3 %collective-permute-start.28 = (f32[128,128]{1,0:T(8,128)S(1)}, f32[128,128]{1,0:T(8,128)S(1)}, u32[]{:S(2)}, u32[]{:S(2)}) collective-permute-start(f32[128,128]{1,0:T(8,128)S(1)} %add.205), channel_id=1, source_target_pairs={{0,2},{1,3},{2,0},{3,1},{4,6},{5,7},{6,4},{7,5},{8,10},{9,11},{10,... | collective-permute-start | bytes 196616 | tf_op jit(solution)/shard_map/ppermute | solution.py:62
  44.2 7.6 %collective-permute-start.24 = (bf16[16,2048]{1,0:T(8,128)(2,1)S(1)}, bf16[16,2048]{1,0:T(8,128)(2,1)S(1)}, u32[]{:S(2)}, u32[]{:S(2)}) collective-permute-start(bf16[16,2048]{1,0:T(8,128)(2,1)S(1)} %broadcast_select_fusion), channel_id=1, source_target_pairs={{0,4},{4,12},{12,8},{8,0},{1,5},{5,13},{13,9},{9,1},{2,6},{6,14},{... | collective-permute-start | bytes 196616 | tf_op jit(solution)/shard_map/ppermute | solution.py:299
  47.0 1.3 %collective-permute-start.25 = (f32[128,64]{1,0:T(8,128)S(1)}, f32[128,64]{1,0:T(8,128)S(1)}, u32[]{:S(2)}, u32[]{:S(2)}) collective-permute-start(f32[128,64]{1,0:T(8,128)S(1)} %shard_map.133), channel_id=1, source_target_pairs={{0,1},{1,0},{2,3},{3,2},{4,5},{5,4},{6,7},{7,6},{8,9},{9,8},{10,11... | collective-permute-start | bytes 98312 | tf_op jit(solution)/shard_map/ppermute | solution.py:62
  48.2 5.9 %collective-permute-start.30 = (bf16[128,512]{1,0:T(8,128)(2,1)S(1)}, bf16[128,512]{1,0:T(8,128)(2,1)S(1)}, u32[]{:S(2)}, u32[]{:S(2)}) collective-permute-start(bf16[128,512]{1,0:T(8,128)(2,1)S(1)} %shard_map.135), channel_id=1, source_target_pairs={{4,0},{12,4},{8,12},{0,8},{5,1},{13,5},{9,13},{1,9},{6,2},{14,6},{... | collective-permute-start | bytes 393224 | tf_op jit(solution)/shard_map/ppermute | solution.py:351
  49.9 8.6 %collective-permute-start.29 = (bf16[128,512]{1,0:T(8,128)(2,1)S(1)}, bf16[128,512]{1,0:T(8,128)(2,1)S(1)}, u32[]{:S(2)}, u32[]{:S(2)}) collective-permute-start(bf16[128,512]{1,0:T(8,128)(2,1)S(1)} %shard_map.135), channel_id=1, source_target_pairs={{0,4},{4,12},{12,8},{8,0},{1,5},{5,13},{13,9},{9,1},{2,6},{6,14},{... | collective-permute-start | bytes 393224 | tf_op jit(solution)/shard_map/ppermute | solution.py:350
  50.3 8.8 %collective-permute-start.26 = (f32[128,64]{1,0:T(8,128)S(1)}, f32[128,64]{1,0:T(8,128)S(1)}, u32[]{:S(2)}, u32[]{:S(2)}) collective-permute-start(f32[128,64]{1,0:T(8,128)S(1)} %add.176), channel_id=1, source_target_pairs={{0,2},{1,3},{2,0},{3,1},{4,6},{5,7},{6,4},{7,5},{8,10},{9,11},{10,... | collective-permute-start | bytes 98312 | tf_op jit(solution)/shard_map/ppermute | solution.py:62
  51.8 22.9 %collective-permute-start.33 = (bf16[64,2048]{1,0:T(8,128)(2,1)S(1)}, bf16[64,2048]{1,0:T(8,128)(2,1)S(1)}, u32[]{:S(2)}, u32[]{:S(2)}) collective-permute-start(bf16[64,2048]{1,0:T(8,128)(2,1)S(1)} %pad_maximum_fusion.1), channel_id=1, source_target_pairs={{0,4},{4,12},{12,8},{8,0},{1,5},{5,13},{13,9},{9,1},{2,6},{6,14},{... | collective-permute-start | bytes 786440 | tf_op jit(solution)/shard_map/ppermute | solution.py:303
  54.1 11.9 %collective-permute-start.32 = (bf16[128,256]{1,0:T(8,128)(2,1)S(1)}, bf16[128,256]{1,0:T(8,128)(2,1)S(1)}, u32[]{:S(2)}, u32[]{:S(2)}) collective-permute-start(bf16[128,256]{1,0:T(8,128)(2,1)S(1)} %get-tuple-element.105.refs_26_), channel_id=1, source_target_pairs={{4,0},{12,4},{8,12},{0,8},{5,1},{13,5},{9,13},{1,9},{6,2},{14,6},{... | collective-permute-start | bytes 196616 | tf_op jit(solution)/shard_map/ppermute | solution.py:358
  58.5 8.3 %collective-permute-start.31 = (bf16[128,256]{1,0:T(8,128)(2,1)S(1)}, bf16[128,256]{1,0:T(8,128)(2,1)S(1)}, u32[]{:S(2)}, u32[]{:S(2)}) collective-permute-start(bf16[128,256]{1,0:T(8,128)(2,1)S(1)} %get-tuple-element.110.refs_20_), channel_id=1, source_target_pairs={{0,4},{4,12},{12,8},{8,0},{1,5},{5,13},{13,9},{9,1},{2,6},{6,14},{... | collective-permute-start | bytes 196616 | tf_op jit(solution)/shard_map/ppermute | solution.py:356
  75.1 1.3 %collective-permute-start.35 = (f32[128,64]{1,0:T(8,128)S(1)}, f32[128,64]{1,0:T(8,128)S(1)}, u32[]{:S(2)}, u32[]{:S(2)}) collective-permute-start(f32[128,64]{1,0:T(8,128)S(1)} %shard_map.140), channel_id=1, source_target_pairs={{0,1},{1,0},{2,3},{3,2},{4,5},{5,4},{6,7},{7,6},{8,9},{9,8},{10,11... | collective-permute-start | bytes 98312 | tf_op jit(solution)/shard_map/ppermute | solution.py:62
  75.2 9.6 %collective-permute-start.34 = (bf16[64,2048]{1,0:T(8,128)(2,1)S(1)}, bf16[64,2048]{1,0:T(8,128)(2,1)S(1)}, u32[]{:S(2)}, u32[]{:S(2)}) collective-permute-start(bf16[64,2048]{1,0:T(8,128)(2,1)S(1)} %collective-permute-done.33.refs_0_), channel_id=1, source_target_pairs={{0,4},{4,12},{12,8},{8,0},{1,5},{5,13},{13,9},{9,1},{2,6},{6,14},{... | collective-permute-start | bytes 786440 | tf_op jit(solution)/shard_map/ppermute | solution.py:303
  76.4 4.3 %collective-permute-start.36 = (f32[128,64]{1,0:T(8,128)S(1)}, f32[128,64]{1,0:T(8,128)S(1)}, u32[]{:S(2)}, u32[]{:S(2)}) collective-permute-start(f32[128,64]{1,0:T(8,128)S(1)} %add.207), channel_id=1, source_target_pairs={{0,2},{1,3},{2,0},{3,1},{4,6},{5,7},{6,4},{7,5},{8,10},{9,11},{10,... | collective-permute-start | bytes 98312 | tf_op jit(solution)/shard_map/ppermute | solution.py:62

commit v2 on v1

--- a/solution.py
+++ b/solution.py
@@ -15,7 +15,8 @@
 EXPONENT_SCALE = HEAD_SIZE ** (-0.5) * math.log2(math.e)
 CHUNK_ROWS = 16
 LAG = 4
-PIECES = 4
+PIECES = 1
+JOINED = 2
 KERNEL_VMEM = 8 << 20
 
 
@@ -80,6 +81,7 @@
 
 
 CONTRACT_LAST = (((1,), (1,)), ((), ()))
+CONTRACT_FIRST = (((0,), (0,)), ((), ()))
 VMEM = pl.BlockSpec(memory_space=pltpu.VMEM)
 SMEM = pl.BlockSpec(memory_space=pltpu.SMEM)
 
@@ -220,6 +222,10 @@
     value_refs = refs[block_count : 2 * block_count]
     out_ref = refs[-1]
     low = low_ref[...].astype(jnp.bfloat16)
+    first = first_head * HEAD_SIZE
+    queries = base_ref[:, first : first + out_ref.shape[1]].astype(jnp.float32) + jnp.dot(
+        low, weight_ref[:, first : first + out_ref.shape[1]], preferred_element_type=jnp.float32
+    )
     group = None
     for lane in range(0, out_ref.shape[1], HEAD_SIZE):
         head = first_head + lane // HEAD_SIZE
@@ -228,19 +234,17 @@
             lanes = slice(group * HEAD_SIZE, (group + 1) * HEAD_SIZE)
             keys = jnp.concatenate([ref[:, lanes] for ref in key_refs], axis=0)
             values = jnp.concatenate([ref[:, lanes] for ref in value_refs], axis=0)
-        at = slice(head * HEAD_SIZE, (head + 1) * HEAD_SIZE)
-        queries = base_ref[:, at].astype(jnp.float32) + jnp.dot(
-            low, weight_ref[:, at], preferred_element_type=jnp.float32
-        )
-        queries = rotate(queries, tables_ref[...]).astype(jnp.bfloat16)
+        turned = rotate(queries[:, lane : lane + HEAD_SIZE], tables_ref[...]).astype(jnp.bfloat16)
         scores = lax.dot_general(
-            queries, keys, CONTRACT_LAST, preferred_element_type=jnp.float32
+            keys, turned, CONTRACT_LAST, preferred_element_type=jnp.float32
         )
         scores = scores + hidden_ref[...]
-        raw = jnp.exp2((scores - jnp.max(scores, axis=1, keepdims=True)) * EXPONENT_SCALE)
-        totals = jnp.sum(raw, axis=1, keepdims=True)
-        mixed = jnp.dot(raw.astype(jnp.bfloat16), values, preferred_element_type=jnp.float32)
-        out_ref[:, lane : lane + HEAD_SIZE] = (mixed / totals).astype(jnp.bfloat16)
+        raw = jnp.exp2((scores - jnp.max(scores, axis=0, keepdims=True)) * EXPONENT_SCALE)
+        totals = jnp.sum(raw, axis=0, keepdims=True)
+        mixed = lax.dot_general(
+            values, raw.astype(jnp.bfloat16), CONTRACT_FIRST, preferred_element_type=jnp.float32
+        )
+        out_ref[:, lane : lane + HEAD_SIZE] = (mixed / totals).T.astype(jnp.bfloat16)
 
 
 def token_positions(stored_block_order, first_row, row_count, half_rows):
@@ -298,8 +302,12 @@
         sent.append(moving)
         arrived.append(lax.ppermute(moving, "ctx", pairs))
     late = []
-    for _ in range(count - 2):
-        moving = late[-1] if late else jnp.concatenate(arrived[-LAG:], axis=0)
+    for turn in range(LAG * (count - 2) // JOINED):
+        if turn < LAG // JOINED:
+            first = len(own) - LAG + turn * JOINED
+            moving = jnp.concatenate(arrived[first : first + JOINED], axis=0)
+        else:
+            moving = late[turn - LAG // JOINED]
         late.append(lax.ppermute(moving, "ctx", pairs))
     stored_block_order = after(stored_block_order, sent[3 * LAG])
 
@@ -316,7 +324,7 @@
                 elif turn < len(own):
                     key, row, array = ("ring", turn), 0, arrived[turn]
                 else:
-                    group, row = divmod(turn - len(own), LAG)
+                    group, row = divmod(turn - len(own), JOINED)
                     key, row, array = ("late", group), row * CHUNK_ROWS, late[group]
                 chunks[key] = array
                 held.append((key, row))
@@ -369,7 +377,7 @@
             for o in offsets
         ]
     )
-    hide = jnp.where(key_pos[None, :] <= query_pos[:, None], 0.0, NEG_BIG)
+    hide = jnp.where(key_pos[:, None] <= query_pos[None, :], 0.0, NEG_BIG)
     local_heads = base_query_rows.shape[1] // HEAD_SIZE
     group_size = local_heads // (pair_width // HEAD_SIZE)
     piece_heads = local_heads // PIECES

time: 86.2 us -> 76.6 us (0.89)
  waiting for transfers between devices: 19.3 us -> 13.3 us
  Pallas kernels: 13.3 us -> 7.92 us
  starting transfers between devices: 48.1 us -> 49.9 us
    ppermute x1, waiting for transfers between devices: 6.87 us -> 0.01 us  [shards(): far = lax.ppermute(back[:, pair_width:], 'ctx', backward)]
    pallas_call x9 -> x6, Pallas kernels: 9.56 us -> 4.17 us  [chunk_call(): pl.pallas_call(body, out_shape=pltpu.VMEM(out_shape.shape, out_shape.dtyp...]
    ppermute x1, starting transfers between devices: 3.05 us -> 0.65 us  [shards(): far = lax.ppermute(back[:, pair_width:], 'ctx', backward)]
    ppermute x1, starting transfers between devices: 0.65 us -> 2.38 us  [shards(): far = lax.ppermute(ahead[:, :pair_width], 'ctx', forward)]
    ppermute x2 -> x4, starting transfers between devices: 2.33 us -> 3.71 us  [shards(): late.append(lax.ppermute(moving, 'ctx', pairs))]
    ppermute x1, waiting for transfers between devices: 0.7 us -> 2.06 us  [shards(): far = lax.ppermute(ahead[:, :pair_width], 'ctx', forward)]
    ppermute x1, waiting for transfers between devices: 1.25 us -> 0.01 us  [shards(): ahead = lax.ppermute(ahead, 'ctx', forward)]
    ppermute x2 -> x4, waiting for transfers between devices: 4.01 us -> 3 us  [shards(): late.append(lax.ppermute(moving, 'ctx', pairs))]
  transfers between devices with their start and end apart: 37 -> 39, of which waited for: 12 -> 8; matrix products, arithmetic and copies ran while one was open for 2% -> 2% of each run, Pallas kernels for 13% -> 8%
where the time goes in v2:
time: 76.6 us; the launch traced here: 76.3 us
  starting transfers between devices  49.9 us (65%)
  waiting for transfers between devices  13.3 us (17%)
  Pallas kernels  7.92 us (10%)
  local copies, waits for them, and re-layouts  2.29 us (3%)
  between operations  1.86 us (2%)
  other arithmetic  1.05 us (1%)
    ppermute x21, starting transfers between devices, shards(): arrived.append(lax.ppermute(moving, 'ctx', pairs))  29.1 us
    ppermute x4, starting transfers between devices, shards(): arrived.append(lax.ppermute(own[turn], 'ctx', pairs))  6.21 us
    ppermute x6, waiting for transfers between devices, doubling_sums(): other = lax.ppermute(sent, axis, pairs)  5.86 us
    ppermute x6, starting transfers between devices, doubling_sums(): other = lax.ppermute(sent, axis, pairs)  4.81 us
    pallas_call x6, Pallas kernels, chunk_call(): pl.pallas_call(body, out_shape=pltpu.VMEM(out_shape.shape, out_shape.dtyp...  4.17 us
    pallas_call x2, Pallas kernels, own_chunks(): pl.pallas_call(body, out_shape=[pltpu.VMEM((CHUNK_ROWS, width), jnp.bfloa...  3.75 us
    ppermute x4, starting transfers between devices, shards(): late.append(lax.ppermute(moving, 'ctx', pairs))  3.71 us
    ppermute x4, waiting for transfers between devices, shards(): late.append(lax.ppermute(moving, 'ctx', pairs))  3 us
  transfers between devices with their start and end apart: 39, of which 8 were waited for; matrix products, arithmetic and copies ran while one was open for 2% of the time, Pallas kernels for 8%

profile of v2, /device:TPU:0, one launch (start us, length us, event | category | flops | bytes accessed | tf_op | source)
XLA Modules:
  0.0 76.3 jit_solution(7304941402176127822)
XLA Ops:
  1.3 0.6 copy-done.4
  1.9 1.6 %shard_map.131 = (bf16[16,2048]{1,0:T(8,128)(2,1)S(1)}, bf16[16,2048]{1,0:T(8,128)(2,1)S(1)}, bf16[16,2048]{1,0:T(8,128)(2,1)S(1)}, bf16[16,2048]{1,0:T(8,128)(2,1)S(1)}) custom-call(s32[1]{0:T(128)S(6)} %copy.17.publisher_ref, s32[4]{0:T(128)S(1)} %copy-done.4, bf16[1,4,192,2048]{3,2,1,0:T(8,128)(2,1)} %refs_0_.3, bf16[1,4,64,2048]{3,2,1,0:T(8,128)(2,1)} %refs_1_.3, ...), custom_call_target="tpu_custom_call" | custom-call | tf_op jit(solution)/shard_map/pallas_call | solution.py:157
  3.5 3.1 %collective-permute-start = (bf16[16,2048]{1,0:T(8,128)(2,1)S(1)}, bf16[16,2048]{1,0:T(8,128)(2,1)S(1)}, u32[]{:S(2)}, u32[]{:S(2)}) collective-permute-start(bf16[16,2048]{1,0:T(8,128)(2,1)S(1)} %get-tuple-element.51.refs_1_), channel_id=1, source_target_pairs={{0,4},{4,12},{12,8},{8,0},{1,5},{5,13},{13,9},{9,1},{2,6},{6,14},{... | collective-permute-start | bytes 196616 | tf_op jit(solution)/shard_map/ppermute | solution.py:295
  6.6 2.6 %collective-permute-start.1 = (bf16[16,2048]{1,0:T(8,128)(2,1)S(1)}, bf16[16,2048]{1,0:T(8,128)(2,1)S(1)}, u32[]{:S(2)}, u32[]{:S(2)}) collective-permute-start(bf16[16,2048]{1,0:T(8,128)(2,1)S(1)} %get-tuple-element.50.refs_0_), channel_id=1, source_target_pairs={{0,4},{4,12},{12,8},{8,0},{1,5},{5,13},{13,9},{9,1},{2,6},{6,14},{... | collective-permute-start | bytes 196616 | tf_op jit(solution)/shard_map/ppermute | solution.py:295
  9.2 0.4 collective-permute-start.4
  9.7 2.2 %shard_map.132 = (bf16[16,2048]{1,0:T(8,128)(2,1)S(1)}, bf16[16,2048]{1,0:T(8,128)(2,1)S(1)}, bf16[16,2048]{1,0:T(8,128)(2,1)S(1)}, bf16[16,2048]{1,0:T(8,128)(2...) custom-call(s32[1]{0:T(128)S(6)} %copy.17.publisher_ref, ...), custom_call_target="tpu_custom_call" | custom-call | tf_op jit(solution)/shard_map/pallas_call | solution.py:157
  12.2 2.0 %collective-permute-start.3 = (bf16[16,2048]{1,0:T(8,128)(2,1)S(1)}, bf16[16,2048]{1,0:T(8,128)(2,1)S(1)}, u32[]{:S(2)}, u32[]{:S(2)}) collective-permute-start(bf16[16,2048]{1,0:T(8,128)(2,1)S(1)} %broadcast_select_fusion.20), channel_id=1, source_target_pairs={{0,4},{4,12},{12,8},{8,0},{1,5},{5,13},{13,9},{9,1},{2,6},{6,14},{... | collective-permute-start | bytes 196616 | tf_op jit(solution)/shard_map/ppermute | solution.py:303
  14.3 2.5 %collective-permute-start.2 = (bf16[16,2048]{1,0:T(8,128)(2,1)S(1)}, bf16[16,2048]{1,0:T(8,128)(2,1)S(1)}, u32[]{:S(2)}, u32[]{:S(2)}) collective-permute-start(bf16[16,2048]{1,0:T(8,128)(2,1)S(1)} %broadcast_select_fusion.19), channel_id=1, source_target_pairs={{0,4},{4,12},{12,8},{8,0},{1,5},{5,13},{13,9},{9,1},{2,6},{6,14},{... | collective-permute-start | bytes 196616 | tf_op jit(solution)/shard_map/ppermute | solution.py:303
  16.8 0.5 collective-permute-start.9
  17.3 1.0 %collective-permute-start.8 = (bf16[16,2048]{1,0:T(8,128)(2,1)S(1)}, bf16[16,2048]{1,0:T(8,128)(2,1)S(1)}, u32[]{:S(2)}, u32[]{:S(2)}) collective-permute-start(bf16[16,2048]{1,0:T(8,128)(2,1)S(1)} %broadcast_select_fusion.17), channel_id=1, source_target_pairs={{0,4},{4,12},{12,8},{8,0},{1,5},{5,13},{13,9},{9,1},{2,6},{6,14},{... | collective-permute-start | bytes 196616 | tf_op jit(solution)/shard_map/ppermute | solution.py:303
  18.3 1.2 %collective-permute-start.7 = (bf16[16,2048]{1,0:T(8,128)(2,1)S(1)}, bf16[16,2048]{1,0:T(8,128)(2,1)S(1)}, u32[]{:S(2)}, u32[]{:S(2)}) collective-permute-start(bf16[16,2048]{1,0:T(8,128)(2,1)S(1)} %broadcast_select_fusion.16), channel_id=1, source_target_pairs={{0,4},{4,12},{12,8},{8,0},{1,5},{5,13},{13,9},{9,1},{2,6},{6,14},{... | collective-permute-start | bytes 196616 | tf_op jit(solution)/shard_map/ppermute | solution.py:303
  19.5 0.7 collective-permute-done.2.refs_13_
  20.2 2.5 %collective-permute-start.6 = (bf16[16,2048]{1,0:T(8,128)(2,1)S(1)}, bf16[16,2048]{1,0:T(8,128)(2,1)S(1)}, u32[]{:S(2)}, u32[]{:S(2)}) collective-permute-start(bf16[16,2048]{1,0:T(8,128)(2,1)S(1)} %broadcast_select_fusion.15), channel_id=1, source_target_pairs={{0,4},{4,12},{12,8},{8,0},{1,5},{5,13},{13,9},{9,1},{2,6},{6,14},{... | collective-permute-start | bytes 196616 | tf_op jit(solution)/shard_map/ppermute | solution.py:303
  22.7 1.4 %collective-permute-start.11 = (bf16[16,2048]{1,0:T(8,128)(2,1)S(1)}, bf16[16,2048]{1,0:T(8,128)(2,1)S(1)}, u32[]{:S(2)}, u32[]{:S(2)}) collective-permute-start(bf16[16,2048]{1,0:T(8,128)(2,1)S(1)} %broadcast_select_fusion.14), channel_id=1, source_target_pairs={{0,4},{4,12},{12,8},{8,0},{1,5},{5,13},{13,9},{9,1},{2,6},{6,14},{... | collective-permute-start | bytes 196616 | tf_op jit(solution)/shard_map/ppermute | solution.py:303
  24.1 1.4 %collective-permute-start.13 = (bf16[16,2048]{1,0:T(8,128)(2,1)S(1)}, bf16[16,2048]{1,0:T(8,128)(2,1)S(1)}, u32[]{:S(2)}, u32[]{:S(2)}) collective-permute-start(bf16[16,2048]{1,0:T(8,128)(2,1)S(1)} %broadcast_select_fusion.13), channel_id=1, source_target_pairs={{0,4},{4,12},{12,8},{8,0},{1,5},{5,13},{13,9},{9,1},{2,6},{6,14},{... | collective-permute-start | bytes 196616 | tf_op jit(solution)/shard_map/ppermute | solution.py:303
  25.5 1.4 %collective-permute-start.15 = (bf16[16,2048]{1,0:T(8,128)(2,1)S(1)}, bf16[16,2048]{1,0:T(8,128)(2,1)S(1)}, u32[]{:S(2)}, u32[]{:S(2)}) collective-permute-start(bf16[16,2048]{1,0:T(8,128)(2,1)S(1)} %broadcast_select_fusion.12), channel_id=1, source_target_pairs={{0,4},{4,12},{12,8},{8,0},{1,5},{5,13},{13,9},{9,1},{2,6},{6,14},{... | collective-permute-start | bytes 196616 | tf_op jit(solution)/shard_map/ppermute | solution.py:303
  26.9 1.7 %collective-permute-start.10 = (bf16[16,2048]{1,0:T(8,128)(2,1)S(1)}, bf16[16,2048]{1,0:T(8,128)(2,1)S(1)}, u32[]{:S(2)}, u32[]{:S(2)}) collective-permute-start(bf16[16,2048]{1,0:T(8,128)(2,1)S(1)} %broadcast_select_fusion.11), channel_id=1, source_target_pairs={{0,4},{4,12},{12,8},{8,0},{1,5},{5,13},{13,9},{9,1},{2,6},{6,14},{... | collective-permute-start | bytes 196616 | tf_op jit(solution)/shard_map/ppermute | solution.py:303
  28.6 1.4 %collective-permute-start.12 = (bf16[16,2048]{1,0:T(8,128)(2,1)S(1)}, bf16[16,2048]{1,0:T(8,128)(2,1)S(1)}, u32[]{:S(2)}, u32[]{:S(2)}) collective-permute-start(bf16[16,2048]{1,0:T(8,128)(2,1)S(1)} %broadcast_select_fusion.10), channel_id=1, source_target_pairs={{0,4},{4,12},{12,8},{8,0},{1,5},{5,13},{13,9},{9,1},{2,6},{6,14},{... | collective-permute-start | bytes 196616 | tf_op jit(solution)/shard_map/ppermute | solution.py:303
  30.0 1.4 %collective-permute-start.14 = (bf16[16,2048]{1,0:T(8,128)(2,1)S(1)}, bf16[16,2048]{1,0:T(8,128)(2,1)S(1)}, u32[]{:S(2)}, u32[]{:S(2)}) collective-permute-start(bf16[16,2048]{1,0:T(8,128)(2,1)S(1)} %broadcast_select_fusion.9), channel_id=1, source_target_pairs={{0,4},{4,12},{12,8},{8,0},{1,5},{5,13},{13,9},{9,1},{2,6},{6,14},{... | collective-permute-start | bytes 196616 | tf_op jit(solution)/shard_map/ppermute | solution.py:303
  32.2 1.4 %collective-permute-start.16 = (bf16[16,2048]{1,0:T(8,128)(2,1)S(1)}, bf16[16,2048]{1,0:T(8,128)(2,1)S(1)}, u32[]{:S(2)}, u32[]{:S(2)}) collective-permute-start(bf16[16,2048]{1,0:T(8,128)(2,1)S(1)} %broadcast_select_fusion.8), channel_id=1, source_target_pairs={{0,4},{4,12},{12,8},{8,0},{1,5},{5,13},{13,9},{9,1},{2,6},{6,14},{... | collective-permute-start | bytes 196616 | tf_op jit(solution)/shard_map/ppermute | solution.py:303
  33.6 1.0 %collective-permute-start.17 = (bf16[16,2048]{1,0:T(8,128)(2,1)S(1)}, bf16[16,2048]{1,0:T(8,128)(2,1)S(1)}, u32[]{:S(2)}, u32[]{:S(2)}) collective-permute-start(bf16[16,2048]{1,0:T(8,128)(2,1)S(1)} %broadcast_select_fusion.7), channel_id=1, source_target_pairs={{0,4},{4,12},{12,8},{8,0},{1,5},{5,13},{13,9},{9,1},{2,6},{6,14},{... | collective-permute-start | bytes 196616 | tf_op jit(solution)/shard_map/ppermute | solution.py:303
  34.6 1.4 %collective-permute-start.18 = (bf16[16,2048]{1,0:T(8,128)(2,1)S(1)}, bf16[16,2048]{1,0:T(8,128)(2,1)S(1)}, u32[]{:S(2)}, u32[]{:S(2)}) collective-permute-start(bf16[16,2048]{1,0:T(8,128)(2,1)S(1)} %broadcast_select_fusion.6), channel_id=1, source_target_pairs={{0,4},{4,12},{12,8},{8,0},{1,5},{5,13},{13,9},{9,1},{2,6},{6,14},{... | collective-permute-start | bytes 196616 | tf_op jit(solution)/shard_map/ppermute | solution.py:303
  36.0 1.4 %collective-permute-start.19 = (bf16[16,2048]{1,0:T(8,128)(2,1)S(1)}, bf16[16,2048]{1,0:T(8,128)(2,1)S(1)}, u32[]{:S(2)}, u32[]{:S(2)}) collective-permute-start(bf16[16,2048]{1,0:T(8,128)(2,1)S(1)} %broadcast_select_fusion.5), channel_id=1, source_target_pairs={{0,4},{4,12},{12,8},{8,0},{1,5},{5,13},{13,9},{9,1},{2,6},{6,14},{... | collective-permute-start | bytes 196616 | tf_op jit(solution)/shard_map/ppermute | solution.py:303
  37.4 0.3 shard_map.134
  37.9 1.4 %collective-permute-start.20 = (bf16[16,2048]{1,0:T(8,128)(2,1)S(1)}, bf16[16,2048]{1,0:T(8,128)(2,1)S(1)}, u32[]{:S(2)}, u32[]{:S(2)}) collective-permute-start(bf16[16,2048]{1,0:T(8,128)(2,1)S(1)} %broadcast_select_fusion.4), channel_id=1, source_target_pairs={{0,4},{4,12},{12,8},{8,0},{1,5},{5,13},{13,9},{9,1},{2,6},{6,14},{... | collective-permute-start | bytes 196616 | tf_op jit(solution)/shard_map/ppermute | solution.py:303
  39.3 1.0 %collective-permute-start.21 = (bf16[16,2048]{1,0:T(8,128)(2,1)S(1)}, bf16[16,2048]{1,0:T(8,128)(2,1)S(1)}, u32[]{:S(2)}, u32[]{:S(2)}) collective-permute-start(bf16[16,2048]{1,0:T(8,128)(2,1)S(1)} %broadcast_select_fusion.3), channel_id=1, source_target_pairs={{0,4},{4,12},{12,8},{8,0},{1,5},{5,13},{13,9},{9,1},{2,6},{6,14},{... | collective-permute-start | bytes 196616 | tf_op jit(solution)/shard_map/ppermute | solution.py:303
  40.3 1.4 %collective-permute-start.22 = (bf16[16,2048]{1,0:T(8,128)(2,1)S(1)}, bf16[16,2048]{1,0:T(8,128)(2,1)S(1)}, u32[]{:S(2)}, u32[]{:S(2)}) collective-permute-start(bf16[16,2048]{1,0:T(8,128)(2,1)S(1)} %broadcast_select_fusion.2), channel_id=1, source_target_pairs={{0,4},{4,12},{12,8},{8,0},{1,5},{5,13},{13,9},{9,1},{2,6},{6,14},{... | collective-permute-start | bytes 196616 | tf_op jit(solution)/shard_map/ppermute | solution.py:303
  41.7 1.6 %collective-permute-start.28 = (f32[128,128]{1,0:T(8,128)S(1)}, f32[128,128]{1,0:T(8,128)S(1)}, u32[]{:S(2)}, u32[]{:S(2)}) collective-permute-start(f32[128,128]{1,0:T(8,128)S(1)} %add.208), channel_id=1, source_target_pairs={{0,2},{1,3},{2,0},{3,1},{4,6},{5,7},{6,4},{7,5},{8,10},{9,11},{10,... | collective-permute-start | bytes 196616 | tf_op jit(solution)/shard_map/ppermute | solution.py:63
  43.3 1.4 %collective-permute-start.23 = (bf16[16,2048]{1,0:T(8,128)(2,1)S(1)}, bf16[16,2048]{1,0:T(8,128)(2,1)S(1)}, u32[]{:S(2)}, u32[]{:S(2)}) collective-permute-start(bf16[16,2048]{1,0:T(8,128)(2,1)S(1)} %broadcast_select_fusion.1), channel_id=1, source_target_pairs={{0,4},{4,12},{12,8},{8,0},{1,5},{5,13},{13,9},{9,1},{2,6},{6,14},{... | collective-permute-start | bytes 196616 | tf_op jit(solution)/shard_map/ppermute | solution.py:303
  44.7 1.4 %collective-permute-done.28 = f32[128,128]{1,0:T(8,128)S(1)} collective-permute-done((f32[128,128]{1,0:T(8,128)S(1)}, f32[128,128]{1,0:T(8,128)S(1)}, u32[]{:S(2)}, u32[]{:S(2)}) %collective-permute-start.28) | collective-permute-done | bytes 65568 | tf_op jit(solution)/shard_map/ppermute | solution.py:63
  46.4 1.4 %collective-permute-start.29 = (bf16[128,512]{1,0:T(8,128)(2,1)S(1)}, bf16[128,512]{1,0:T(8,128)(2,1)S(1)}, u32[]{:S(2)}, u32[]{:S(2)}) collective-permute-start(bf16[128,512]{1,0:T(8,128)(2,1)S(1)} %shard_map.135), channel_id=1, source_target_pairs={{0,4},{4,12},{12,8},{8,0},{1,5},{5,13},{13,9},{9,1},{2,6},{6,14},{... | collective-permute-start | bytes 393224 | tf_op jit(solution)/shard_map/ppermute | solution.py:358
  47.8 1.6 %collective-permute-start.30 = (bf16[128,512]{1,0:T(8,128)(2,1)S(1)}, bf16[128,512]{1,0:T(8,128)(2,1)S(1)}, u32[]{:S(2)}, u32[]{:S(2)}) collective-permute-start(bf16[128,512]{1,0:T(8,128)(2,1)S(1)} %shard_map.135), channel_id=1, source_target_pairs={{4,0},{12,4},{8,12},{0,8},{5,1},{13,5},{9,13},{1,9},{6,2},{14,6},{... | collective-permute-start | bytes 393224 | tf_op jit(solution)/shard_map/ppermute | solution.py:359
  49.7 0.5 collective-permute-start.24
  50.2 1.2 %collective-permute-done.25 = f32[128,64]{1,0:T(8,128)S(1)} collective-permute-done((f32[128,64]{1,0:T(8,128)S(1)}, f32[128,64]{1,0:T(8,128)S(1)}, u32[]{:S(2)}, u32[]{:S(2)}) %collective-permute-start.25) | collective-permute-done | bytes 32800 | tf_op jit(solution)/shard_map/ppermute | solution.py:63
  51.5 2.2 %collective-permute-start.33 = (bf16[32,2048]{1,0:T(8,128)(2,1)S(1)}, bf16[32,2048]{1,0:T(8,128)(2,1)S(1)}, u32[]{:S(2)}, u32[]{:S(2)}) collective-permute-start(bf16[32,2048]{1,0:T(8,128)(2,1)S(1)} %pad_maximum_fusion.1), channel_id=1, source_target_pairs={{0,4},{4,12},{12,8},{8,0},{1,5},{5,13},{13,9},{9,1},{2,6},{6,14},{... | collective-permute-start | bytes 393224 | tf_op jit(solution)/shard_map/ppermute | solution.py:311
  53.7 1.6 %collective-permute-start.26 = (f32[128,64]{1,0:T(8,128)S(1)}, f32[128,64]{1,0:T(8,128)S(1)}, u32[]{:S(2)}, u32[]{:S(2)}) collective-permute-start(f32[128,64]{1,0:T(8,128)S(1)} %add.179), channel_id=1, source_target_pairs={{0,2},{1,3},{2,0},{3,1},{4,6},{5,7},{6,4},{7,5},{8,10},{9,11},{10,... | collective-permute-start | bytes 98312 | tf_op jit(solution)/shard_map/ppermute | solution.py:63
  55.3 1.6 %collective-permute-done.24.refs_15_.refs_13_.refs_11_ = bf16[16,2048]{1,0:T(8,128)(2,1)S(1)} collective-permute-done((bf16[16,2048]{1,0:T(8,128)(2,1)S(1)}, bf16[16,2048]{1,0:T(8,128)(2,1)S(1)}, u32[]{:S(2)}, u32[]{:S(2)}) %collective-permute-start.24) | collective-permute-done | bytes 65568 | tf_op jit(solution)/shard_map/ppermute | solution.py:303
  57.0 2.4 %collective-permute-start.31 = (bf16[128,256]{1,0:T(8,128)(2,1)S(1)}, bf16[128,256]{1,0:T(8,128)(2,1)S(1)}, u32[]{:S(2)}, u32[]{:S(2)}) collective-permute-start(bf16[128,256]{1,0:T(8,128)(2,1)S(1)} %get-tuple-element.110.refs_20_), channel_id=1, source_target_pairs={{0,4},{4,12},{12,8},{8,0},{1,5},{5,13},{13,9},{9,1},{2,6},{6,14},{... | collective-permute-start | bytes 196616 | tf_op jit(solution)/shard_map/ppermute | solution.py:364
  59.4 0.7 collective-permute-start.32
  60.0 1.4 %collective-permute-start.35 = (bf16[32,2048]{1,0:T(8,128)(2,1)S(1)}, bf16[32,2048]{1,0:T(8,128)(2,1)S(1)}, u32[]{:S(2)}, u32[]{:S(2)}) collective-permute-start(bf16[32,2048]{1,0:T(8,128)(2,1)S(1)} %collective-permute-done.33.refs_0_), channel_id=1, source_target_pairs={{0,4},{4,12},{12,8},{8,0},{1,5},{5,13},{13,9},{9,1},{2,6},{6,14},{... | collective-permute-start | bytes 393224 | tf_op jit(solution)/shard_map/ppermute | solution.py:311
  61.4 3.0 %collective-permute-done.34.refs_1_ = bf16[32,2048]{1,0:T(8,128)(2,1)S(1)} collective-permute-done((bf16[32,2048]{1,0:T(8,128)(2,1)S(1)}, bf16[32,2048]{1,0:T(8,128)(2,1)S(1)}, u32[]{:S(2)}, u32[]{:S(2)}) %collective-permute-start.34) | collective-permute-done | bytes 131104 | tf_op jit(solution)/shard_map/ppermute | solution.py:311
  64.5 2.1 %collective-permute-done.31.refs_23_ = bf16[128,256]{1,0:T(8,128)(2,1)S(1)} collective-permute-done((bf16[128,256]{1,0:T(8,128)(2,1)S(1)}, bf16[128,256]{1,0:T(8,128)(2,1)S(1)}, u32[]{:S(2)}, u32[]{:S(2)}) %collective-permute-start.31) | collective-permute-done | bytes 65568 | tf_op jit(solution)/shard_map/ppermute | solution.py:364
  66.5 2.6 %shard_map.136.refs_14_ = bf16[128,2048]{1,0:T(8,128)(2,1)S(1)} custom-call(s32[1]{0:T(128)} %bitcast.1.behind_ref, bf16[16,2048]{1,0:T(8,128)(2,1)S(1)} %get-tuple-element.55.refs_0_, bf16[16,2048]{1,0:T(8,128)(2,1)S(1)} %get-tuple-element.56.refs_1_, bf16[16,2048]{1,0:T(8,128)(2,1)S(1)} %get-tuple-element.57.refs_2_, ...), custom_call_target="tpu_custom_call" | custom-call | tf_op jit(solution)/shard_map/pallas_call | solution.py:106
  69.5 1.2 %collective-permute-done.37 = f32[128,64]{1,0:T(8,128)S(1)} collective-permute-done((f32[128,64]{1,0:T(8,128)S(1)}, f32[128,64]{1,0:T(8,128)S(1)}, u32[]{:S(2)}, u32[]{:S(2)}) %collective-permute-start.37) | collective-permute-done | bytes 32800 | tf_op jit(solution)/shard_map/ppermute | solution.py:63
  70.8 1.5 %collective-permute-start.38 = (f32[128,64]{1,0:T(8,128)S(1)}, f32[128,64]{1,0:T(8,128)S(1)}, u32[]{:S(2)}, u32[]{:S(2)}) collective-permute-start(f32[128,64]{1,0:T(8,128)S(1)} %add.210), channel_id=1, source_target_pairs={{0,2},{1,3},{2,0},{3,1},{4,6},{5,7},{6,4},{7,5},{8,10},{9,11},{10,... | collective-permute-start | bytes 98312 | tf_op jit(solution)/shard_map/ppermute | solution.py:63
  72.3 0.8 %copy.15 = bf16[128,2048]{1,0:T(8,128)(2,1)} copy(bf16[128,2048]{1,0:T(8,128)(2,1)S(1)} %shard_map.136.refs_14_) | data formatting | bytes 1048576
  73.1 2.0 %collective-permute-done.38 = f32[128,64]{1,0:T(8,128)S(1)} collective-permute-done((f32[128,64]{1,0:T(8,128)S(1)}, f32[128,64]{1,0:T(8,128)S(1)}, u32[]{:S(2)}, u32[]{:S(2)}) %collective-permute-start.38) | collective-permute-done | bytes 32800 | tf_op jit(solution)/shard_map/ppermute | solution.py:63
  75.5 0.8 %copy.16 = bf16[128,2048]{1,0:T(8,128)(2,1)} copy(bf16[128,2048]{1,0:T(8,128)(2,1)S(1)} %shard_map.138) | data formatting | bytes 1048576
  (100 shorter events, 2.7 us)
Async XLA Ops:
  1.3 0.7 copy-start.4
  1.9 7.8 %copy-start.5 = (s32[4]{0:T(128)S(1)}, s32[4]{0:T(128)}, u32[]{:S(2)}) copy-start(s32[4]{0:T(128)} %version_ref.3) | copy-start | bytes 52
  3.5 10.7 %collective-permute-start = (bf16[16,2048]{1,0:T(8,128)(2,1)S(1)}, bf16[16,2048]{1,0:T(8,128)(2,1)S(1)}, u32[]{:S(2)}, u32[]{:S(2)}) collective-permute-start(bf16[16,2048]{1,0:T(8,128)(2,1)S(1)} %get-tuple-element.51.refs_1_), channel_id=1, source_target_pairs={{0,4},{4,12},{12,8},{8,0},{1,5},{5,13},{13,9},{9,1},{2,6},{6,14},{... | collective-permute-start | bytes 196616 | tf_op jit(solution)/shard_map/ppermute | solution.py:295
  6.6 5.6 %collective-permute-start.1 = (bf16[16,2048]{1,0:T(8,128)(2,1)S(1)}, bf16[16,2048]{1,0:T(8,128)(2,1)S(1)}, u32[]{:S(2)}, u32[]{:S(2)}) collective-permute-start(bf16[16,2048]{1,0:T(8,128)(2,1)S(1)} %get-tuple-element.50.refs_0_), channel_id=1, source_target_pairs={{0,4},{4,12},{12,8},{8,0},{1,5},{5,13},{13,9},{9,1},{2,6},{6,14},{... | collective-permute-start | bytes 196616 | tf_op jit(solution)/shard_map/ppermute | solution.py:295
  9.2 8.1 %collective-permute-start.4 = (bf16[16,2048]{1,0:T(8,128)(2,1)S(1)}, bf16[16,2048]{1,0:T(8,128)(2,1)S(1)}, u32[]{:S(2)}, u32[]{:S(2)}) collective-permute-start(bf16[16,2048]{1,0:T(8,128)(2,1)S(1)} %get-tuple-element.53.refs_3_), channel_id=1, source_target_pairs={{0,4},{4,12},{12,8},{8,0},{1,5},{5,13},{13,9},{9,1},{2,6},{6,14},{... | collective-permute-start | bytes 196616 | tf_op jit(solution)/shard_map/ppermute | solution.py:295
  9.7 7.1 %collective-permute-start.5 = (bf16[16,2048]{1,0:T(8,128)(2,1)S(1)}, bf16[16,2048]{1,0:T(8,128)(2,1)S(1)}, u32[]{:S(2)}, u32[]{:S(2)}) collective-permute-start(bf16[16,2048]{1,0:T(8,128)(2,1)S(1)} %get-tuple-element.52.refs_2_), channel_id=1, source_target_pairs={{0,4},{4,12},{12,8},{8,0},{1,5},{5,13},{13,9},{9,1},{2,6},{6,14},{... | collective-permute-start | bytes 196616 | tf_op jit(solution)/shard_map/ppermute | solution.py:295
  9.7 21.7 %copy-start.6 = (s32[8]{0:T(128)S(1)}, s32[8]{0:T(128)}, u32[]{:S(2)}) copy-start(s32[8]{0:T(128)} %param.16) | copy-start | bytes 100
  11.9 25.5 %copy-start = (bf16[128,2048]{1,0:T(8,128)(2,1)S(1)}, bf16[128,2048]{1,0:T(8,128)(2,1)}, u32[]{:S(2)}) copy-start(bf16[128,2048]{1,0:T(8,128)(2,1)} %refs_24_.1) | copy-start | bytes 1572868
  12.2 6.1 %collective-permute-start.3 = (bf16[16,2048]{1,0:T(8,128)(2,1)S(1)}, bf16[16,2048]{1,0:T(8,128)(2,1)S(1)}, u32[]{:S(2)}, u32[]{:S(2)}) collective-permute-start(bf16[16,2048]{1,0:T(8,128)(2,1)S(1)} %broadcast_select_fusion.20), channel_id=1, source_target_pairs={{0,4},{4,12},{12,8},{8,0},{1,5},{5,13},{13,9},{9,1},{2,6},{6,14},{... | collective-permute-start | bytes 196616 | tf_op jit(solution)/shard_map/ppermute | solution.py:303
  14.3 5.9 %collective-permute-start.2 = (bf16[16,2048]{1,0:T(8,128)(2,1)S(1)}, bf16[16,2048]{1,0:T(8,128)(2,1)S(1)}, u32[]{:S(2)}, u32[]{:S(2)}) collective-permute-start(bf16[16,2048]{1,0:T(8,128)(2,1)S(1)} %broadcast_select_fusion.19), channel_id=1, source_target_pairs={{0,4},{4,12},{12,8},{8,0},{1,5},{5,13},{13,9},{9,1},{2,6},{6,14},{... | collective-permute-start | bytes 196616 | tf_op jit(solution)/shard_map/ppermute | solution.py:303
  16.8 5.9 %collective-permute-start.9 = (bf16[16,2048]{1,0:T(8,128)(2,1)S(1)}, bf16[16,2048]{1,0:T(8,128)(2,1)S(1)}, u32[]{:S(2)}, u32[]{:S(2)}) collective-permute-start(bf16[16,2048]{1,0:T(8,128)(2,1)S(1)} %broadcast_select_fusion.18), channel_id=1, source_target_pairs={{0,4},{4,12},{12,8},{8,0},{1,5},{5,13},{13,9},{9,1},{2,6},{6,14},{... | collective-permute-start | bytes 196616 | tf_op jit(solution)/shard_map/ppermute | solution.py:303
  17.3 6.8 %collective-permute-start.8 = (bf16[16,2048]{1,0:T(8,128)(2,1)S(1)}, bf16[16,2048]{1,0:T(8,128)(2,1)S(1)}, u32[]{:S(2)}, u32[]{:S(2)}) collective-permute-start(bf16[16,2048]{1,0:T(8,128)(2,1)S(1)} %broadcast_select_fusion.17), channel_id=1, source_target_pairs={{0,4},{4,12},{12,8},{8,0},{1,5},{5,13},{13,9},{9,1},{2,6},{6,14},{... | collective-permute-start | bytes 196616 | tf_op jit(solution)/shard_map/ppermute | solution.py:303
  18.3 7.2 %collective-permute-start.7 = (bf16[16,2048]{1,0:T(8,128)(2,1)S(1)}, bf16[16,2048]{1,0:T(8,128)(2,1)S(1)}, u32[]{:S(2)}, u32[]{:S(2)}) collective-permute-start(bf16[16,2048]{1,0:T(8,128)(2,1)S(1)} %broadcast_select_fusion.16), channel_id=1, source_target_pairs={{0,4},{4,12},{12,8},{8,0},{1,5},{5,13},{13,9},{9,1},{2,6},{6,14},{... | collective-permute-start | bytes 196616 | tf_op jit(solution)/shard_map/ppermute | solution.py:303
  20.2 25.9 %copy-start.2 = (bf16[128,256]{1,0:T(8,128)(2,1)S(1)}, bf16[128,256]{1,0:T(8,128)(2,1)}, u32[]{:S(2)}) copy-start(bf16[128,256]{1,0:T(8,128)(2,1)} %refs_5_.1) | copy-start | bytes 196612
  20.2 25.9 %copy-start.3 = (bf16[128,256]{1,0:T(8,128)(2,1)S(1)}, bf16[128,256]{1,0:T(8,128)(2,1)}, u32[]{:S(2)}) copy-start(bf16[128,256]{1,0:T(8,128)(2,1)} %refs_6_.1) | copy-start | bytes 196612
  20.2 6.7 %collective-permute-start.6 = (bf16[16,2048]{1,0:T(8,128)(2,1)S(1)}, bf16[16,2048]{1,0:T(8,128)(2,1)S(1)}, u32[]{:S(2)}, u32[]{:S(2)}) collective-permute-start(bf16[16,2048]{1,0:T(8,128)(2,1)S(1)} %broadcast_select_fusion.15), channel_id=1, source_target_pairs={{0,4},{4,12},{12,8},{8,0},{1,5},{5,13},{13,9},{9,1},{2,6},{6,14},{... | collective-permute-start | bytes 196616 | tf_op jit(solution)/shard_map/ppermute | solution.py:303
  22.7 5.9 %collective-permute-start.11 = (bf16[16,2048]{1,0:T(8,128)(2,1)S(1)}, bf16[16,2048]{1,0:T(8,128)(2,1)S(1)}, u32[]{:S(2)}, u32[]{:S(2)}) collective-permute-start(bf16[16,2048]{1,0:T(8,128)(2,1)S(1)} %broadcast_select_fusion.14), channel_id=1, source_target_pairs={{0,4},{4,12},{12,8},{8,0},{1,5},{5,13},{13,9},{9,1},{2,6},{6,14},{... | collective-permute-start | bytes 196616 | tf_op jit(solution)/shard_map/ppermute | solution.py:303
  24.1 5.9 %collective-permute-start.13 = (bf16[16,2048]{1,0:T(8,128)(2,1)S(1)}, bf16[16,2048]{1,0:T(8,128)(2,1)S(1)}, u32[]{:S(2)}, u32[]{:S(2)}) collective-permute-start(bf16[16,2048]{1,0:T(8,128)(2,1)S(1)} %broadcast_select_fusion.13), channel_id=1, source_target_pairs={{0,4},{4,12},{12,8},{8,0},{1,5},{5,13},{13,9},{9,1},{2,6},{6,14},{... | collective-permute-start | bytes 196616 | tf_op jit(solution)/shard_map/ppermute | solution.py:303
  25.5 6.7 %collective-permute-start.15 = (bf16[16,2048]{1,0:T(8,128)(2,1)S(1)}, bf16[16,2048]{1,0:T(8,128)(2,1)S(1)}, u32[]{:S(2)}, u32[]{:S(2)}) collective-permute-start(bf16[16,2048]{1,0:T(8,128)(2,1)S(1)} %broadcast_select_fusion.12), channel_id=1, source_target_pairs={{0,4},{4,12},{12,8},{8,0},{1,5},{5,13},{13,9},{9,1},{2,6},{6,14},{... | collective-permute-start | bytes 196616 | tf_op jit(solution)/shard_map/ppermute | solution.py:303
  26.9 6.7 %collective-permute-start.10 = (bf16[16,2048]{1,0:T(8,128)(2,1)S(1)}, bf16[16,2048]{1,0:T(8,128)(2,1)S(1)}, u32[]{:S(2)}, u32[]{:S(2)}) collective-permute-start(bf16[16,2048]{1,0:T(8,128)(2,1)S(1)} %broadcast_select_fusion.11), channel_id=1, source_target_pairs={{0,4},{4,12},{12,8},{8,0},{1,5},{5,13},{13,9},{9,1},{2,6},{6,14},{... | collective-permute-start | bytes 196616 | tf_op jit(solution)/shard_map/ppermute | solution.py:303
  28.6 6.0 %collective-permute-start.12 = (bf16[16,2048]{1,0:T(8,128)(2,1)S(1)}, bf16[16,2048]{1,0:T(8,128)(2,1)S(1)}, u32[]{:S(2)}, u32[]{:S(2)}) collective-permute-start(bf16[16,2048]{1,0:T(8,128)(2,1)S(1)} %broadcast_select_fusion.10), channel_id=1, source_target_pairs={{0,4},{4,12},{12,8},{8,0},{1,5},{5,13},{13,9},{9,1},{2,6},{6,14},{... | collective-permute-start | bytes 196616 | tf_op jit(solution)/shard_map/ppermute | solution.py:303
  30.0 6.0 %collective-permute-start.14 = (bf16[16,2048]{1,0:T(8,128)(2,1)S(1)}, bf16[16,2048]{1,0:T(8,128)(2,1)S(1)}, u32[]{:S(2)}, u32[]{:S(2)}) collective-permute-start(bf16[16,2048]{1,0:T(8,128)(2,1)S(1)} %broadcast_select_fusion.9), channel_id=1, source_target_pairs={{0,4},{4,12},{12,8},{8,0},{1,5},{5,13},{13,9},{9,1},{2,6},{6,14},{... | collective-permute-start | bytes 196616 | tf_op jit(solution)/shard_map/ppermute | solution.py:303
  32.2 5.7 %collective-permute-start.16 = (bf16[16,2048]{1,0:T(8,128)(2,1)S(1)}, bf16[16,2048]{1,0:T(8,128)(2,1)S(1)}, u32[]{:S(2)}, u32[]{:S(2)}) collective-permute-start(bf16[16,2048]{1,0:T(8,128)(2,1)S(1)} %broadcast_select_fusion.8), channel_id=1, source_target_pairs={{0,4},{4,12},{12,8},{8,0},{1,5},{5,13},{13,9},{9,1},{2,6},{6,14},{... | collective-permute-start | bytes 196616 | tf_op jit(solution)/shard_map/ppermute | solution.py:303
  33.6 5.7 %collective-permute-start.17 = (bf16[16,2048]{1,0:T(8,128)(2,1)S(1)}, bf16[16,2048]{1,0:T(8,128)(2,1)S(1)}, u32[]{:S(2)}, u32[]{:S(2)}) collective-permute-start(bf16[16,2048]{1,0:T(8,128)(2,1)S(1)} %broadcast_select_fusion.7), channel_id=1, source_target_pairs={{0,4},{4,12},{12,8},{8,0},{1,5},{5,13},{13,9},{9,1},{2,6},{6,14},{... | collective-permute-start | bytes 196616 | tf_op jit(solution)/shard_map/ppermute | solution.py:303
  34.6 5.7 %collective-permute-start.18 = (bf16[16,2048]{1,0:T(8,128)(2,1)S(1)}, bf16[16,2048]{1,0:T(8,128)(2,1)S(1)}, u32[]{:S(2)}, u32[]{:S(2)}) collective-permute-start(bf16[16,2048]{1,0:T(8,128)(2,1)S(1)} %broadcast_select_fusion.6), channel_id=1, source_target_pairs={{0,4},{4,12},{12,8},{8,0},{1,5},{5,13},{13,9},{9,1},{2,6},{6,14},{... | collective-permute-start | bytes 196616 | tf_op jit(solution)/shard_map/ppermute | solution.py:303
  36.0 5.7 %collective-permute-start.19 = (bf16[16,2048]{1,0:T(8,128)(2,1)S(1)}, bf16[16,2048]{1,0:T(8,128)(2,1)S(1)}, u32[]{:S(2)}, u32[]{:S(2)}) collective-permute-start(bf16[16,2048]{1,0:T(8,128)(2,1)S(1)} %broadcast_select_fusion.5), channel_id=1, source_target_pairs={{0,4},{4,12},{12,8},{8,0},{1,5},{5,13},{13,9},{9,1},{2,6},{6,14},{... | collective-permute-start | bytes 196616 | tf_op jit(solution)/shard_map/ppermute | solution.py:303
  37.8 28.8 %copy-start.1 = (bf16[128,2048]{1,0:T(8,128)(2,1)S(1)}, bf16[128,2048]{1,0:T(8,128)(2,1)}, u32[]{:S(2)}) copy-start(bf16[128,2048]{1,0:T(8,128)(2,1)} %refs_17_.1) | copy-start | bytes 1572868
  37.8 3.9 %collective-permute-start.27 = (f32[128,128]{1,0:T(8,128)S(1)}, f32[128,128]{1,0:T(8,128)S(1)}, u32[]{:S(2)}, u32[]{:S(2)}) collective-permute-start(f32[128,128]{1,0:T(8,128)S(1)} %shard_map.134), channel_id=1, source_target_pairs={{0,1},{1,0},{2,3},{3,2},{4,5},{5,4},{6,7},{7,6},{8,9},{9,8},{10,11... | collective-permute-start | bytes 196616 | tf_op jit(solution)/shard_map/ppermute | solution.py:63
  37.9 9.9 %collective-permute-start.20 = (bf16[16,2048]{1,0:T(8,128)(2,1)S(1)}, bf16[16,2048]{1,0:T(8,128)(2,1)S(1)}, u32[]{:S(2)}, u32[]{:S(2)}) collective-permute-start(bf16[16,2048]{1,0:T(8,128)(2,1)S(1)} %broadcast_select_fusion.4), channel_id=1, source_target_pairs={{0,4},{4,12},{12,8},{8,0},{1,5},{5,13},{13,9},{9,1},{2,6},{6,14},{... | collective-permute-start | bytes 196616 | tf_op jit(solution)/shard_map/ppermute | solution.py:303
  39.3 10.4 %collective-permute-start.21 = (bf16[16,2048]{1,0:T(8,128)(2,1)S(1)}, bf16[16,2048]{1,0:T(8,128)(2,1)S(1)}, u32[]{:S(2)}, u32[]{:S(2)}) collective-permute-start(bf16[16,2048]{1,0:T(8,128)(2,1)S(1)} %broadcast_select_fusion.3), channel_id=1, source_target_pairs={{0,4},{4,12},{12,8},{8,0},{1,5},{5,13},{13,9},{9,1},{2,6},{6,14},{... | collective-permute-start | bytes 196616 | tf_op jit(solution)/shard_map/ppermute | solution.py:303
  40.3 9.9 %collective-permute-start.22 = (bf16[16,2048]{1,0:T(8,128)(2,1)S(1)}, bf16[16,2048]{1,0:T(8,128)(2,1)S(1)}, u32[]{:S(2)}, u32[]{:S(2)}) collective-permute-start(bf16[16,2048]{1,0:T(8,128)(2,1)S(1)} %broadcast_select_fusion.2), channel_id=1, source_target_pairs={{0,4},{4,12},{12,8},{8,0},{1,5},{5,13},{13,9},{9,1},{2,6},{6,14},{... | collective-permute-start | bytes 196616 | tf_op jit(solution)/shard_map/ppermute | solution.py:303
  41.7 4.3 %collective-permute-start.28 = (f32[128,128]{1,0:T(8,128)S(1)}, f32[128,128]{1,0:T(8,128)S(1)}, u32[]{:S(2)}, u32[]{:S(2)}) collective-permute-start(f32[128,128]{1,0:T(8,128)S(1)} %add.208), channel_id=1, source_target_pairs={{0,2},{1,3},{2,0},{3,1},{4,6},{5,7},{6,4},{7,5},{8,10},{9,11},{10,... | collective-permute-start | bytes 196616 | tf_op jit(solution)/shard_map/ppermute | solution.py:63
  43.3 10.4 %collective-permute-start.23 = (bf16[16,2048]{1,0:T(8,128)(2,1)S(1)}, bf16[16,2048]{1,0:T(8,128)(2,1)S(1)}, u32[]{:S(2)}, u32[]{:S(2)}) collective-permute-start(bf16[16,2048]{1,0:T(8,128)(2,1)S(1)} %broadcast_select_fusion.1), channel_id=1, source_target_pairs={{0,4},{4,12},{12,8},{8,0},{1,5},{5,13},{13,9},{9,1},{2,6},{6,14},{... | collective-permute-start | bytes 196616 | tf_op jit(solution)/shard_map/ppermute | solution.py:303
  46.4 10.6 %collective-permute-start.29 = (bf16[128,512]{1,0:T(8,128)(2,1)S(1)}, bf16[128,512]{1,0:T(8,128)(2,1)S(1)}, u32[]{:S(2)}, u32[]{:S(2)}) collective-permute-start(bf16[128,512]{1,0:T(8,128)(2,1)S(1)} %shard_map.135), channel_id=1, source_target_pairs={{0,4},{4,12},{12,8},{8,0},{1,5},{5,13},{13,9},{9,1},{2,6},{6,14},{... | collective-permute-start | bytes 393224 | tf_op jit(solution)/shard_map/ppermute | solution.py:358
  47.8 11.6 %collective-permute-start.30 = (bf16[128,512]{1,0:T(8,128)(2,1)S(1)}, bf16[128,512]{1,0:T(8,128)(2,1)S(1)}, u32[]{:S(2)}, u32[]{:S(2)}) collective-permute-start(bf16[128,512]{1,0:T(8,128)(2,1)S(1)} %shard_map.135), channel_id=1, source_target_pairs={{4,0},{12,4},{8,12},{0,8},{5,1},{13,5},{9,13},{1,9},{6,2},{14,6},{... | collective-permute-start | bytes 393224 | tf_op jit(solution)/shard_map/ppermute | solution.py:359
  49.7 7.1 %collective-permute-start.24 = (bf16[16,2048]{1,0:T(8,128)(2,1)S(1)}, bf16[16,2048]{1,0:T(8,128)(2,1)S(1)}, u32[]{:S(2)}, u32[]{:S(2)}) collective-permute-start(bf16[16,2048]{1,0:T(8,128)(2,1)S(1)} %broadcast_select_fusion), channel_id=1, source_target_pairs={{0,4},{4,12},{12,8},{8,0},{1,5},{5,13},{13,9},{9,1},{2,6},{6,14},{... | collective-permute-start | bytes 196616 | tf_op jit(solution)/shard_map/ppermute | solution.py:303
  50.2 1.3 %collective-permute-start.25 = (f32[128,64]{1,0:T(8,128)S(1)}, f32[128,64]{1,0:T(8,128)S(1)}, u32[]{:S(2)}, u32[]{:S(2)}) collective-permute-start(f32[128,64]{1,0:T(8,128)S(1)} %shard_map.133), channel_id=1, source_target_pairs={{0,1},{1,0},{2,3},{3,2},{4,5},{5,4},{6,7},{7,6},{8,9},{9,8},{10,11... | collective-permute-start | bytes 98312 | tf_op jit(solution)/shard_map/ppermute | solution.py:63
  51.5 8.6 %collective-permute-start.33 = (bf16[32,2048]{1,0:T(8,128)(2,1)S(1)}, bf16[32,2048]{1,0:T(8,128)(2,1)S(1)}, u32[]{:S(2)}, u32[]{:S(2)}) collective-permute-start(bf16[32,2048]{1,0:T(8,128)(2,1)S(1)} %pad_maximum_fusion.1), channel_id=1, source_target_pairs={{0,4},{4,12},{12,8},{8,0},{1,5},{5,13},{13,9},{9,1},{2,6},{6,14},{... | collective-permute-start | bytes 393224 | tf_op jit(solution)/shard_map/ppermute | solution.py:311
  53.7 10.8 %collective-permute-start.26 = (f32[128,64]{1,0:T(8,128)S(1)}, f32[128,64]{1,0:T(8,128)S(1)}, u32[]{:S(2)}, u32[]{:S(2)}) collective-permute-start(f32[128,64]{1,0:T(8,128)S(1)} %add.179), channel_id=1, source_target_pairs={{0,2},{1,3},{2,0},{3,1},{4,6},{5,7},{6,4},{7,5},{8,10},{9,11},{10,... | collective-permute-start | bytes 98312 | tf_op jit(solution)/shard_map/ppermute | solution.py:63
  56.9 7.6 %collective-permute-start.34 = (bf16[32,2048]{1,0:T(8,128)(2,1)S(1)}, bf16[32,2048]{1,0:T(8,128)(2,1)S(1)}, u32[]{:S(2)}, u32[]{:S(2)}) collective-permute-start(bf16[32,2048]{1,0:T(8,128)(2,1)S(1)} %pad_maximum_fusion.2), channel_id=1, source_target_pairs={{0,4},{4,12},{12,8},{8,0},{1,5},{5,13},{13,9},{9,1},{2,6},{6,14},{... | collective-permute-start | bytes 393224 | tf_op jit(solution)/shard_map/ppermute | solution.py:311
  57.0 9.6 %collective-permute-start.31 = (bf16[128,256]{1,0:T(8,128)(2,1)S(1)}, bf16[128,256]{1,0:T(8,128)(2,1)S(1)}, u32[]{:S(2)}, u32[]{:S(2)}) collective-permute-start(bf16[128,256]{1,0:T(8,128)(2,1)S(1)} %get-tuple-element.110.refs_20_), channel_id=1, source_target_pairs={{0,4},{4,12},{12,8},{8,0},{1,5},{5,13},{13,9},{9,1},{2,6},{6,14},{... | collective-permute-start | bytes 196616 | tf_op jit(solution)/shard_map/ppermute | solution.py:364
  59.4 7.2 %collective-permute-start.32 = (bf16[128,256]{1,0:T(8,128)(2,1)S(1)}, bf16[128,256]{1,0:T(8,128)(2,1)S(1)}, u32[]{:S(2)}, u32[]{:S(2)}) collective-permute-start(bf16[128,256]{1,0:T(8,128)(2,1)S(1)} %get-tuple-element.105.refs_26_), channel_id=1, source_target_pairs={{4,0},{12,4},{8,12},{0,8},{5,1},{13,5},{9,13},{1,9},{6,2},{14,6},{... | collective-permute-start | bytes 196616 | tf_op jit(solution)/shard_map/ppermute | solution.py:366
  60.0 15.1 %collective-permute-start.35 = (bf16[32,2048]{1,0:T(8,128)(2,1)S(1)}, bf16[32,2048]{1,0:T(8,128)(2,1)S(1)}, u32[]{:S(2)}, u32[]{:S(2)}) collective-permute-start(bf16[32,2048]{1,0:T(8,128)(2,1)S(1)} %collective-permute-done.33.refs_0_), channel_id=1, source_target_pairs={{0,4},{4,12},{12,8},{8,0},{1,5},{5,13},{13,9},{9,1},{2,6},{6,14},{... | collective-permute-start | bytes 393224 | tf_op jit(solution)/shard_map/ppermute | solution.py:311
  64.4 10.7 %collective-permute-start.36 = (bf16[32,2048]{1,0:T(8,128)(2,1)S(1)}, bf16[32,2048]{1,0:T(8,128)(2,1)S(1)}, u32[]{:S(2)}, u32[]{:S(2)}) collective-permute-start(bf16[32,2048]{1,0:T(8,128)(2,1)S(1)} %collective-permute-done.34.refs_1_), channel_id=1, source_target_pairs={{0,4},{4,12},{12,8},{8,0},{1,5},{5,13},{13,9},{9,1},{2,6},{6,14},{... | collective-permute-start | bytes 393224 | tf_op jit(solution)/shard_map/ppermute | solution.py:311
  69.5 1.3 %collective-permute-start.37 = (f32[128,64]{1,0:T(8,128)S(1)}, f32[128,64]{1,0:T(8,128)S(1)}, u32[]{:S(2)}, u32[]{:S(2)}) collective-permute-start(f32[128,64]{1,0:T(8,128)S(1)} %shard_map.137), channel_id=1, source_target_pairs={{0,1},{1,0},{2,3},{3,2},{4,5},{5,4},{6,7},{7,6},{8,9},{9,8},{10,11... | collective-permute-start | bytes 98312 | tf_op jit(solution)/shard_map/ppermute | solution.py:63
  70.8 4.3 %collective-permute-start.38 = (f32[128,64]{1,0:T(8,128)S(1)}, f32[128,64]{1,0:T(8,128)S(1)}, u32[]{:S(2)}, u32[]{:S(2)}) collective-permute-start(f32[128,64]{1,0:T(8,128)S(1)} %add.210), channel_id=1, source_target_pairs={{0,2},{1,3},{2,0},{3,1},{4,6},{5,7},{6,4},{7,5},{8,10},{9,11},{10,... | collective-permute-start | bytes 98312 | tf_op jit(solution)/shard_map/ppermute | solution.py:63

commit v3 on v2

--- a/solution.py
+++ b/solution.py
@@ -15,7 +15,6 @@
 EXPONENT_SCALE = HEAD_SIZE ** (-0.5) * math.log2(math.e)
 CHUNK_ROWS = 16
 LAG = 4
-PIECES = 1
 JOINED = 2
 KERNEL_VMEM = 8 << 20
 
@@ -171,25 +170,24 @@
     )
 
 
-def low_kernel(weight_ref, *refs):
-    out_ref = refs[-1]
-    total, lane = None, 0
-    for rows_ref in refs[:-1]:
-        ends = lane + rows_ref.shape[1]
-        part = lax.dot_general(
-            rows_ref[...],
-            weight_ref[:, lane:ends],
-            CONTRACT_LAST,
-            preferred_element_type=jnp.float32,
-        )
-        total = part if total is None else total + part
-        lane = ends
-    out_ref[...] = total
+def low_kernel(weight_ref, rows_ref, out_ref):
+    out_ref[...] = lax.dot_general(
+        rows_ref[...], weight_ref[...], CONTRACT_LAST, preferred_element_type=jnp.float32
+    )
+
+
+def out_low_kernel(weight_ref, rows_ref, out_ref):
+    out_ref[...] = lax.dot_general(
+        weight_ref[...], rows_ref[...], CONTRACT_LAST, preferred_element_type=jnp.float32
+    )
 
 
 def up_kernel(weight_ref, low_ref, out_ref):
-    out_ref[...] = jnp.dot(
-        low_ref[...].astype(jnp.bfloat16), weight_ref[...], preferred_element_type=jnp.float32
+    out_ref[...] = lax.dot_general(
+        low_ref[...].astype(jnp.bfloat16),
+        weight_ref[...],
+        CONTRACT_FIRST,
+        preferred_element_type=jnp.float32,
     ).astype(out_ref.dtype)
 
 
@@ -216,19 +214,18 @@
 
 
 def attend_kernel(
-    first_head, group_size, block_count, weight_ref, low_ref, base_ref, tables_ref, hidden_ref, *refs
+    group_size, block_count, weight_ref, low_ref, base_ref, tables_ref, hidden_ref, *refs
 ):
     key_refs = refs[:block_count]
     value_refs = refs[block_count : 2 * block_count]
     out_ref = refs[-1]
     low = low_ref[...].astype(jnp.bfloat16)
-    first = first_head * HEAD_SIZE
-    queries = base_ref[:, first : first + out_ref.shape[1]].astype(jnp.float32) + jnp.dot(
-        low, weight_ref[:, first : first + out_ref.shape[1]], preferred_element_type=jnp.float32
+    queries = base_ref[...].astype(jnp.float32) + jnp.dot(
+        low, weight_ref[...], preferred_element_type=jnp.float32
     )
     group = None
     for lane in range(0, out_ref.shape[1], HEAD_SIZE):
-        head = first_head + lane // HEAD_SIZE
+        head = lane // HEAD_SIZE
         if head // group_size != group:
             group = head // group_size
             lanes = slice(group * HEAD_SIZE, (group + 1) * HEAD_SIZE)
@@ -284,7 +281,7 @@
         output_up_weight,
     )
     own = []
-    for chunk_range in (slice(0, LAG), slice(LAG, None)):
+    for chunk_range in (slice(0, None),):
         own += own_chunks(chunk_range, publisher, version, *weights)
     per = rank // CHUNK_ROWS
 
@@ -380,23 +377,18 @@
     hide = jnp.where(key_pos[:, None] <= query_pos[None, :], 0.0, NEG_BIG)
     local_heads = base_query_rows.shape[1] // HEAD_SIZE
     group_size = local_heads // (pair_width // HEAD_SIZE)
-    piece_heads = local_heads // PIECES
-    pieces_out = [
-        on_chunks(
-            functools.partial(attend_kernel, piece * piece_heads, group_size, len(offsets)),
-            3 * per + 1,
-            per,
-            [query_sums[-1], base_query_rows, tables, hide]
-            + [key_blocks[o] for o in offsets]
-            + [value_blocks[o] for o in offsets],
-            (local_rows, piece_heads * HEAD_SIZE),
-            jnp.bfloat16,
-        )
-        for piece in range(PIECES)
-    ]
-    attended = jnp.concatenate(pieces_out, axis=1)
-    part = on_chunks(low_kernel, 4 * per + 1, per, pieces_out, (local_rows, rank), jnp.float32)
-    out_low = doubling_sums(part, "tp", jnp.float32)[-1]
+    attended = on_chunks(
+        functools.partial(attend_kernel, group_size, len(offsets)),
+        3 * per + 1,
+        per,
+        [query_sums[-1], base_query_rows, tables, hide]
+        + [key_blocks[o] for o in offsets]
+        + [value_blocks[o] for o in offsets],
+        base_query_rows.shape,
+        jnp.bfloat16,
+    )
+    part = on_chunks(out_low_kernel, 4 * per + 1, per, [attended], (rank, local_rows), jnp.float32)
+    out_low = doubling_sums(part, "tp", jnp.bfloat16)[-1]
     adapted = on_chunks(up_kernel, 5 * per + 1, per, [out_low], attended.shape, jnp.bfloat16)
     return (attended, adapted)
 

time: 76.6 us -> 81.5 us (1.064)
  waiting for transfers between devices: 13.3 us -> 18.3 us
  starting transfers between devices: 49.9 us -> 51.4 us
  Pallas kernels: 7.92 us -> 6.45 us
    ppermute x4, waiting for transfers between devices: 3 us -> 6.02 us  [shards(): late.append(lax.ppermute(moving, 'ctx', pairs))]
    ppermute x1, waiting for transfers between devices: 2.06 us -> 4.84 us  [shards(): far = lax.ppermute(ahead[:, :pair_width], 'ctx', forward)]
    ppermute x6, waiting for transfers between devices: 5.86 us -> 3.8 us  [doubling_sums(): other = lax.ppermute(sent, axis, pairs)]
    ppermute x4, waiting for transfers between devices: 0.01 us -> 1.92 us  [shards(): arrived.append(lax.ppermute(own[turn], 'ctx', pairs))]
    pallas_call x2 -> x1, Pallas kernels: 3.75 us -> 2.25 us  [own_chunks(): pl.pallas_call(body, out_shape=[pltpu.VMEM((CHUNK_ROWS, width), jnp.bfloa...]
    ppermute x21, starting transfers between devices: 29.1 us -> 30 us  [shards(): arrived.append(lax.ppermute(moving, 'ctx', pairs))]
    unnamed x16 -> x14, local copies, waits for them, and re-layouts: 2.26 us -> 2.26 us
  transfers between devices with their start and end apart: 39 -> 39, of which waited for: 8 -> 9; matrix products, arithmetic and copies ran while one was open for 2% -> 2% of each run, Pallas kernels for 8% -> 4%
where the time goes in v3:
time: 81.5 us; the launch traced here: 81.3 us
  starting transfers between devices  51.4 us (63%)
  waiting for transfers between devices  18.3 us (22%)
  Pallas kernels  6.45 us (8%)
  local copies, waits for them, and re-layouts  2.29 us (3%)
  between operations  1.76 us (2%)
  other arithmetic  1.05 us (1%)
    ppermute x21, starting transfers between devices, shards(): arrived.append(lax.ppermute(moving, 'ctx', pairs))  30 us
    ppermute x4, starting transfers between devices, shards(): arrived.append(lax.ppermute(own[turn], 'ctx', pairs))  6.21 us
    ppermute x4, waiting for transfers between devices, shards(): late.append(lax.ppermute(moving, 'ctx', pairs))  6.02 us
    ppermute x1, waiting for transfers between devices, shards(): far = lax.ppermute(ahead[:, :pair_width], 'ctx', forward)  4.84 us
    ppermute x6, starting transfers between devices, doubling_sums(): other = lax.ppermute(sent, axis, pairs)  4.81 us
    ppermute x4, starting transfers between devices, shards(): late.append(lax.ppermute(moving, 'ctx', pairs))  4.42 us
    pallas_call x6, Pallas kernels, chunk_call(): pl.pallas_call(body, out_shape=pltpu.VMEM(out_shape.shape, out_shape.dtyp...  4.19 us
    ppermute x6, waiting for transfers between devices, doubling_sums(): other = lax.ppermute(sent, axis, pairs)  3.8 us
  transfers between devices with their start and end apart: 39, of which 9 were waited for; matrix products, arithmetic and copies ran while one was open for 2% of the time, Pallas kernels for 4%

profile of v3, /device:TPU:0, one launch (start us, length us, event | category | flops | bytes accessed | tf_op | source)
XLA Modules:
  0.0 81.3 jit_solution(2061435376914799160)
XLA Ops:
  1.3 0.6 copy-done.4
  1.9 2.3 %shard_map.131 = (bf16[16,2048]{1,0:T(8,128)(2,1)S(1)}, bf16[16,2048]{1,0:T(8,128)(2,1)S(1)}, bf16[16,2048]{1,0:T(8,128)(2,1)S(1)}, bf16[16,2048]{1,0:T(8,128)(2...) custom-call(s32[1]{0:T(128)S(6)} %copy.17.publisher_ref, ...), custom_call_target="tpu_custom_call" | custom-call | tf_op jit(solution)/shard_map/pallas_call | solution.py:156
  4.2 3.1 %collective-permute-start = (bf16[16,2048]{1,0:T(8,128)(2,1)S(1)}, bf16[16,2048]{1,0:T(8,128)(2,1)S(1)}, u32[]{:S(2)}, u32[]{:S(2)}) collective-permute-start(bf16[16,2048]{1,0:T(8,128)(2,1)S(1)} %get-tuple-element.51.refs_1_), channel_id=1, source_target_pairs={{0,4},{4,12},{12,8},{8,0},{1,5},{5,13},{13,9},{9,1},{2,6},{6,14},{... | collective-permute-start | bytes 196616 | tf_op jit(solution)/shard_map/ppermute | solution.py:292
  7.3 2.6 %collective-permute-start.1 = (bf16[16,2048]{1,0:T(8,128)(2,1)S(1)}, bf16[16,2048]{1,0:T(8,128)(2,1)S(1)}, u32[]{:S(2)}, u32[]{:S(2)}) collective-permute-start(bf16[16,2048]{1,0:T(8,128)(2,1)S(1)} %get-tuple-element.50.refs_0_), channel_id=1, source_target_pairs={{0,4},{4,12},{12,8},{8,0},{1,5},{5,13},{13,9},{9,1},{2,6},{6,14},{... | collective-permute-start | bytes 196616 | tf_op jit(solution)/shard_map/ppermute | solution.py:292
  9.9 0.4 collective-permute-start.4
  10.6 1.9 %collective-permute-done.1.refs_8_ = bf16[16,2048]{1,0:T(8,128)(2,1)S(1)} collective-permute-done((bf16[16,2048]{1,0:T(8,128)(2,1)S(1)}, bf16[16,2048]{1,0:T(8,128)(2,1)S(1)}, u32[]{:S(2)}, u32[]{:S(2)}) %collective-permute-start.1) | collective-permute-done | bytes 65568 | tf_op jit(solution)/shard_map/ppermute | solution.py:292
  12.5 2.4 %collective-permute-start.3 = (bf16[16,2048]{1,0:T(8,128)(2,1)S(1)}, bf16[16,2048]{1,0:T(8,128)(2,1)S(1)}, u32[]{:S(2)}, u32[]{:S(2)}) collective-permute-start(bf16[16,2048]{1,0:T(8,128)(2,1)S(1)} %broadcast_select_fusion.20), channel_id=1, source_target_pairs={{0,4},{4,12},{12,8},{8,0},{1,5},{5,13},{13,9},{9,1},{2,6},{6,14},{... | collective-permute-start | bytes 196616 | tf_op jit(solution)/shard_map/ppermute | solution.py:300
  14.9 2.4 %collective-permute-start.2 = (bf16[16,2048]{1,0:T(8,128)(2,1)S(1)}, bf16[16,2048]{1,0:T(8,128)(2,1)S(1)}, u32[]{:S(2)}, u32[]{:S(2)}) collective-permute-start(bf16[16,2048]{1,0:T(8,128)(2,1)S(1)} %broadcast_select_fusion.19), channel_id=1, source_target_pairs={{0,4},{4,12},{12,8},{8,0},{1,5},{5,13},{13,9},{9,1},{2,6},{6,14},{... | collective-permute-start | bytes 196616 | tf_op jit(solution)/shard_map/ppermute | solution.py:300
  17.4 1.8 %collective-permute-start.8 = (bf16[16,2048]{1,0:T(8,128)(2,1)S(1)}, bf16[16,2048]{1,0:T(8,128)(2,1)S(1)}, u32[]{:S(2)}, u32[]{:S(2)}) collective-permute-start(bf16[16,2048]{1,0:T(8,128)(2,1)S(1)} %broadcast_select_fusion.17), channel_id=1, source_target_pairs={{0,4},{4,12},{12,8},{8,0},{1,5},{5,13},{13,9},{9,1},{2,6},{6,14},{... | collective-permute-start | bytes 196616 | tf_op jit(solution)/shard_map/ppermute | solution.py:300
  19.3 0.9 %collective-permute-start.7 = (bf16[16,2048]{1,0:T(8,128)(2,1)S(1)}, bf16[16,2048]{1,0:T(8,128)(2,1)S(1)}, u32[]{:S(2)}, u32[]{:S(2)}) collective-permute-start(bf16[16,2048]{1,0:T(8,128)(2,1)S(1)} %broadcast_select_fusion.16), channel_id=1, source_target_pairs={{0,4},{4,12},{12,8},{8,0},{1,5},{5,13},{13,9},{9,1},{2,6},{6,14},{... | collective-permute-start | bytes 196616 | tf_op jit(solution)/shard_map/ppermute | solution.py:300
  20.3 3.0 %collective-permute-start.6 = (bf16[16,2048]{1,0:T(8,128)(2,1)S(1)}, bf16[16,2048]{1,0:T(8,128)(2,1)S(1)}, u32[]{:S(2)}, u32[]{:S(2)}) collective-permute-start(bf16[16,2048]{1,0:T(8,128)(2,1)S(1)} %broadcast_select_fusion.15), channel_id=1, source_target_pairs={{0,4},{4,12},{12,8},{8,0},{1,5},{5,13},{13,9},{9,1},{2,6},{6,14},{... | collective-permute-start | bytes 196616 | tf_op jit(solution)/shard_map/ppermute | solution.py:300
  23.3 1.4 %collective-permute-start.11 = (bf16[16,2048]{1,0:T(8,128)(2,1)S(1)}, bf16[16,2048]{1,0:T(8,128)(2,1)S(1)}, u32[]{:S(2)}, u32[]{:S(2)}) collective-permute-start(bf16[16,2048]{1,0:T(8,128)(2,1)S(1)} %broadcast_select_fusion.14), channel_id=1, source_target_pairs={{0,4},{4,12},{12,8},{8,0},{1,5},{5,13},{13,9},{9,1},{2,6},{6,14},{... | collective-permute-start | bytes 196616 | tf_op jit(solution)/shard_map/ppermute | solution.py:300
  24.7 1.4 %collective-permute-start.13 = (bf16[16,2048]{1,0:T(8,128)(2,1)S(1)}, bf16[16,2048]{1,0:T(8,128)(2,1)S(1)}, u32[]{:S(2)}, u32[]{:S(2)}) collective-permute-start(bf16[16,2048]{1,0:T(8,128)(2,1)S(1)} %broadcast_select_fusion.13), channel_id=1, source_target_pairs={{0,4},{4,12},{12,8},{8,0},{1,5},{5,13},{13,9},{9,1},{2,6},{6,14},{... | collective-permute-start | bytes 196616 | tf_op jit(solution)/shard_map/ppermute | solution.py:300
  26.1 1.4 %collective-permute-start.15 = (bf16[16,2048]{1,0:T(8,128)(2,1)S(1)}, bf16[16,2048]{1,0:T(8,128)(2,1)S(1)}, u32[]{:S(2)}, u32[]{:S(2)}) collective-permute-start(bf16[16,2048]{1,0:T(8,128)(2,1)S(1)} %broadcast_select_fusion.12), channel_id=1, source_target_pairs={{0,4},{4,12},{12,8},{8,0},{1,5},{5,13},{13,9},{9,1},{2,6},{6,14},{... | collective-permute-start | bytes 196616 | tf_op jit(solution)/shard_map/ppermute | solution.py:300
  27.5 1.7 %collective-permute-start.10 = (bf16[16,2048]{1,0:T(8,128)(2,1)S(1)}, bf16[16,2048]{1,0:T(8,128)(2,1)S(1)}, u32[]{:S(2)}, u32[]{:S(2)}) collective-permute-start(bf16[16,2048]{1,0:T(8,128)(2,1)S(1)} %broadcast_select_fusion.11), channel_id=1, source_target_pairs={{0,4},{4,12},{12,8},{8,0},{1,5},{5,13},{13,9},{9,1},{2,6},{6,14},{... | collective-permute-start | bytes 196616 | tf_op jit(solution)/shard_map/ppermute | solution.py:300
  29.2 1.4 %collective-permute-start.12 = (bf16[16,2048]{1,0:T(8,128)(2,1)S(1)}, bf16[16,2048]{1,0:T(8,128)(2,1)S(1)}, u32[]{:S(2)}, u32[]{:S(2)}) collective-permute-start(bf16[16,2048]{1,0:T(8,128)(2,1)S(1)} %broadcast_select_fusion.10), channel_id=1, source_target_pairs={{0,4},{4,12},{12,8},{8,0},{1,5},{5,13},{13,9},{9,1},{2,6},{6,14},{... | collective-permute-start | bytes 196616 | tf_op jit(solution)/shard_map/ppermute | solution.py:300
  30.6 1.4 %collective-permute-start.14 = (bf16[16,2048]{1,0:T(8,128)(2,1)S(1)}, bf16[16,2048]{1,0:T(8,128)(2,1)S(1)}, u32[]{:S(2)}, u32[]{:S(2)}) collective-permute-start(bf16[16,2048]{1,0:T(8,128)(2,1)S(1)} %broadcast_select_fusion.9), channel_id=1, source_target_pairs={{0,4},{4,12},{12,8},{8,0},{1,5},{5,13},{13,9},{9,1},{2,6},{6,14},{... | collective-permute-start | bytes 196616 | tf_op jit(solution)/shard_map/ppermute | solution.py:300
  32.7 1.4 %collective-permute-start.16 = (bf16[16,2048]{1,0:T(8,128)(2,1)S(1)}, bf16[16,2048]{1,0:T(8,128)(2,1)S(1)}, u32[]{:S(2)}, u32[]{:S(2)}) collective-permute-start(bf16[16,2048]{1,0:T(8,128)(2,1)S(1)} %broadcast_select_fusion.8), channel_id=1, source_target_pairs={{0,4},{4,12},{12,8},{8,0},{1,5},{5,13},{13,9},{9,1},{2,6},{6,14},{... | collective-permute-start | bytes 196616 | tf_op jit(solution)/shard_map/ppermute | solution.py:300
  34.2 1.0 %collective-permute-start.17 = (bf16[16,2048]{1,0:T(8,128)(2,1)S(1)}, bf16[16,2048]{1,0:T(8,128)(2,1)S(1)}, u32[]{:S(2)}, u32[]{:S(2)}) collective-permute-start(bf16[16,2048]{1,0:T(8,128)(2,1)S(1)} %broadcast_select_fusion.7), channel_id=1, source_target_pairs={{0,4},{4,12},{12,8},{8,0},{1,5},{5,13},{13,9},{9,1},{2,6},{6,14},{... | collective-permute-start | bytes 196616 | tf_op jit(solution)/shard_map/ppermute | solution.py:300
  35.2 1.4 %collective-permute-start.18 = (bf16[16,2048]{1,0:T(8,128)(2,1)S(1)}, bf16[16,2048]{1,0:T(8,128)(2,1)S(1)}, u32[]{:S(2)}, u32[]{:S(2)}) collective-permute-start(bf16[16,2048]{1,0:T(8,128)(2,1)S(1)} %broadcast_select_fusion.6), channel_id=1, source_target_pairs={{0,4},{4,12},{12,8},{8,0},{1,5},{5,13},{13,9},{9,1},{2,6},{6,14},{... | collective-permute-start | bytes 196616 | tf_op jit(solution)/shard_map/ppermute | solution.py:300
  36.6 1.4 %collective-permute-start.19 = (bf16[16,2048]{1,0:T(8,128)(2,1)S(1)}, bf16[16,2048]{1,0:T(8,128)(2,1)S(1)}, u32[]{:S(2)}, u32[]{:S(2)}) collective-permute-start(bf16[16,2048]{1,0:T(8,128)(2,1)S(1)} %broadcast_select_fusion.5), channel_id=1, source_target_pairs={{0,4},{4,12},{12,8},{8,0},{1,5},{5,13},{13,9},{9,1},{2,6},{6,14},{... | collective-permute-start | bytes 196616 | tf_op jit(solution)/shard_map/ppermute | solution.py:300
  38.0 0.3 shard_map.133
  38.4 1.4 %collective-permute-start.20 = (bf16[16,2048]{1,0:T(8,128)(2,1)S(1)}, bf16[16,2048]{1,0:T(8,128)(2,1)S(1)}, u32[]{:S(2)}, u32[]{:S(2)}) collective-permute-start(bf16[16,2048]{1,0:T(8,128)(2,1)S(1)} %broadcast_select_fusion.4), channel_id=1, source_target_pairs={{0,4},{4,12},{12,8},{8,0},{1,5},{5,13},{13,9},{9,1},{2,6},{6,14},{... | collective-permute-start | bytes 196616 | tf_op jit(solution)/shard_map/ppermute | solution.py:300
  39.8 1.0 %collective-permute-start.21 = (bf16[16,2048]{1,0:T(8,128)(2,1)S(1)}, bf16[16,2048]{1,0:T(8,128)(2,1)S(1)}, u32[]{:S(2)}, u32[]{:S(2)}) collective-permute-start(bf16[16,2048]{1,0:T(8,128)(2,1)S(1)} %broadcast_select_fusion.3), channel_id=1, source_target_pairs={{0,4},{4,12},{12,8},{8,0},{1,5},{5,13},{13,9},{9,1},{2,6},{6,14},{... | collective-permute-start | bytes 196616 | tf_op jit(solution)/shard_map/ppermute | solution.py:300
  40.8 1.4 %collective-permute-start.22 = (bf16[16,2048]{1,0:T(8,128)(2,1)S(1)}, bf16[16,2048]{1,0:T(8,128)(2,1)S(1)}, u32[]{:S(2)}, u32[]{:S(2)}) collective-permute-start(bf16[16,2048]{1,0:T(8,128)(2,1)S(1)} %broadcast_select_fusion.2), channel_id=1, source_target_pairs={{0,4},{4,12},{12,8},{8,0},{1,5},{5,13},{13,9},{9,1},{2,6},{6,14},{... | collective-permute-start | bytes 196616 | tf_op jit(solution)/shard_map/ppermute | solution.py:300
  42.3 1.6 %collective-permute-start.28 = (f32[128,128]{1,0:T(8,128)S(1)}, f32[128,128]{1,0:T(8,128)S(1)}, u32[]{:S(2)}, u32[]{:S(2)}) collective-permute-start(f32[128,128]{1,0:T(8,128)S(1)} %add.208), channel_id=1, source_target_pairs={{0,2},{1,3},{2,0},{3,1},{4,6},{5,7},{6,4},{7,5},{8,10},{9,11},{10,... | collective-permute-start | bytes 196616 | tf_op jit(solution)/shard_map/ppermute | solution.py:62
  43.8 1.4 %collective-permute-start.23 = (bf16[16,2048]{1,0:T(8,128)(2,1)S(1)}, bf16[16,2048]{1,0:T(8,128)(2,1)S(1)}, u32[]{:S(2)}, u32[]{:S(2)}) collective-permute-start(bf16[16,2048]{1,0:T(8,128)(2,1)S(1)} %broadcast_select_fusion.1), channel_id=1, source_target_pairs={{0,4},{4,12},{12,8},{8,0},{1,5},{5,13},{13,9},{9,1},{2,6},{6,14},{... | collective-permute-start | bytes 196616 | tf_op jit(solution)/shard_map/ppermute | solution.py:300
  45.2 1.4 %collective-permute-done.28 = f32[128,128]{1,0:T(8,128)S(1)} collective-permute-done((f32[128,128]{1,0:T(8,128)S(1)}, f32[128,128]{1,0:T(8,128)S(1)}, u32[]{:S(2)}, u32[]{:S(2)}) %collective-permute-start.28) | collective-permute-done | bytes 65568 | tf_op jit(solution)/shard_map/ppermute | solution.py:62
  46.9 1.4 %collective-permute-start.29 = (bf16[128,512]{1,0:T(8,128)(2,1)S(1)}, bf16[128,512]{1,0:T(8,128)(2,1)S(1)}, u32[]{:S(2)}, u32[]{:S(2)}) collective-permute-start(bf16[128,512]{1,0:T(8,128)(2,1)S(1)} %shard_map.134), channel_id=1, source_target_pairs={{0,4},{4,12},{12,8},{8,0},{1,5},{5,13},{13,9},{9,1},{2,6},{6,14},{... | collective-permute-start | bytes 393224 | tf_op jit(solution)/shard_map/ppermute | solution.py:355
  48.3 1.6 %collective-permute-start.30 = (bf16[128,512]{1,0:T(8,128)(2,1)S(1)}, bf16[128,512]{1,0:T(8,128)(2,1)S(1)}, u32[]{:S(2)}, u32[]{:S(2)}) collective-permute-start(bf16[128,512]{1,0:T(8,128)(2,1)S(1)} %shard_map.134), channel_id=1, source_target_pairs={{4,0},{12,4},{8,12},{0,8},{5,1},{13,5},{9,13},{1,9},{6,2},{14,6},{... | collective-permute-start | bytes 393224 | tf_op jit(solution)/shard_map/ppermute | solution.py:356
  50.3 0.5 collective-permute-start.24
  50.8 1.2 %collective-permute-done.25 = f32[128,64]{1,0:T(8,128)S(1)} collective-permute-done((f32[128,64]{1,0:T(8,128)S(1)}, f32[128,64]{1,0:T(8,128)S(1)}, u32[]{:S(2)}, u32[]{:S(2)}) %collective-permute-start.25) | collective-permute-done | bytes 32800 | tf_op jit(solution)/shard_map/ppermute | solution.py:62
  52.0 2.2 %collective-permute-start.33 = (bf16[32,2048]{1,0:T(8,128)(2,1)S(1)}, bf16[32,2048]{1,0:T(8,128)(2,1)S(1)}, u32[]{:S(2)}, u32[]{:S(2)}) collective-permute-start(bf16[32,2048]{1,0:T(8,128)(2,1)S(1)} %pad_maximum_fusion.1), channel_id=1, source_target_pairs={{0,4},{4,12},{12,8},{8,0},{1,5},{5,13},{13,9},{9,1},{2,6},{6,14},{... | collective-permute-start | bytes 393224 | tf_op jit(solution)/shard_map/ppermute | solution.py:308
  54.3 1.6 %collective-permute-start.26 = (f32[128,64]{1,0:T(8,128)S(1)}, f32[128,64]{1,0:T(8,128)S(1)}, u32[]{:S(2)}, u32[]{:S(2)}) collective-permute-start(f32[128,64]{1,0:T(8,128)S(1)} %add.179), channel_id=1, source_target_pairs={{0,2},{1,3},{2,0},{3,1},{4,6},{5,7},{6,4},{7,5},{8,10},{9,11},{10,... | collective-permute-start | bytes 98312 | tf_op jit(solution)/shard_map/ppermute | solution.py:62
  55.8 1.6 %collective-permute-done.24.refs_15_.refs_13_.refs_11_ = bf16[16,2048]{1,0:T(8,128)(2,1)S(1)} collective-permute-done((bf16[16,2048]{1,0:T(8,128)(2,1)S(1)}, bf16[16,2048]{1,0:T(8,128)(2,1)S(1)}, u32[]{:S(2)}, u32[]{:S(2)}) %collective-permute-start.24) | collective-permute-done | bytes 65568 | tf_op jit(solution)/shard_map/ppermute | solution.py:300
  57.5 2.4 %collective-permute-start.31 = (bf16[128,256]{1,0:T(8,128)(2,1)S(1)}, bf16[128,256]{1,0:T(8,128)(2,1)S(1)}, u32[]{:S(2)}, u32[]{:S(2)}) collective-permute-start(bf16[128,256]{1,0:T(8,128)(2,1)S(1)} %get-tuple-element.110.refs_20_), channel_id=1, source_target_pairs={{0,4},{4,12},{12,8},{8,0},{1,5},{5,13},{13,9},{9,1},{2,6},{6,14},{... | collective-permute-start | bytes 196616 | tf_op jit(solution)/shard_map/ppermute | solution.py:361
  59.9 0.7 collective-permute-start.32
  60.6 4.8 %collective-permute-done.31.refs_23_ = bf16[128,256]{1,0:T(8,128)(2,1)S(1)} collective-permute-done((bf16[128,256]{1,0:T(8,128)(2,1)S(1)}, bf16[128,256]{1,0:T(8,128)(2,1)S(1)}, u32[]{:S(2)}, u32[]{:S(2)}) %collective-permute-start.31) | collective-permute-done | bytes 65568 | tf_op jit(solution)/shard_map/ppermute | solution.py:361
  65.4 2.6 %shard_map.135.refs_14_ = bf16[128,2048]{1,0:T(8,128)(2,1)S(1)} custom-call(s32[1]{0:T(128)} %bitcast.1.behind_ref, bf16[16,2048]{1,0:T(8,128)(2,1)S(1)} %get-tuple-element.55.refs_0_, bf16[16,2048]{1,0:T(8,128)(2,1)S(1)} %get-tuple-element.56.refs_1_, bf16[16,2048]{1,0:T(8,128)(2,1)S(1)} %get-tuple-element.57.refs_2_, ...), custom_call_target="tpu_custom_call" | custom-call | tf_op jit(solution)/shard_map/pallas_call | solution.py:105
  68.0 0.3 shard_map.136
  68.5 1.2 %collective-permute-done.37 = bf16[64,128]{1,0:T(8,128)(2,1)S(1)} collective-permute-done((bf16[64,128]{1,0:T(8,128)(2,1)S(1)}, bf16[64,128]{1,0:T(8,128)(2,1)S(1)}, u32[]{:S(2)}, u32[]{:S(2)}) %collective-permute-start.37) | collective-permute-done | bytes 16416 | tf_op jit(solution)/shard_map/ppermute | solution.py:62
  69.7 1.6 %collective-permute-start.38 = (bf16[64,128]{1,0:T(8,128)(2,1)S(1)}, bf16[64,128]{1,0:T(8,128)(2,1)S(1)}, u32[]{:S(2)}, u32[]{:S(2)}) collective-permute-start(bf16[64,128]{1,0:T(8,128)(2,1)S(1)} %add_convert_fusion), channel_id=1, source_target_pairs={{0,2},{1,3},{2,0},{3,1},{4,6},{5,7},{6,4},{7,5},{8,10},{9,11},{10,... | collective-permute-start | bytes 49160 | tf_op jit(solution)/shard_map/ppermute | solution.py:62
  71.5 0.8 copy.15
  72.3 1.8 %collective-permute-start.36 = (bf16[32,2048]{1,0:T(8,128)(2,1)S(1)}, bf16[32,2048]{1,0:T(8,128)(2,1)S(1)}, u32[]{:S(2)}, u32[]{:S(2)}) collective-permute-start(bf16[32,2048]{1,0:T(8,128)(2,1)S(1)} %collective-permute-done.34.refs_1_), channel_id=1, source_target_pairs={{0,4},{4,12},{12,8},{8,0},{1,5},{5,13},{13,9},{9,1},{2,6},{6,14},{... | collective-permute-start | bytes 393224 | tf_op jit(solution)/shard_map/ppermute | solution.py:308
  74.2 4.3 %collective-permute-done.35.refs_2_ = bf16[32,2048]{1,0:T(8,128)(2,1)S(1)} collective-permute-done((bf16[32,2048]{1,0:T(8,128)(2,1)S(1)}, bf16[32,2048]{1,0:T(8,128)(2,1)S(1)}, u32[]{:S(2)}, u32[]{:S(2)}) %collective-permute-start.35) | collective-permute-done | bytes 131104 | tf_op jit(solution)/shard_map/ppermute | solution.py:308
  78.5 1.7 %collective-permute-done.36.refs_3_ = bf16[32,2048]{1,0:T(8,128)(2,1)S(1)} collective-permute-done((bf16[32,2048]{1,0:T(8,128)(2,1)S(1)}, bf16[32,2048]{1,0:T(8,128)(2,1)S(1)}, u32[]{:S(2)}, u32[]{:S(2)}) %collective-permute-start.36) | collective-permute-done | bytes 131104 | tf_op jit(solution)/shard_map/ppermute | solution.py:308
  80.2 0.3 shard_map.137
  80.5 0.8 copy.16
  (98 shorter events, 2.6 us)
Async XLA Ops:
  1.3 0.7 copy-start.4
  1.9 30.0 %copy-start.5 = (s32[8]{0:T(128)S(1)}, s32[8]{0:T(128)}, u32[]{:S(2)}) copy-start(s32[8]{0:T(128)} %param.16) | copy-start | bytes 100
  4.2 33.8 %copy-start = (bf16[128,2048]{1,0:T(8,128)(2,1)S(1)}, bf16[128,2048]{1,0:T(8,128)(2,1)}, u32[]{:S(2)}) copy-start(bf16[128,2048]{1,0:T(8,128)(2,1)} %refs_24_.1) | copy-start | bytes 1572868
  4.2 10.7 %collective-permute-start = (bf16[16,2048]{1,0:T(8,128)(2,1)S(1)}, bf16[16,2048]{1,0:T(8,128)(2,1)S(1)}, u32[]{:S(2)}, u32[]{:S(2)}) collective-permute-start(bf16[16,2048]{1,0:T(8,128)(2,1)S(1)} %get-tuple-element.51.refs_1_), channel_id=1, source_target_pairs={{0,4},{4,12},{12,8},{8,0},{1,5},{5,13},{13,9},{9,1},{2,6},{6,14},{... | collective-permute-start | bytes 196616 | tf_op jit(solution)/shard_map/ppermute | solution.py:292
  7.3 5.2 %collective-permute-start.1 = (bf16[16,2048]{1,0:T(8,128)(2,1)S(1)}, bf16[16,2048]{1,0:T(8,128)(2,1)S(1)}, u32[]{:S(2)}, u32[]{:S(2)}) collective-permute-start(bf16[16,2048]{1,0:T(8,128)(2,1)S(1)} %get-tuple-element.50.refs_0_), channel_id=1, source_target_pairs={{0,4},{4,12},{12,8},{8,0},{1,5},{5,13},{13,9},{9,1},{2,6},{6,14},{... | collective-permute-start | bytes 196616 | tf_op jit(solution)/shard_map/ppermute | solution.py:292
  9.9 7.5 %collective-permute-start.4 = (bf16[16,2048]{1,0:T(8,128)(2,1)S(1)}, bf16[16,2048]{1,0:T(8,128)(2,1)S(1)}, u32[]{:S(2)}, u32[]{:S(2)}) collective-permute-start(bf16[16,2048]{1,0:T(8,128)(2,1)S(1)} %get-tuple-element.53.refs_3_), channel_id=1, source_target_pairs={{0,4},{4,12},{12,8},{8,0},{1,5},{5,13},{13,9},{9,1},{2,6},{6,14},{... | collective-permute-start | bytes 196616 | tf_op jit(solution)/shard_map/ppermute | solution.py:292
  10.4 7.0 %collective-permute-start.5 = (bf16[16,2048]{1,0:T(8,128)(2,1)S(1)}, bf16[16,2048]{1,0:T(8,128)(2,1)S(1)}, u32[]{:S(2)}, u32[]{:S(2)}) collective-permute-start(bf16[16,2048]{1,0:T(8,128)(2,1)S(1)} %get-tuple-element.52.refs_2_), channel_id=1, source_target_pairs={{0,4},{4,12},{12,8},{8,0},{1,5},{5,13},{13,9},{9,1},{2,6},{6,14},{... | collective-permute-start | bytes 196616 | tf_op jit(solution)/shard_map/ppermute | solution.py:292
  12.5 6.8 %collective-permute-start.3 = (bf16[16,2048]{1,0:T(8,128)(2,1)S(1)}, bf16[16,2048]{1,0:T(8,128)(2,1)S(1)}, u32[]{:S(2)}, u32[]{:S(2)}) collective-permute-start(bf16[16,2048]{1,0:T(8,128)(2,1)S(1)} %broadcast_select_fusion.20), channel_id=1, source_target_pairs={{0,4},{4,12},{12,8},{8,0},{1,5},{5,13},{13,9},{9,1},{2,6},{6,14},{... | collective-permute-start | bytes 196616 | tf_op jit(solution)/shard_map/ppermute | solution.py:300
  14.9 5.3 %collective-permute-start.2 = (bf16[16,2048]{1,0:T(8,128)(2,1)S(1)}, bf16[16,2048]{1,0:T(8,128)(2,1)S(1)}, u32[]{:S(2)}, u32[]{:S(2)}) collective-permute-start(bf16[16,2048]{1,0:T(8,128)(2,1)S(1)} %broadcast_select_fusion.19), channel_id=1, source_target_pairs={{0,4},{4,12},{12,8},{8,0},{1,5},{5,13},{13,9},{9,1},{2,6},{6,14},{... | collective-permute-start | bytes 196616 | tf_op jit(solution)/shard_map/ppermute | solution.py:300
  17.3 5.9 %collective-permute-start.9 = (bf16[16,2048]{1,0:T(8,128)(2,1)S(1)}, bf16[16,2048]{1,0:T(8,128)(2,1)S(1)}, u32[]{:S(2)}, u32[]{:S(2)}) collective-permute-start(bf16[16,2048]{1,0:T(8,128)(2,1)S(1)} %broadcast_select_fusion.18), channel_id=1, source_target_pairs={{0,4},{4,12},{12,8},{8,0},{1,5},{5,13},{13,9},{9,1},{2,6},{6,14},{... | collective-permute-start | bytes 196616 | tf_op jit(solution)/shard_map/ppermute | solution.py:300
  17.4 7.2 %collective-permute-start.8 = (bf16[16,2048]{1,0:T(8,128)(2,1)S(1)}, bf16[16,2048]{1,0:T(8,128)(2,1)S(1)}, u32[]{:S(2)}, u32[]{:S(2)}) collective-permute-start(bf16[16,2048]{1,0:T(8,128)(2,1)S(1)} %broadcast_select_fusion.17), channel_id=1, source_target_pairs={{0,4},{4,12},{12,8},{8,0},{1,5},{5,13},{13,9},{9,1},{2,6},{6,14},{... | collective-permute-start | bytes 196616 | tf_op jit(solution)/shard_map/ppermute | solution.py:300
  19.3 6.8 %collective-permute-start.7 = (bf16[16,2048]{1,0:T(8,128)(2,1)S(1)}, bf16[16,2048]{1,0:T(8,128)(2,1)S(1)}, u32[]{:S(2)}, u32[]{:S(2)}) collective-permute-start(bf16[16,2048]{1,0:T(8,128)(2,1)S(1)} %broadcast_select_fusion.16), channel_id=1, source_target_pairs={{0,4},{4,12},{12,8},{8,0},{1,5},{5,13},{13,9},{9,1},{2,6},{6,14},{... | collective-permute-start | bytes 196616 | tf_op jit(solution)/shard_map/ppermute | solution.py:300
  20.3 26.4 %copy-start.2 = (bf16[128,256]{1,0:T(8,128)(2,1)S(1)}, bf16[128,256]{1,0:T(8,128)(2,1)}, u32[]{:S(2)}) copy-start(bf16[128,256]{1,0:T(8,128)(2,1)} %refs_5_.1) | copy-start | bytes 196612
  20.3 26.4 %copy-start.3 = (bf16[128,256]{1,0:T(8,128)(2,1)S(1)}, bf16[128,256]{1,0:T(8,128)(2,1)}, u32[]{:S(2)}) copy-start(bf16[128,256]{1,0:T(8,128)(2,1)} %refs_6_.1) | copy-start | bytes 196612
  20.3 7.2 %collective-permute-start.6 = (bf16[16,2048]{1,0:T(8,128)(2,1)S(1)}, bf16[16,2048]{1,0:T(8,128)(2,1)S(1)}, u32[]{:S(2)}, u32[]{:S(2)}) collective-permute-start(bf16[16,2048]{1,0:T(8,128)(2,1)S(1)} %broadcast_select_fusion.15), channel_id=1, source_target_pairs={{0,4},{4,12},{12,8},{8,0},{1,5},{5,13},{13,9},{9,1},{2,6},{6,14},{... | collective-permute-start | bytes 196616 | tf_op jit(solution)/shard_map/ppermute | solution.py:300
  23.3 5.9 %collective-permute-start.11 = (bf16[16,2048]{1,0:T(8,128)(2,1)S(1)}, bf16[16,2048]{1,0:T(8,128)(2,1)S(1)}, u32[]{:S(2)}, u32[]{:S(2)}) collective-permute-start(bf16[16,2048]{1,0:T(8,128)(2,1)S(1)} %broadcast_select_fusion.14), channel_id=1, source_target_pairs={{0,4},{4,12},{12,8},{8,0},{1,5},{5,13},{13,9},{9,1},{2,6},{6,14},{... | collective-permute-start | bytes 196616 | tf_op jit(solution)/shard_map/ppermute | solution.py:300
  24.7 5.9 %collective-permute-start.13 = (bf16[16,2048]{1,0:T(8,128)(2,1)S(1)}, bf16[16,2048]{1,0:T(8,128)(2,1)S(1)}, u32[]{:S(2)}, u32[]{:S(2)}) collective-permute-start(bf16[16,2048]{1,0:T(8,128)(2,1)S(1)} %broadcast_select_fusion.13), channel_id=1, source_target_pairs={{0,4},{4,12},{12,8},{8,0},{1,5},{5,13},{13,9},{9,1},{2,6},{6,14},{... | collective-permute-start | bytes 196616 | tf_op jit(solution)/shard_map/ppermute | solution.py:300
  26.1 6.7 %collective-permute-start.15 = (bf16[16,2048]{1,0:T(8,128)(2,1)S(1)}, bf16[16,2048]{1,0:T(8,128)(2,1)S(1)}, u32[]{:S(2)}, u32[]{:S(2)}) collective-permute-start(bf16[16,2048]{1,0:T(8,128)(2,1)S(1)} %broadcast_select_fusion.12), channel_id=1, source_target_pairs={{0,4},{4,12},{12,8},{8,0},{1,5},{5,13},{13,9},{9,1},{2,6},{6,14},{... | collective-permute-start | bytes 196616 | tf_op jit(solution)/shard_map/ppermute | solution.py:300
  27.5 6.7 %collective-permute-start.10 = (bf16[16,2048]{1,0:T(8,128)(2,1)S(1)}, bf16[16,2048]{1,0:T(8,128)(2,1)S(1)}, u32[]{:S(2)}, u32[]{:S(2)}) collective-permute-start(bf16[16,2048]{1,0:T(8,128)(2,1)S(1)} %broadcast_select_fusion.11), channel_id=1, source_target_pairs={{0,4},{4,12},{12,8},{8,0},{1,5},{5,13},{13,9},{9,1},{2,6},{6,14},{... | collective-permute-start | bytes 196616 | tf_op jit(solution)/shard_map/ppermute | solution.py:300
  29.2 6.0 %collective-permute-start.12 = (bf16[16,2048]{1,0:T(8,128)(2,1)S(1)}, bf16[16,2048]{1,0:T(8,128)(2,1)S(1)}, u32[]{:S(2)}, u32[]{:S(2)}) collective-permute-start(bf16[16,2048]{1,0:T(8,128)(2,1)S(1)} %broadcast_select_fusion.10), channel_id=1, source_target_pairs={{0,4},{4,12},{12,8},{8,0},{1,5},{5,13},{13,9},{9,1},{2,6},{6,14},{... | collective-permute-start | bytes 196616 | tf_op jit(solution)/shard_map/ppermute | solution.py:300
  30.6 6.0 %collective-permute-start.14 = (bf16[16,2048]{1,0:T(8,128)(2,1)S(1)}, bf16[16,2048]{1,0:T(8,128)(2,1)S(1)}, u32[]{:S(2)}, u32[]{:S(2)}) collective-permute-start(bf16[16,2048]{1,0:T(8,128)(2,1)S(1)} %broadcast_select_fusion.9), channel_id=1, source_target_pairs={{0,4},{4,12},{12,8},{8,0},{1,5},{5,13},{13,9},{9,1},{2,6},{6,14},{... | collective-permute-start | bytes 196616 | tf_op jit(solution)/shard_map/ppermute | solution.py:300
  32.7 5.7 %collective-permute-start.16 = (bf16[16,2048]{1,0:T(8,128)(2,1)S(1)}, bf16[16,2048]{1,0:T(8,128)(2,1)S(1)}, u32[]{:S(2)}, u32[]{:S(2)}) collective-permute-start(bf16[16,2048]{1,0:T(8,128)(2,1)S(1)} %broadcast_select_fusion.8), channel_id=1, source_target_pairs={{0,4},{4,12},{12,8},{8,0},{1,5},{5,13},{13,9},{9,1},{2,6},{6,14},{... | collective-permute-start | bytes 196616 | tf_op jit(solution)/shard_map/ppermute | solution.py:300
  34.2 5.7 %collective-permute-start.17 = (bf16[16,2048]{1,0:T(8,128)(2,1)S(1)}, bf16[16,2048]{1,0:T(8,128)(2,1)S(1)}, u32[]{:S(2)}, u32[]{:S(2)}) collective-permute-start(bf16[16,2048]{1,0:T(8,128)(2,1)S(1)} %broadcast_select_fusion.7), channel_id=1, source_target_pairs={{0,4},{4,12},{12,8},{8,0},{1,5},{5,13},{13,9},{9,1},{2,6},{6,14},{... | collective-permute-start | bytes 196616 | tf_op jit(solution)/shard_map/ppermute | solution.py:300
  35.2 5.7 %collective-permute-start.18 = (bf16[16,2048]{1,0:T(8,128)(2,1)S(1)}, bf16[16,2048]{1,0:T(8,128)(2,1)S(1)}, u32[]{:S(2)}, u32[]{:S(2)}) collective-permute-start(bf16[16,2048]{1,0:T(8,128)(2,1)S(1)} %broadcast_select_fusion.6), channel_id=1, source_target_pairs={{0,4},{4,12},{12,8},{8,0},{1,5},{5,13},{13,9},{9,1},{2,6},{6,14},{... | collective-permute-start | bytes 196616 | tf_op jit(solution)/shard_map/ppermute | solution.py:300
  36.6 5.7 %collective-permute-start.19 = (bf16[16,2048]{1,0:T(8,128)(2,1)S(1)}, bf16[16,2048]{1,0:T(8,128)(2,1)S(1)}, u32[]{:S(2)}, u32[]{:S(2)}) collective-permute-start(bf16[16,2048]{1,0:T(8,128)(2,1)S(1)} %broadcast_select_fusion.5), channel_id=1, source_target_pairs={{0,4},{4,12},{12,8},{8,0},{1,5},{5,13},{13,9},{9,1},{2,6},{6,14},{... | collective-permute-start | bytes 196616 | tf_op jit(solution)/shard_map/ppermute | solution.py:300
  38.3 27.1 %copy-start.1 = (bf16[128,2048]{1,0:T(8,128)(2,1)S(1)}, bf16[128,2048]{1,0:T(8,128)(2,1)}, u32[]{:S(2)}) copy-start(bf16[128,2048]{1,0:T(8,128)(2,1)} %refs_17_.1) | copy-start | bytes 1572868
  38.3 3.9 %collective-permute-start.27 = (f32[128,128]{1,0:T(8,128)S(1)}, f32[128,128]{1,0:T(8,128)S(1)}, u32[]{:S(2)}, u32[]{:S(2)}) collective-permute-start(f32[128,128]{1,0:T(8,128)S(1)} %shard_map.133), channel_id=1, source_target_pairs={{0,1},{1,0},{2,3},{3,2},{4,5},{5,4},{6,7},{7,6},{8,9},{9,8},{10,11... | collective-permute-start | bytes 196616 | tf_op jit(solution)/shard_map/ppermute | solution.py:62
  38.4 9.9 %collective-permute-start.20 = (bf16[16,2048]{1,0:T(8,128)(2,1)S(1)}, bf16[16,2048]{1,0:T(8,128)(2,1)S(1)}, u32[]{:S(2)}, u32[]{:S(2)}) collective-permute-start(bf16[16,2048]{1,0:T(8,128)(2,1)S(1)} %broadcast_select_fusion.4), channel_id=1, source_target_pairs={{0,4},{4,12},{12,8},{8,0},{1,5},{5,13},{13,9},{9,1},{2,6},{6,14},{... | collective-permute-start | bytes 196616 | tf_op jit(solution)/shard_map/ppermute | solution.py:300
  39.8 10.4 %collective-permute-start.21 = (bf16[16,2048]{1,0:T(8,128)(2,1)S(1)}, bf16[16,2048]{1,0:T(8,128)(2,1)S(1)}, u32[]{:S(2)}, u32[]{:S(2)}) collective-permute-start(bf16[16,2048]{1,0:T(8,128)(2,1)S(1)} %broadcast_select_fusion.3), channel_id=1, source_target_pairs={{0,4},{4,12},{12,8},{8,0},{1,5},{5,13},{13,9},{9,1},{2,6},{6,14},{... | collective-permute-start | bytes 196616 | tf_op jit(solution)/shard_map/ppermute | solution.py:300
  40.8 9.9 %collective-permute-start.22 = (bf16[16,2048]{1,0:T(8,128)(2,1)S(1)}, bf16[16,2048]{1,0:T(8,128)(2,1)S(1)}, u32[]{:S(2)}, u32[]{:S(2)}) collective-permute-start(bf16[16,2048]{1,0:T(8,128)(2,1)S(1)} %broadcast_select_fusion.2), channel_id=1, source_target_pairs={{0,4},{4,12},{12,8},{8,0},{1,5},{5,13},{13,9},{9,1},{2,6},{6,14},{... | collective-permute-start | bytes 196616 | tf_op jit(solution)/shard_map/ppermute | solution.py:300
  42.3 4.3 %collective-permute-start.28 = (f32[128,128]{1,0:T(8,128)S(1)}, f32[128,128]{1,0:T(8,128)S(1)}, u32[]{:S(2)}, u32[]{:S(2)}) collective-permute-start(f32[128,128]{1,0:T(8,128)S(1)} %add.208), channel_id=1, source_target_pairs={{0,2},{1,3},{2,0},{3,1},{4,6},{5,7},{6,4},{7,5},{8,10},{9,11},{10,... | collective-permute-start | bytes 196616 | tf_op jit(solution)/shard_map/ppermute | solution.py:62
  43.8 10.4 %collective-permute-start.23 = (bf16[16,2048]{1,0:T(8,128)(2,1)S(1)}, bf16[16,2048]{1,0:T(8,128)(2,1)S(1)}, u32[]{:S(2)}, u32[]{:S(2)}) collective-permute-start(bf16[16,2048]{1,0:T(8,128)(2,1)S(1)} %broadcast_select_fusion.1), channel_id=1, source_target_pairs={{0,4},{4,12},{12,8},{8,0},{1,5},{5,13},{13,9},{9,1},{2,6},{6,14},{... | collective-permute-start | bytes 196616 | tf_op jit(solution)/shard_map/ppermute | solution.py:300
  46.9 10.6 %collective-permute-start.29 = (bf16[128,512]{1,0:T(8,128)(2,1)S(1)}, bf16[128,512]{1,0:T(8,128)(2,1)S(1)}, u32[]{:S(2)}, u32[]{:S(2)}) collective-permute-start(bf16[128,512]{1,0:T(8,128)(2,1)S(1)} %shard_map.134), channel_id=1, source_target_pairs={{0,4},{4,12},{12,8},{8,0},{1,5},{5,13},{13,9},{9,1},{2,6},{6,14},{... | collective-permute-start | bytes 393224 | tf_op jit(solution)/shard_map/ppermute | solution.py:355
  48.3 11.6 %collective-permute-start.30 = (bf16[128,512]{1,0:T(8,128)(2,1)S(1)}, bf16[128,512]{1,0:T(8,128)(2,1)S(1)}, u32[]{:S(2)}, u32[]{:S(2)}) collective-permute-start(bf16[128,512]{1,0:T(8,128)(2,1)S(1)} %shard_map.134), channel_id=1, source_target_pairs={{4,0},{12,4},{8,12},{0,8},{5,1},{13,5},{9,13},{1,9},{6,2},{14,6},{... | collective-permute-start | bytes 393224 | tf_op jit(solution)/shard_map/ppermute | solution.py:356
  50.3 7.1 %collective-permute-start.24 = (bf16[16,2048]{1,0:T(8,128)(2,1)S(1)}, bf16[16,2048]{1,0:T(8,128)(2,1)S(1)}, u32[]{:S(2)}, u32[]{:S(2)}) collective-permute-start(bf16[16,2048]{1,0:T(8,128)(2,1)S(1)} %broadcast_select_fusion), channel_id=1, source_target_pairs={{0,4},{4,12},{12,8},{8,0},{1,5},{5,13},{13,9},{9,1},{2,6},{6,14},{... | collective-permute-start | bytes 196616 | tf_op jit(solution)/shard_map/ppermute | solution.py:300
  50.7 1.3 %collective-permute-start.25 = (f32[128,64]{1,0:T(8,128)S(1)}, f32[128,64]{1,0:T(8,128)S(1)}, u32[]{:S(2)}, u32[]{:S(2)}) collective-permute-start(f32[128,64]{1,0:T(8,128)S(1)} %shard_map.132), channel_id=1, source_target_pairs={{0,1},{1,0},{2,3},{3,2},{4,5},{5,4},{6,7},{7,6},{8,9},{9,8},{10,11... | collective-permute-start | bytes 98312 | tf_op jit(solution)/shard_map/ppermute | solution.py:62
  52.0 16.0 %collective-permute-start.33 = (bf16[32,2048]{1,0:T(8,128)(2,1)S(1)}, bf16[32,2048]{1,0:T(8,128)(2,1)S(1)}, u32[]{:S(2)}, u32[]{:S(2)}) collective-permute-start(bf16[32,2048]{1,0:T(8,128)(2,1)S(1)} %pad_maximum_fusion.1), channel_id=1, source_target_pairs={{0,4},{4,12},{12,8},{8,0},{1,5},{5,13},{13,9},{9,1},{2,6},{6,14},{... | collective-permute-start | bytes 393224 | tf_op jit(solution)/shard_map/ppermute | solution.py:308
  54.3 6.3 %collective-permute-start.26 = (f32[128,64]{1,0:T(8,128)S(1)}, f32[128,64]{1,0:T(8,128)S(1)}, u32[]{:S(2)}, u32[]{:S(2)}) collective-permute-start(f32[128,64]{1,0:T(8,128)S(1)} %add.179), channel_id=1, source_target_pairs={{0,2},{1,3},{2,0},{3,1},{4,6},{5,7},{6,4},{7,5},{8,10},{9,11},{10,... | collective-permute-start | bytes 98312 | tf_op jit(solution)/shard_map/ppermute | solution.py:62
  57.4 10.6 %collective-permute-start.34 = (bf16[32,2048]{1,0:T(8,128)(2,1)S(1)}, bf16[32,2048]{1,0:T(8,128)(2,1)S(1)}, u32[]{:S(2)}, u32[]{:S(2)}) collective-permute-start(bf16[32,2048]{1,0:T(8,128)(2,1)S(1)} %pad_maximum_fusion.2), channel_id=1, source_target_pairs={{0,4},{4,12},{12,8},{8,0},{1,5},{5,13},{13,9},{9,1},{2,6},{6,14},{... | collective-permute-start | bytes 393224 | tf_op jit(solution)/shard_map/ppermute | solution.py:308
  57.5 7.9 %collective-permute-start.31 = (bf16[128,256]{1,0:T(8,128)(2,1)S(1)}, bf16[128,256]{1,0:T(8,128)(2,1)S(1)}, u32[]{:S(2)}, u32[]{:S(2)}) collective-permute-start(bf16[128,256]{1,0:T(8,128)(2,1)S(1)} %get-tuple-element.110.refs_20_), channel_id=1, source_target_pairs={{0,4},{4,12},{12,8},{8,0},{1,5},{5,13},{13,9},{9,1},{2,6},{6,14},{... | collective-permute-start | bytes 196616 | tf_op jit(solution)/shard_map/ppermute | solution.py:361
  59.9 5.5 %collective-permute-start.32 = (bf16[128,256]{1,0:T(8,128)(2,1)S(1)}, bf16[128,256]{1,0:T(8,128)(2,1)S(1)}, u32[]{:S(2)}, u32[]{:S(2)}) collective-permute-start(bf16[128,256]{1,0:T(8,128)(2,1)S(1)} %get-tuple-element.105.refs_26_), channel_id=1, source_target_pairs={{4,0},{12,4},{8,12},{0,8},{5,1},{13,5},{9,13},{1,9},{6,2},{14,6},{... | collective-permute-start | bytes 196616 | tf_op jit(solution)/shard_map/ppermute | solution.py:363
  68.4 1.2 %collective-permute-start.37 = (bf16[64,128]{1,0:T(8,128)(2,1)S(1)}, bf16[64,128]{1,0:T(8,128)(2,1)S(1)}, u32[]{:S(2)}, u32[]{:S(2)}) collective-permute-start(bf16[64,128]{1,0:T(8,128)(2,1)S(1)} %convert_element_type.26), channel_id=1, source_target_pairs={{0,1},{1,0},{2,3},{3,2},{4,5},{5,4},{6,7},{7,6},{8,9},{9,8},{10,11... | collective-permute-start | bytes 49160 | tf_op jit(solution)/shard_map/ppermute | solution.py:62
  69.7 4.5 %collective-permute-start.38 = (bf16[64,128]{1,0:T(8,128)(2,1)S(1)}, bf16[64,128]{1,0:T(8,128)(2,1)S(1)}, u32[]{:S(2)}, u32[]{:S(2)}) collective-permute-start(bf16[64,128]{1,0:T(8,128)(2,1)S(1)} %add_convert_fusion), channel_id=1, source_target_pairs={{0,2},{1,3},{2,0},{3,1},{4,6},{5,7},{6,4},{7,5},{8,10},{9,11},{10,... | collective-permute-start | bytes 49160 | tf_op jit(solution)/shard_map/ppermute | solution.py:62
  71.2 7.3 %collective-permute-start.35 = (bf16[32,2048]{1,0:T(8,128)(2,1)S(1)}, bf16[32,2048]{1,0:T(8,128)(2,1)S(1)}, u32[]{:S(2)}, u32[]{:S(2)}) collective-permute-start(bf16[32,2048]{1,0:T(8,128)(2,1)S(1)} %collective-permute-done.33.refs_0_), channel_id=1, source_target_pairs={{0,4},{4,12},{12,8},{8,0},{1,5},{5,13},{13,9},{9,1},{2,6},{6,14},{... | collective-permute-start | bytes 393224 | tf_op jit(solution)/shard_map/ppermute | solution.py:308
  72.3 7.8 %collective-permute-start.36 = (bf16[32,2048]{1,0:T(8,128)(2,1)S(1)}, bf16[32,2048]{1,0:T(8,128)(2,1)S(1)}, u32[]{:S(2)}, u32[]{:S(2)}) collective-permute-start(bf16[32,2048]{1,0:T(8,128)(2,1)S(1)} %collective-permute-done.34.refs_1_), channel_id=1, source_target_pairs={{0,4},{4,12},{12,8},{8,0},{1,5},{5,13},{13,9},{9,1},{2,6},{6,14},{... | collective-permute-start | bytes 393224 | tf_op jit(solution)/shard_map/ppermute | solution.py:308

commit v4 on v3

--- a/solution.py
+++ b/solution.py
@@ -16,6 +16,7 @@
 CHUNK_ROWS = 16
 LAG = 4
 JOINED = 2
+UP_BLOCKS = 4
 KERNEL_VMEM = 8 << 20
 
 
@@ -85,14 +86,14 @@
 SMEM = pl.BlockSpec(memory_space=pltpu.SMEM)
 
 
-def chunk_call(kernel, behind, candidates, chunks, operands, out_shape):
+def chunk_call(kernel, behind, candidates, chunks, operands, out_shape, scratch=()):
     names = sorted(chunks)
     rows, width = CHUNK_ROWS, chunks[names[0]].shape[1]
     number = len(candidates[0])
 
     def body(behind_ref, *refs):
         chunk_refs = dict(zip(names, refs))
-        weight_ref = refs[-1]
+        weight_ref = refs[len(names) + len(operands) + 1]
         for distance, held in enumerate(candidates):
 
             @pl.when(behind_ref[0] == distance)
@@ -100,14 +101,15 @@
                 for i, (name, row) in enumerate(held):
                     weight_ref[i * rows : (i + 1) * rows, :] = chunk_refs[name][row : row + rows]
 
-        kernel(weight_ref, *refs[len(names) : -1])
+        last = len(names) + len(operands) + 1
+        kernel(weight_ref, *refs[len(names) : last], *refs[last + 1 :])
 
     return pl.pallas_call(
         body,
-        out_shape=pltpu.VMEM(out_shape.shape, out_shape.dtype),
+        out_shape=out_shape if scratch else pltpu.VMEM(out_shape.shape, out_shape.dtype),
         in_specs=[SMEM] + [VMEM] * (len(names) + len(operands)),
-        out_specs=VMEM,
-        scratch_shapes=[pltpu.VMEM((number * rows, width), jnp.bfloat16)],
+        out_specs=pl.BlockSpec(memory_space=pltpu.HBM) if scratch else VMEM,
+        scratch_shapes=[pltpu.VMEM((number * rows, width), jnp.bfloat16), *scratch],
         compiler_params=pltpu.CompilerParams(vmem_limit_bytes=KERNEL_VMEM),
     )(
         behind,
@@ -182,13 +184,20 @@
     )
 
 
-def up_kernel(weight_ref, low_ref, out_ref):
-    out_ref[...] = lax.dot_general(
-        low_ref[...].astype(jnp.bfloat16),
-        weight_ref[...],
-        CONTRACT_FIRST,
-        preferred_element_type=jnp.float32,
-    ).astype(out_ref.dtype)
+def up_kernel(weight_ref, low_ref, out_hbm, rows_ref, sem):
+    low = low_ref[...].astype(jnp.bfloat16)
+    step = rows_ref.shape[1] // UP_BLOCKS
+    copies = []
+    for block in range(UP_BLOCKS):
+        lanes = pl.ds(block * step, step)
+        rows_ref[:, lanes] = lax.dot_general(
+            low, weight_ref[:, lanes], CONTRACT_FIRST, preferred_element_type=jnp.float32
+        ).astype(rows_ref.dtype)
+        copy = pltpu.make_async_copy(rows_ref.at[:, lanes], out_hbm.at[:, lanes], sem.at[block])
+        copy.start()
+        copies.append(copy)
+    for copy in copies:
+        copy.wait()
 
 
 def pair_kernel(weight_ref, low_ref, keys_ref, values_ref, tables_ref, out_ref):
@@ -213,16 +222,21 @@
     out_ref[:, width:] = values.astype(jnp.bfloat16)
 
 
-def attend_kernel(
-    group_size, block_count, weight_ref, low_ref, base_ref, tables_ref, hidden_ref, *refs
-):
+def query_kernel(weight_ref, low_ref, base_ref, tables_ref, out_ref):
+    low = low_ref[...].astype(jnp.bfloat16)
+    queries = base_ref[...].astype(jnp.float32) + jnp.dot(
+        low, weight_ref[...], preferred_element_type=jnp.float32
+    )
+    for lane in range(0, out_ref.shape[1], HEAD_SIZE):
+        out_ref[:, lane : lane + HEAD_SIZE] = rotate(
+            queries[:, lane : lane + HEAD_SIZE], tables_ref[...]
+        ).astype(jnp.bfloat16)
+
+
+def attend_kernel(group_size, block_count, queries_ref, hidden_ref, *refs):
     key_refs = refs[:block_count]
     value_refs = refs[block_count : 2 * block_count]
     out_ref = refs[-1]
-    low = low_ref[...].astype(jnp.bfloat16)
-    queries = base_ref[...].astype(jnp.float32) + jnp.dot(
-        low, weight_ref[...], preferred_element_type=jnp.float32
-    )
     group = None
     for lane in range(0, out_ref.shape[1], HEAD_SIZE):
         head = lane // HEAD_SIZE
@@ -231,7 +245,7 @@
             lanes = slice(group * HEAD_SIZE, (group + 1) * HEAD_SIZE)
             keys = jnp.concatenate([ref[:, lanes] for ref in key_refs], axis=0)
             values = jnp.concatenate([ref[:, lanes] for ref in value_refs], axis=0)
-        turned = rotate(queries[:, lane : lane + HEAD_SIZE], tables_ref[...]).astype(jnp.bfloat16)
+        turned = queries_ref[:, lane : lane + HEAD_SIZE]
         scores = lax.dot_general(
             keys, turned, CONTRACT_LAST, preferred_element_type=jnp.float32
         )
@@ -310,7 +324,7 @@
 
     distance = jnp.full((1,), behind, jnp.int32)
 
-    def on_chunks(kernel, first, number, operands, shape, dtype):
+    def on_chunks(kernel, first, number, operands, shape, dtype, scratch=()):
         chunks, candidates = {}, []
         for hop in range(-1, count - 1):
             held = []
@@ -327,7 +341,13 @@
                 held.append((key, row))
             candidates.append(held)
         return chunk_call(
-            kernel, distance, candidates, chunks, operands, jax.ShapeDtypeStruct(shape, dtype)
+            kernel,
+            distance,
+            candidates,
+            chunks,
+            operands,
+            jax.ShapeDtypeStruct(shape, dtype),
+            scratch,
         )
 
     local_rows = hidden.shape[0]
@@ -377,19 +397,37 @@
     hide = jnp.where(key_pos[:, None] <= query_pos[None, :], 0.0, NEG_BIG)
     local_heads = base_query_rows.shape[1] // HEAD_SIZE
     group_size = local_heads // (pair_width // HEAD_SIZE)
-    attended = on_chunks(
-        functools.partial(attend_kernel, group_size, len(offsets)),
+    queries = on_chunks(
+        query_kernel,
         3 * per + 1,
         per,
-        [query_sums[-1], base_query_rows, tables, hide]
-        + [key_blocks[o] for o in offsets]
-        + [value_blocks[o] for o in offsets],
+        [query_sums[-1], base_query_rows, tables],
         base_query_rows.shape,
         jnp.bfloat16,
     )
+    operands = [queries, hide]
+    operands += [key_blocks[o] for o in offsets] + [value_blocks[o] for o in offsets]
+    attended = pl.pallas_call(
+        functools.partial(attend_kernel, group_size, len(offsets)),
+        out_shape=pltpu.VMEM(queries.shape, jnp.bfloat16),
+        in_specs=[VMEM] * len(operands),
+        out_specs=VMEM,
+        compiler_params=pltpu.CompilerParams(vmem_limit_bytes=KERNEL_VMEM),
+    )(*[pltpu.with_memory_space_constraint(x, pltpu.VMEM) for x in operands])
     part = on_chunks(out_low_kernel, 4 * per + 1, per, [attended], (rank, local_rows), jnp.float32)
     out_low = doubling_sums(part, "tp", jnp.bfloat16)[-1]
-    adapted = on_chunks(up_kernel, 5 * per + 1, per, [out_low], attended.shape, jnp.bfloat16)
+    adapted = on_chunks(
+        up_kernel,
+        5 * per + 1,
+        per,
+        [out_low],
+        attended.shape,
+        jnp.bfloat16,
+        (
+            pltpu.VMEM(attended.shape, jnp.bfloat16),
+            pltpu.SemaphoreType.DMA((UP_BLOCKS,)),
+        ),
+    )
     return (attended, adapted)
 
 

time: 81.5 us -> 80.1 us (0.983)
  waiting for transfers between devices: 18.3 us -> 17.2 us
  Pallas kernels: 6.45 us -> 7.37 us
    ppermute x1, waiting for transfers between devices: 4.84 us -> 1.08 us  [shards(): far = lax.ppermute(ahead[:, :pair_width], 'ctx', forward)]
    ppermute x1, waiting for transfers between devices: 0.01 us -> 3.45 us  [shards(): far = lax.ppermute(back[:, pair_width:], 'ctx', backward)]
    ppermute x1, starting transfers between devices: 2.38 us -> 0.06 us  [shards(): far = lax.ppermute(ahead[:, :pair_width], 'ctx', forward)]
    ppermute x21, starting transfers between devices: 30 us -> 32.1 us  [shards(): arrived.append(lax.ppermute(moving, 'ctx', pairs))]
    ppermute x1, starting transfers between devices: 0.65 us -> 2.7 us  [shards(): far = lax.ppermute(back[:, pair_width:], 'ctx', backward)]
    ppermute x4, waiting for transfers between devices: 1.92 us -> 0.27 us  [shards(): arrived.append(lax.ppermute(own[turn], 'ctx', pairs))]
    ppermute x4, starting transfers between devices: 4.42 us -> 3.06 us  [shards(): late.append(lax.ppermute(moving, 'ctx', pairs))]
    ppermute x21, waiting for transfers between devices: 1.75 us -> 2.78 us  [shards(): arrived.append(lax.ppermute(moving, 'ctx', pairs))]
  transfers between devices with their start and end apart: 39 -> 39, of which waited for: 9 -> 11; matrix products, arithmetic and copies ran while one was open for 2% -> 2% of each run, Pallas kernels for 4% -> 5%
where the time goes in v4:
time: 80.1 us; the launch traced here: 79.9 us
  starting transfers between devices  51 us (64%)
  waiting for transfers between devices  17.2 us (21%)
  Pallas kernels  7.37 us (9%)
  between operations  1.73 us (2%)
  local copies, waits for them, and re-layouts  1.5 us (2%)
  other arithmetic  1.05 us (1%)
    ppermute x21, starting transfers between devices, shards(): arrived.append(lax.ppermute(moving, 'ctx', pairs))  32.1 us
    ppermute x4, starting transfers between devices, shards(): arrived.append(lax.ppermute(own[turn], 'ctx', pairs))  6.21 us
    ppermute x4, waiting for transfers between devices, shards(): late.append(lax.ppermute(moving, 'ctx', pairs))  5.85 us
    ppermute x6, starting transfers between devices, doubling_sums(): other = lax.ppermute(sent, axis, pairs)  4.82 us
    ppermute x6, waiting for transfers between devices, doubling_sums(): other = lax.ppermute(sent, axis, pairs)  3.8 us
    ppermute x1, waiting for transfers between devices, shards(): far = lax.ppermute(back[:, pair_width:], 'ctx', backward)  3.45 us
    ppermute x4, starting transfers between devices, shards(): late.append(lax.ppermute(moving, 'ctx', pairs))  3.06 us
    pallas_call x6, Pallas kernels, chunk_call(): pl.pallas_call(body, out_shape=out_shape if scratch else pltpu.VMEM(out_s...  2.91 us
  transfers between devices with their start and end apart: 39, of which 11 were waited for; matrix products, arithmetic and copies ran while one was open for 2% of the time, Pallas kernels for 5%

profile of v4, /device:TPU:0, one launch (start us, length us, event | category | flops | bytes accessed | tf_op | source)
XLA Modules:
  0.0 79.9 jit_solution(15792089304965734525)
XLA Ops:
  1.3 0.6 copy-done.4
  1.9 2.3 %shard_map.131 = (bf16[16,2048]{1,0:T(8,128)(2,1)S(1)}, bf16[16,2048]{1,0:T(8,128)(2,1)S(1)}, bf16[16,2048]{1,0:T(8,128)(2,1)S(1)}, bf16[16,2048]{1,0:T(8,128)(2...) custom-call(s32[1]{0:T(128)S(6)} %copy.16.publisher_ref, ...), custom_call_target="tpu_custom_call" | custom-call | tf_op jit(solution)/shard_map/pallas_call | solution.py:158
  4.2 3.1 %collective-permute-start.1 = (bf16[16,2048]{1,0:T(8,128)(2,1)S(1)}, bf16[16,2048]{1,0:T(8,128)(2,1)S(1)}, u32[]{:S(2)}, u32[]{:S(2)}) collective-permute-start(bf16[16,2048]{1,0:T(8,128)(2,1)S(1)} %get-tuple-element.50.refs_0_), channel_id=1, source_target_pairs={{0,4},{4,12},{12,8},{8,0},{1,5},{5,13},{13,9},{9,1},{2,6},{6,14},{... | collective-permute-start | bytes 196616 | tf_op jit(solution)/shard_map/ppermute | solution.py:306
  7.3 2.6 %collective-permute-start = (bf16[16,2048]{1,0:T(8,128)(2,1)S(1)}, bf16[16,2048]{1,0:T(8,128)(2,1)S(1)}, u32[]{:S(2)}, u32[]{:S(2)}) collective-permute-start(bf16[16,2048]{1,0:T(8,128)(2,1)S(1)} %get-tuple-element.51.refs_1_), channel_id=1, source_target_pairs={{0,4},{4,12},{12,8},{8,0},{1,5},{5,13},{13,9},{9,1},{2,6},{6,14},{... | collective-permute-start | bytes 196616 | tf_op jit(solution)/shard_map/ppermute | solution.py:306
  9.9 0.4 collective-permute-start.5
  10.8 1.7 %collective-permute-start.3 = (bf16[16,2048]{1,0:T(8,128)(2,1)S(1)}, bf16[16,2048]{1,0:T(8,128)(2,1)S(1)}, u32[]{:S(2)}, u32[]{:S(2)}) collective-permute-start(bf16[16,2048]{1,0:T(8,128)(2,1)S(1)} %broadcast_select_fusion.20), channel_id=1, source_target_pairs={{0,4},{4,12},{12,8},{8,0},{1,5},{5,13},{13,9},{9,1},{2,6},{6,14},{... | collective-permute-start | bytes 196616 | tf_op jit(solution)/shard_map/ppermute | solution.py:314
  12.5 3.4 %collective-permute-start.2 = (bf16[16,2048]{1,0:T(8,128)(2,1)S(1)}, bf16[16,2048]{1,0:T(8,128)(2,1)S(1)}, u32[]{:S(2)}, u32[]{:S(2)}) collective-permute-start(bf16[16,2048]{1,0:T(8,128)(2,1)S(1)} %broadcast_select_fusion.19), channel_id=1, source_target_pairs={{0,4},{4,12},{12,8},{8,0},{1,5},{5,13},{13,9},{9,1},{2,6},{6,14},{... | collective-permute-start | bytes 196616 | tf_op jit(solution)/shard_map/ppermute | solution.py:314
  15.9 1.4 %collective-permute-start.9 = (bf16[16,2048]{1,0:T(8,128)(2,1)S(1)}, bf16[16,2048]{1,0:T(8,128)(2,1)S(1)}, u32[]{:S(2)}, u32[]{:S(2)}) collective-permute-start(bf16[16,2048]{1,0:T(8,128)(2,1)S(1)} %broadcast_select_fusion.18), channel_id=1, source_target_pairs={{0,4},{4,12},{12,8},{8,0},{1,5},{5,13},{13,9},{9,1},{2,6},{6,14},{... | collective-permute-start | bytes 196616 | tf_op jit(solution)/shard_map/ppermute | solution.py:314
  17.3 1.4 %collective-permute-start.8 = (bf16[16,2048]{1,0:T(8,128)(2,1)S(1)}, bf16[16,2048]{1,0:T(8,128)(2,1)S(1)}, u32[]{:S(2)}, u32[]{:S(2)}) collective-permute-start(bf16[16,2048]{1,0:T(8,128)(2,1)S(1)} %broadcast_select_fusion.17), channel_id=1, source_target_pairs={{0,4},{4,12},{12,8},{8,0},{1,5},{5,13},{13,9},{9,1},{2,6},{6,14},{... | collective-permute-start | bytes 196616 | tf_op jit(solution)/shard_map/ppermute | solution.py:314
  18.7 1.4 %collective-permute-start.7 = (bf16[16,2048]{1,0:T(8,128)(2,1)S(1)}, bf16[16,2048]{1,0:T(8,128)(2,1)S(1)}, u32[]{:S(2)}, u32[]{:S(2)}) collective-permute-start(bf16[16,2048]{1,0:T(8,128)(2,1)S(1)} %broadcast_select_fusion.16), channel_id=1, source_target_pairs={{0,4},{4,12},{12,8},{8,0},{1,5},{5,13},{13,9},{9,1},{2,6},{6,14},{... | collective-permute-start | bytes 196616 | tf_op jit(solution)/shard_map/ppermute | solution.py:314
  20.1 1.7 %collective-permute-start.6 = (bf16[16,2048]{1,0:T(8,128)(2,1)S(1)}, bf16[16,2048]{1,0:T(8,128)(2,1)S(1)}, u32[]{:S(2)}, u32[]{:S(2)}) collective-permute-start(bf16[16,2048]{1,0:T(8,128)(2,1)S(1)} %broadcast_select_fusion.15), channel_id=1, source_target_pairs={{0,4},{4,12},{12,8},{8,0},{1,5},{5,13},{13,9},{9,1},{2,6},{6,14},{... | collective-permute-start | bytes 196616 | tf_op jit(solution)/shard_map/ppermute | solution.py:314
  21.9 1.4 %collective-permute-start.11 = (bf16[16,2048]{1,0:T(8,128)(2,1)S(1)}, bf16[16,2048]{1,0:T(8,128)(2,1)S(1)}, u32[]{:S(2)}, u32[]{:S(2)}) collective-permute-start(bf16[16,2048]{1,0:T(8,128)(2,1)S(1)} %broadcast_select_fusion.14), channel_id=1, source_target_pairs={{0,4},{4,12},{12,8},{8,0},{1,5},{5,13},{13,9},{9,1},{2,6},{6,14},{... | collective-permute-start | bytes 196616 | tf_op jit(solution)/shard_map/ppermute | solution.py:314
  23.3 1.4 %collective-permute-start.13 = (bf16[16,2048]{1,0:T(8,128)(2,1)S(1)}, bf16[16,2048]{1,0:T(8,128)(2,1)S(1)}, u32[]{:S(2)}, u32[]{:S(2)}) collective-permute-start(bf16[16,2048]{1,0:T(8,128)(2,1)S(1)} %broadcast_select_fusion.13), channel_id=1, source_target_pairs={{0,4},{4,12},{12,8},{8,0},{1,5},{5,13},{13,9},{9,1},{2,6},{6,14},{... | collective-permute-start | bytes 196616 | tf_op jit(solution)/shard_map/ppermute | solution.py:314
  24.7 1.4 %collective-permute-start.15 = (bf16[16,2048]{1,0:T(8,128)(2,1)S(1)}, bf16[16,2048]{1,0:T(8,128)(2,1)S(1)}, u32[]{:S(2)}, u32[]{:S(2)}) collective-permute-start(bf16[16,2048]{1,0:T(8,128)(2,1)S(1)} %broadcast_select_fusion.12), channel_id=1, source_target_pairs={{0,4},{4,12},{12,8},{8,0},{1,5},{5,13},{13,9},{9,1},{2,6},{6,14},{... | collective-permute-start | bytes 196616 | tf_op jit(solution)/shard_map/ppermute | solution.py:314
  26.1 1.7 %collective-permute-start.10 = (bf16[16,2048]{1,0:T(8,128)(2,1)S(1)}, bf16[16,2048]{1,0:T(8,128)(2,1)S(1)}, u32[]{:S(2)}, u32[]{:S(2)}) collective-permute-start(bf16[16,2048]{1,0:T(8,128)(2,1)S(1)} %broadcast_select_fusion.11), channel_id=1, source_target_pairs={{0,4},{4,12},{12,8},{8,0},{1,5},{5,13},{13,9},{9,1},{2,6},{6,14},{... | collective-permute-start | bytes 196616 | tf_op jit(solution)/shard_map/ppermute | solution.py:314
  27.9 1.4 %collective-permute-start.12 = (bf16[16,2048]{1,0:T(8,128)(2,1)S(1)}, bf16[16,2048]{1,0:T(8,128)(2,1)S(1)}, u32[]{:S(2)}, u32[]{:S(2)}) collective-permute-start(bf16[16,2048]{1,0:T(8,128)(2,1)S(1)} %broadcast_select_fusion.10), channel_id=1, source_target_pairs={{0,4},{4,12},{12,8},{8,0},{1,5},{5,13},{13,9},{9,1},{2,6},{6,14},{... | collective-permute-start | bytes 196616 | tf_op jit(solution)/shard_map/ppermute | solution.py:314
  29.3 1.4 %collective-permute-start.14 = (bf16[16,2048]{1,0:T(8,128)(2,1)S(1)}, bf16[16,2048]{1,0:T(8,128)(2,1)S(1)}, u32[]{:S(2)}, u32[]{:S(2)}) collective-permute-start(bf16[16,2048]{1,0:T(8,128)(2,1)S(1)} %broadcast_select_fusion.9), channel_id=1, source_target_pairs={{0,4},{4,12},{12,8},{8,0},{1,5},{5,13},{13,9},{9,1},{2,6},{6,14},{... | collective-permute-start | bytes 196616 | tf_op jit(solution)/shard_map/ppermute | solution.py:314
  31.4 1.3 %collective-permute-start.16 = (bf16[16,2048]{1,0:T(8,128)(2,1)S(1)}, bf16[16,2048]{1,0:T(8,128)(2,1)S(1)}, u32[]{:S(2)}, u32[]{:S(2)}) collective-permute-start(bf16[16,2048]{1,0:T(8,128)(2,1)S(1)} %broadcast_select_fusion.8), channel_id=1, source_target_pairs={{0,4},{4,12},{12,8},{8,0},{1,5},{5,13},{13,9},{9,1},{2,6},{6,14},{... | collective-permute-start | bytes 196616 | tf_op jit(solution)/shard_map/ppermute | solution.py:314
  32.6 1.1 %collective-permute-start.17 = (bf16[16,2048]{1,0:T(8,128)(2,1)S(1)}, bf16[16,2048]{1,0:T(8,128)(2,1)S(1)}, u32[]{:S(2)}, u32[]{:S(2)}) collective-permute-start(bf16[16,2048]{1,0:T(8,128)(2,1)S(1)} %broadcast_select_fusion.7), channel_id=1, source_target_pairs={{0,4},{4,12},{12,8},{8,0},{1,5},{5,13},{13,9},{9,1},{2,6},{6,14},{... | collective-permute-start | bytes 196616 | tf_op jit(solution)/shard_map/ppermute | solution.py:314
  33.8 1.3 %collective-permute-start.18 = (bf16[16,2048]{1,0:T(8,128)(2,1)S(1)}, bf16[16,2048]{1,0:T(8,128)(2,1)S(1)}, u32[]{:S(2)}, u32[]{:S(2)}) collective-permute-start(bf16[16,2048]{1,0:T(8,128)(2,1)S(1)} %broadcast_select_fusion.6), channel_id=1, source_target_pairs={{0,4},{4,12},{12,8},{8,0},{1,5},{5,13},{13,9},{9,1},{2,6},{6,14},{... | collective-permute-start | bytes 196616 | tf_op jit(solution)/shard_map/ppermute | solution.py:314
  35.2 1.4 %collective-permute-start.19 = (bf16[16,2048]{1,0:T(8,128)(2,1)S(1)}, bf16[16,2048]{1,0:T(8,128)(2,1)S(1)}, u32[]{:S(2)}, u32[]{:S(2)}) collective-permute-start(bf16[16,2048]{1,0:T(8,128)(2,1)S(1)} %broadcast_select_fusion.5), channel_id=1, source_target_pairs={{0,4},{4,12},{12,8},{8,0},{1,5},{5,13},{13,9},{9,1},{2,6},{6,14},{... | collective-permute-start | bytes 196616 | tf_op jit(solution)/shard_map/ppermute | solution.py:314
  36.6 0.3 shard_map.134
  37.1 1.4 %collective-permute-start.20 = (bf16[16,2048]{1,0:T(8,128)(2,1)S(1)}, bf16[16,2048]{1,0:T(8,128)(2,1)S(1)}, u32[]{:S(2)}, u32[]{:S(2)}) collective-permute-start(bf16[16,2048]{1,0:T(8,128)(2,1)S(1)} %broadcast_select_fusion.4), channel_id=1, source_target_pairs={{0,4},{4,12},{12,8},{8,0},{1,5},{5,13},{13,9},{9,1},{2,6},{6,14},{... | collective-permute-start | bytes 196616 | tf_op jit(solution)/shard_map/ppermute | solution.py:314
  38.5 1.0 %collective-permute-start.21 = (bf16[16,2048]{1,0:T(8,128)(2,1)S(1)}, bf16[16,2048]{1,0:T(8,128)(2,1)S(1)}, u32[]{:S(2)}, u32[]{:S(2)}) collective-permute-start(bf16[16,2048]{1,0:T(8,128)(2,1)S(1)} %broadcast_select_fusion.3), channel_id=1, source_target_pairs={{0,4},{4,12},{12,8},{8,0},{1,5},{5,13},{13,9},{9,1},{2,6},{6,14},{... | collective-permute-start | bytes 196616 | tf_op jit(solution)/shard_map/ppermute | solution.py:314
  39.5 1.4 %collective-permute-start.22 = (bf16[16,2048]{1,0:T(8,128)(2,1)S(1)}, bf16[16,2048]{1,0:T(8,128)(2,1)S(1)}, u32[]{:S(2)}, u32[]{:S(2)}) collective-permute-start(bf16[16,2048]{1,0:T(8,128)(2,1)S(1)} %broadcast_select_fusion.2), channel_id=1, source_target_pairs={{0,4},{4,12},{12,8},{8,0},{1,5},{5,13},{13,9},{9,1},{2,6},{6,14},{... | collective-permute-start | bytes 196616 | tf_op jit(solution)/shard_map/ppermute | solution.py:314
  40.9 1.6 %collective-permute-start.28 = (f32[128,128]{1,0:T(8,128)S(1)}, f32[128,128]{1,0:T(8,128)S(1)}, u32[]{:S(2)}, u32[]{:S(2)}) collective-permute-start(f32[128,128]{1,0:T(8,128)S(1)} %add.208), channel_id=1, source_target_pairs={{0,2},{1,3},{2,0},{3,1},{4,6},{5,7},{6,4},{7,5},{8,10},{9,11},{10,... | collective-permute-start | bytes 196616 | tf_op jit(solution)/shard_map/ppermute | solution.py:63
  42.5 1.4 %collective-permute-start.23 = (bf16[16,2048]{1,0:T(8,128)(2,1)S(1)}, bf16[16,2048]{1,0:T(8,128)(2,1)S(1)}, u32[]{:S(2)}, u32[]{:S(2)}) collective-permute-start(bf16[16,2048]{1,0:T(8,128)(2,1)S(1)} %broadcast_select_fusion.1), channel_id=1, source_target_pairs={{0,4},{4,12},{12,8},{8,0},{1,5},{5,13},{13,9},{9,1},{2,6},{6,14},{... | collective-permute-start | bytes 196616 | tf_op jit(solution)/shard_map/ppermute | solution.py:314
  43.9 1.4 %collective-permute-done.28 = f32[128,128]{1,0:T(8,128)S(1)} collective-permute-done((f32[128,128]{1,0:T(8,128)S(1)}, f32[128,128]{1,0:T(8,128)S(1)}, u32[]{:S(2)}, u32[]{:S(2)}) %collective-permute-start.28) | collective-permute-done | bytes 65568 | tf_op jit(solution)/shard_map/ppermute | solution.py:63
  45.6 1.6 %collective-permute-start.30 = (bf16[128,512]{1,0:T(8,128)(2,1)S(1)}, bf16[128,512]{1,0:T(8,128)(2,1)S(1)}, u32[]{:S(2)}, u32[]{:S(2)}) collective-permute-start(bf16[128,512]{1,0:T(8,128)(2,1)S(1)} %shard_map.135), channel_id=1, source_target_pairs={{4,0},{12,4},{8,12},{0,8},{5,1},{13,5},{9,13},{1,9},{6,2},{14,6},{... | collective-permute-start | bytes 393224 | tf_op jit(solution)/shard_map/ppermute | solution.py:376
  47.2 0.5 collective-permute-start.29
  48.0 2.3 %collective-permute-start.24 = (bf16[16,2048]{1,0:T(8,128)(2,1)S(1)}, bf16[16,2048]{1,0:T(8,128)(2,1)S(1)}, u32[]{:S(2)}, u32[]{:S(2)}) collective-permute-start(bf16[16,2048]{1,0:T(8,128)(2,1)S(1)} %broadcast_select_fusion), channel_id=1, source_target_pairs={{0,4},{4,12},{12,8},{8,0},{1,5},{5,13},{13,9},{9,1},{2,6},{6,14},{... | collective-permute-start | bytes 196616 | tf_op jit(solution)/shard_map/ppermute | solution.py:314
  50.3 1.2 %collective-permute-done.25 = f32[128,64]{1,0:T(8,128)S(1)} collective-permute-done((f32[128,64]{1,0:T(8,128)S(1)}, f32[128,64]{1,0:T(8,128)S(1)}, u32[]{:S(2)}, u32[]{:S(2)}) %collective-permute-start.25) | collective-permute-done | bytes 32800 | tf_op jit(solution)/shard_map/ppermute | solution.py:63
  51.6 0.4 collective-permute-start.33
  52.0 1.6 %collective-permute-start.26 = (f32[128,64]{1,0:T(8,128)S(1)}, f32[128,64]{1,0:T(8,128)S(1)}, u32[]{:S(2)}, u32[]{:S(2)}) collective-permute-start(f32[128,64]{1,0:T(8,128)S(1)} %add.179), channel_id=1, source_target_pairs={{0,2},{1,3},{2,0},{3,1},{4,6},{5,7},{6,4},{7,5},{8,10},{9,11},{10,... | collective-permute-start | bytes 98312 | tf_op jit(solution)/shard_map/ppermute | solution.py:63
  53.6 2.6 %collective-permute-done.24.refs_15_.refs_13_.refs_11_ = bf16[16,2048]{1,0:T(8,128)(2,1)S(1)} collective-permute-done((bf16[16,2048]{1,0:T(8,128)(2,1)S(1)}, bf16[16,2048]{1,0:T(8,128)(2,1)S(1)}, u32[]{:S(2)}, u32[]{:S(2)}) %collective-permute-start.24) | collective-permute-done | bytes 65568 | tf_op jit(solution)/shard_map/ppermute | solution.py:314
  56.5 2.7 %collective-permute-start.32 = (bf16[128,256]{1,0:T(8,128)(2,1)S(1)}, bf16[128,256]{1,0:T(8,128)(2,1)S(1)}, u32[]{:S(2)}, u32[]{:S(2)}) collective-permute-start(bf16[128,256]{1,0:T(8,128)(2,1)S(1)} %get-tuple-element.105.refs_6_), channel_id=1, source_target_pairs={{4,0},{12,4},{8,12},{0,8},{5,1},{13,5},{9,13},{1,9},{6,2},{14,6},{... | collective-permute-start | bytes 196616 | tf_op jit(solution)/shard_map/ppermute | solution.py:383
  59.4 0.6 shard_map.133.queries_ref
  59.9 3.4 %collective-permute-done.32.refs_7_ = bf16[128,256]{1,0:T(8,128)(2,1)S(1)} collective-permute-done((bf16[128,256]{1,0:T(8,128)(2,1)S(1)}, bf16[128,256]{1,0:T(8,128)(2,1)S(1)}, u32[]{:S(2)}, u32[]{:S(2)}) %collective-permute-start.32) | collective-permute-done | bytes 65568 | tf_op jit(solution)/shard_map/ppermute | solution.py:383
  63.4 1.1 %collective-permute-done.31.refs_3_ = bf16[128,256]{1,0:T(8,128)(2,1)S(1)} collective-permute-done((bf16[128,256]{1,0:T(8,128)(2,1)S(1)}, bf16[128,256]{1,0:T(8,128)(2,1)S(1)}, u32[]{:S(2)}, u32[]{:S(2)}) %collective-permute-start.31) | collective-permute-done | bytes 65568 | tf_op jit(solution)/shard_map/ppermute | solution.py:381
  64.5 2.2 %shard_map.136.refs_14_ = bf16[128,2048]{1,0:T(8,128)(2,1)S(1)} custom-call(bf16[128,2048]{1,0:T(8,128)(2,1)S(1)} %shard_map.133.queries_ref, f32[512,128]{1,0:T(8,128)S(1)} %compare_select_fusion.hidden_ref, bf16[128,256]{1,0:T(8,128)(2,1)S(1)} %get-tuple-element.110.refs_0_, bf16[128,256]{1,0:T(8,128)(2,1)S(1)} %get-tuple-element.108.refs_1_, ...), custom_call_target="tpu_custom_call" | custom-call | tf_op jit(solution)/shard_map/pallas_call | solution.py:410
  66.7 0.3 shard_map.137
  67.1 1.2 %collective-permute-done.37 = bf16[64,128]{1,0:T(8,128)(2,1)S(1)} collective-permute-done((bf16[64,128]{1,0:T(8,128)(2,1)S(1)}, bf16[64,128]{1,0:T(8,128)(2,1)S(1)}, u32[]{:S(2)}, u32[]{:S(2)}) %collective-permute-start.37) | collective-permute-done | bytes 16416 | tf_op jit(solution)/shard_map/ppermute | solution.py:63
  68.3 1.6 %collective-permute-start.38 = (bf16[64,128]{1,0:T(8,128)(2,1)S(1)}, bf16[64,128]{1,0:T(8,128)(2,1)S(1)}, u32[]{:S(2)}, u32[]{:S(2)}) collective-permute-start(bf16[64,128]{1,0:T(8,128)(2,1)S(1)} %add_convert_fusion), channel_id=1, source_target_pairs={{0,2},{1,3},{2,0},{3,1},{4,6},{5,7},{6,4},{7,5},{8,10},{9,11},{10,... | collective-permute-start | bytes 49160 | tf_op jit(solution)/shard_map/ppermute | solution.py:63
  69.9 0.8 copy.15
  70.7 2.3 %collective-permute-start.36 = (bf16[32,2048]{1,0:T(8,128)(2,1)S(1)}, bf16[32,2048]{1,0:T(8,128)(2,1)S(1)}, u32[]{:S(2)}, u32[]{:S(2)}) collective-permute-start(bf16[32,2048]{1,0:T(8,128)(2,1)S(1)} %collective-permute-done.34.refs_1_), channel_id=1, source_target_pairs={{0,4},{4,12},{12,8},{8,0},{1,5},{5,13},{13,9},{9,1},{2,6},{6,14},{... | collective-permute-start | bytes 393224 | tf_op jit(solution)/shard_map/ppermute | solution.py:322
  73.0 4.2 %collective-permute-done.35.refs_2_ = bf16[32,2048]{1,0:T(8,128)(2,1)S(1)} collective-permute-done((bf16[32,2048]{1,0:T(8,128)(2,1)S(1)}, bf16[32,2048]{1,0:T(8,128)(2,1)S(1)}, u32[]{:S(2)}, u32[]{:S(2)}) %collective-permute-start.35) | collective-permute-done | bytes 131104 | tf_op jit(solution)/shard_map/ppermute | solution.py:322
  77.2 1.7 %collective-permute-done.36.refs_3_ = bf16[32,2048]{1,0:T(8,128)(2,1)S(1)} collective-permute-done((bf16[32,2048]{1,0:T(8,128)(2,1)S(1)}, bf16[32,2048]{1,0:T(8,128)(2,1)S(1)}, u32[]{:S(2)}, u32[]{:S(2)}) %collective-permute-start.36) | collective-permute-done | bytes 131104 | tf_op jit(solution)/shard_map/ppermute | solution.py:322
  78.8 1.1 %shard_map.138 = bf16[128,2048]{1,0:T(8,128)(2,1)} custom-call(s32[1]{0:T(128)} %bitcast.1.behind_ref, bf16[32,2048]{1,0:T(8,128)(2,1)S(1)} %collective-permute-done.33.refs_0_, bf16[32,2048]{1,0:T(8,128)(2,1)S(1)} %collective-permute-done.34.refs_1_, bf16[32,2048]{1,0:T(8,128)(2,1)S(1)} %collective-permute-done.35.refs_2_, ...), custom_call_target="tpu_custom_call" | custom-call | tf_op jit(solution)/shard_map/pallas_call | solution.py:107
  (98 shorter events, 2.8 us)
Async XLA Ops:
  1.3 0.7 copy-start.4
  1.9 25.8 %copy-start.5 = (s32[8]{0:T(128)S(1)}, s32[8]{0:T(128)}, u32[]{:S(2)}) copy-start(s32[8]{0:T(128)} %param.16) | copy-start | bytes 100
  4.2 32.4 %copy-start = (bf16[128,2048]{1,0:T(8,128)(2,1)S(1)}, bf16[128,2048]{1,0:T(8,128)(2,1)}, u32[]{:S(2)}) copy-start(bf16[128,2048]{1,0:T(8,128)(2,1)} %refs_24_.1) | copy-start | bytes 1572868
  4.2 6.6 %collective-permute-start.1 = (bf16[16,2048]{1,0:T(8,128)(2,1)S(1)}, bf16[16,2048]{1,0:T(8,128)(2,1)S(1)}, u32[]{:S(2)}, u32[]{:S(2)}) collective-permute-start(bf16[16,2048]{1,0:T(8,128)(2,1)S(1)} %get-tuple-element.50.refs_0_), channel_id=1, source_target_pairs={{0,4},{4,12},{12,8},{8,0},{1,5},{5,13},{13,9},{9,1},{2,6},{6,14},{... | collective-permute-start | bytes 196616 | tf_op jit(solution)/shard_map/ppermute | solution.py:306
  7.3 5.2 %collective-permute-start = (bf16[16,2048]{1,0:T(8,128)(2,1)S(1)}, bf16[16,2048]{1,0:T(8,128)(2,1)S(1)}, u32[]{:S(2)}, u32[]{:S(2)}) collective-permute-start(bf16[16,2048]{1,0:T(8,128)(2,1)S(1)} %get-tuple-element.51.refs_1_), channel_id=1, source_target_pairs={{0,4},{4,12},{12,8},{8,0},{1,5},{5,13},{13,9},{9,1},{2,6},{6,14},{... | collective-permute-start | bytes 196616 | tf_op jit(solution)/shard_map/ppermute | solution.py:306
  9.9 6.0 %collective-permute-start.5 = (bf16[16,2048]{1,0:T(8,128)(2,1)S(1)}, bf16[16,2048]{1,0:T(8,128)(2,1)S(1)}, u32[]{:S(2)}, u32[]{:S(2)}) collective-permute-start(bf16[16,2048]{1,0:T(8,128)(2,1)S(1)} %get-tuple-element.52.refs_2_), channel_id=1, source_target_pairs={{0,4},{4,12},{12,8},{8,0},{1,5},{5,13},{13,9},{9,1},{2,6},{6,14},{... | collective-permute-start | bytes 196616 | tf_op jit(solution)/shard_map/ppermute | solution.py:306
  10.4 7.0 %collective-permute-start.4 = (bf16[16,2048]{1,0:T(8,128)(2,1)S(1)}, bf16[16,2048]{1,0:T(8,128)(2,1)S(1)}, u32[]{:S(2)}, u32[]{:S(2)}) collective-permute-start(bf16[16,2048]{1,0:T(8,128)(2,1)S(1)} %get-tuple-element.53.refs_3_), channel_id=1, source_target_pairs={{0,4},{4,12},{12,8},{8,0},{1,5},{5,13},{13,9},{9,1},{2,6},{6,14},{... | collective-permute-start | bytes 196616 | tf_op jit(solution)/shard_map/ppermute | solution.py:306
  10.8 7.9 %collective-permute-start.3 = (bf16[16,2048]{1,0:T(8,128)(2,1)S(1)}, bf16[16,2048]{1,0:T(8,128)(2,1)S(1)}, u32[]{:S(2)}, u32[]{:S(2)}) collective-permute-start(bf16[16,2048]{1,0:T(8,128)(2,1)S(1)} %broadcast_select_fusion.20), channel_id=1, source_target_pairs={{0,4},{4,12},{12,8},{8,0},{1,5},{5,13},{13,9},{9,1},{2,6},{6,14},{... | collective-permute-start | bytes 196616 | tf_op jit(solution)/shard_map/ppermute | solution.py:314
  12.5 7.6 %collective-permute-start.2 = (bf16[16,2048]{1,0:T(8,128)(2,1)S(1)}, bf16[16,2048]{1,0:T(8,128)(2,1)S(1)}, u32[]{:S(2)}, u32[]{:S(2)}) collective-permute-start(bf16[16,2048]{1,0:T(8,128)(2,1)S(1)} %broadcast_select_fusion.19), channel_id=1, source_target_pairs={{0,4},{4,12},{12,8},{8,0},{1,5},{5,13},{13,9},{9,1},{2,6},{6,14},{... | collective-permute-start | bytes 196616 | tf_op jit(solution)/shard_map/ppermute | solution.py:314
  15.9 5.9 %collective-permute-start.9 = (bf16[16,2048]{1,0:T(8,128)(2,1)S(1)}, bf16[16,2048]{1,0:T(8,128)(2,1)S(1)}, u32[]{:S(2)}, u32[]{:S(2)}) collective-permute-start(bf16[16,2048]{1,0:T(8,128)(2,1)S(1)} %broadcast_select_fusion.18), channel_id=1, source_target_pairs={{0,4},{4,12},{12,8},{8,0},{1,5},{5,13},{13,9},{9,1},{2,6},{6,14},{... | collective-permute-start | bytes 196616 | tf_op jit(solution)/shard_map/ppermute | solution.py:314
  17.3 5.9 %collective-permute-start.8 = (bf16[16,2048]{1,0:T(8,128)(2,1)S(1)}, bf16[16,2048]{1,0:T(8,128)(2,1)S(1)}, u32[]{:S(2)}, u32[]{:S(2)}) collective-permute-start(bf16[16,2048]{1,0:T(8,128)(2,1)S(1)} %broadcast_select_fusion.17), channel_id=1, source_target_pairs={{0,4},{4,12},{12,8},{8,0},{1,5},{5,13},{13,9},{9,1},{2,6},{6,14},{... | collective-permute-start | bytes 196616 | tf_op jit(solution)/shard_map/ppermute | solution.py:314
  18.7 5.9 %collective-permute-start.7 = (bf16[16,2048]{1,0:T(8,128)(2,1)S(1)}, bf16[16,2048]{1,0:T(8,128)(2,1)S(1)}, u32[]{:S(2)}, u32[]{:S(2)}) collective-permute-start(bf16[16,2048]{1,0:T(8,128)(2,1)S(1)} %broadcast_select_fusion.16), channel_id=1, source_target_pairs={{0,4},{4,12},{12,8},{8,0},{1,5},{5,13},{13,9},{9,1},{2,6},{6,14},{... | collective-permute-start | bytes 196616 | tf_op jit(solution)/shard_map/ppermute | solution.py:314
  20.1 25.2 %copy-start.2 = (bf16[128,256]{1,0:T(8,128)(2,1)S(1)}, bf16[128,256]{1,0:T(8,128)(2,1)}, u32[]{:S(2)}) copy-start(bf16[128,256]{1,0:T(8,128)(2,1)} %refs_5_.1) | copy-start | bytes 196612
  20.1 25.2 %copy-start.3 = (bf16[128,256]{1,0:T(8,128)(2,1)S(1)}, bf16[128,256]{1,0:T(8,128)(2,1)}, u32[]{:S(2)}) copy-start(bf16[128,256]{1,0:T(8,128)(2,1)} %refs_6_.1) | copy-start | bytes 196612
  20.1 5.9 %collective-permute-start.6 = (bf16[16,2048]{1,0:T(8,128)(2,1)S(1)}, bf16[16,2048]{1,0:T(8,128)(2,1)S(1)}, u32[]{:S(2)}, u32[]{:S(2)}) collective-permute-start(bf16[16,2048]{1,0:T(8,128)(2,1)S(1)} %broadcast_select_fusion.15), channel_id=1, source_target_pairs={{0,4},{4,12},{12,8},{8,0},{1,5},{5,13},{13,9},{9,1},{2,6},{6,14},{... | collective-permute-start | bytes 196616 | tf_op jit(solution)/shard_map/ppermute | solution.py:314
  21.9 5.9 %collective-permute-start.11 = (bf16[16,2048]{1,0:T(8,128)(2,1)S(1)}, bf16[16,2048]{1,0:T(8,128)(2,1)S(1)}, u32[]{:S(2)}, u32[]{:S(2)}) collective-permute-start(bf16[16,2048]{1,0:T(8,128)(2,1)S(1)} %broadcast_select_fusion.14), channel_id=1, source_target_pairs={{0,4},{4,12},{12,8},{8,0},{1,5},{5,13},{13,9},{9,1},{2,6},{6,14},{... | collective-permute-start | bytes 196616 | tf_op jit(solution)/shard_map/ppermute | solution.py:314
  23.3 6.0 %collective-permute-start.13 = (bf16[16,2048]{1,0:T(8,128)(2,1)S(1)}, bf16[16,2048]{1,0:T(8,128)(2,1)S(1)}, u32[]{:S(2)}, u32[]{:S(2)}) collective-permute-start(bf16[16,2048]{1,0:T(8,128)(2,1)S(1)} %broadcast_select_fusion.13), channel_id=1, source_target_pairs={{0,4},{4,12},{12,8},{8,0},{1,5},{5,13},{13,9},{9,1},{2,6},{6,14},{... | collective-permute-start | bytes 196616 | tf_op jit(solution)/shard_map/ppermute | solution.py:314
  24.7 6.7 %collective-permute-start.15 = (bf16[16,2048]{1,0:T(8,128)(2,1)S(1)}, bf16[16,2048]{1,0:T(8,128)(2,1)S(1)}, u32[]{:S(2)}, u32[]{:S(2)}) collective-permute-start(bf16[16,2048]{1,0:T(8,128)(2,1)S(1)} %broadcast_select_fusion.12), channel_id=1, source_target_pairs={{0,4},{4,12},{12,8},{8,0},{1,5},{5,13},{13,9},{9,1},{2,6},{6,14},{... | collective-permute-start | bytes 196616 | tf_op jit(solution)/shard_map/ppermute | solution.py:314
  26.1 6.6 %collective-permute-start.10 = (bf16[16,2048]{1,0:T(8,128)(2,1)S(1)}, bf16[16,2048]{1,0:T(8,128)(2,1)S(1)}, u32[]{:S(2)}, u32[]{:S(2)}) collective-permute-start(bf16[16,2048]{1,0:T(8,128)(2,1)S(1)} %broadcast_select_fusion.11), channel_id=1, source_target_pairs={{0,4},{4,12},{12,8},{8,0},{1,5},{5,13},{13,9},{9,1},{2,6},{6,14},{... | collective-permute-start | bytes 196616 | tf_op jit(solution)/shard_map/ppermute | solution.py:314
  27.9 5.9 %collective-permute-start.12 = (bf16[16,2048]{1,0:T(8,128)(2,1)S(1)}, bf16[16,2048]{1,0:T(8,128)(2,1)S(1)}, u32[]{:S(2)}, u32[]{:S(2)}) collective-permute-start(bf16[16,2048]{1,0:T(8,128)(2,1)S(1)} %broadcast_select_fusion.10), channel_id=1, source_target_pairs={{0,4},{4,12},{12,8},{8,0},{1,5},{5,13},{13,9},{9,1},{2,6},{6,14},{... | collective-permute-start | bytes 196616 | tf_op jit(solution)/shard_map/ppermute | solution.py:314
  29.3 5.9 %collective-permute-start.14 = (bf16[16,2048]{1,0:T(8,128)(2,1)S(1)}, bf16[16,2048]{1,0:T(8,128)(2,1)S(1)}, u32[]{:S(2)}, u32[]{:S(2)}) collective-permute-start(bf16[16,2048]{1,0:T(8,128)(2,1)S(1)} %broadcast_select_fusion.9), channel_id=1, source_target_pairs={{0,4},{4,12},{12,8},{8,0},{1,5},{5,13},{13,9},{9,1},{2,6},{6,14},{... | collective-permute-start | bytes 196616 | tf_op jit(solution)/shard_map/ppermute | solution.py:314
  31.4 5.7 %collective-permute-start.16 = (bf16[16,2048]{1,0:T(8,128)(2,1)S(1)}, bf16[16,2048]{1,0:T(8,128)(2,1)S(1)}, u32[]{:S(2)}, u32[]{:S(2)}) collective-permute-start(bf16[16,2048]{1,0:T(8,128)(2,1)S(1)} %broadcast_select_fusion.8), channel_id=1, source_target_pairs={{0,4},{4,12},{12,8},{8,0},{1,5},{5,13},{13,9},{9,1},{2,6},{6,14},{... | collective-permute-start | bytes 196616 | tf_op jit(solution)/shard_map/ppermute | solution.py:314
  32.6 5.8 %collective-permute-start.17 = (bf16[16,2048]{1,0:T(8,128)(2,1)S(1)}, bf16[16,2048]{1,0:T(8,128)(2,1)S(1)}, u32[]{:S(2)}, u32[]{:S(2)}) collective-permute-start(bf16[16,2048]{1,0:T(8,128)(2,1)S(1)} %broadcast_select_fusion.7), channel_id=1, source_target_pairs={{0,4},{4,12},{12,8},{8,0},{1,5},{5,13},{13,9},{9,1},{2,6},{6,14},{... | collective-permute-start | bytes 196616 | tf_op jit(solution)/shard_map/ppermute | solution.py:314
  33.8 5.7 %collective-permute-start.18 = (bf16[16,2048]{1,0:T(8,128)(2,1)S(1)}, bf16[16,2048]{1,0:T(8,128)(2,1)S(1)}, u32[]{:S(2)}, u32[]{:S(2)}) collective-permute-start(bf16[16,2048]{1,0:T(8,128)(2,1)S(1)} %broadcast_select_fusion.6), channel_id=1, source_target_pairs={{0,4},{4,12},{12,8},{8,0},{1,5},{5,13},{13,9},{9,1},{2,6},{6,14},{... | collective-permute-start | bytes 196616 | tf_op jit(solution)/shard_map/ppermute | solution.py:314
  35.2 5.7 %collective-permute-start.19 = (bf16[16,2048]{1,0:T(8,128)(2,1)S(1)}, bf16[16,2048]{1,0:T(8,128)(2,1)S(1)}, u32[]{:S(2)}, u32[]{:S(2)}) collective-permute-start(bf16[16,2048]{1,0:T(8,128)(2,1)S(1)} %broadcast_select_fusion.5), channel_id=1, source_target_pairs={{0,4},{4,12},{12,8},{8,0},{1,5},{5,13},{13,9},{9,1},{2,6},{6,14},{... | collective-permute-start | bytes 196616 | tf_op jit(solution)/shard_map/ppermute | solution.py:314
  37.0 22.4 %copy-start.1 = (bf16[128,2048]{1,0:T(8,128)(2,1)S(1)}, bf16[128,2048]{1,0:T(8,128)(2,1)}, u32[]{:S(2)}) copy-start(bf16[128,2048]{1,0:T(8,128)(2,1)} %refs_17_.1) | copy-start | bytes 1572868
  37.0 3.9 %collective-permute-start.27 = (f32[128,128]{1,0:T(8,128)S(1)}, f32[128,128]{1,0:T(8,128)S(1)}, u32[]{:S(2)}, u32[]{:S(2)}) collective-permute-start(f32[128,128]{1,0:T(8,128)S(1)} %shard_map.134), channel_id=1, source_target_pairs={{0,1},{1,0},{2,3},{3,2},{4,5},{5,4},{6,7},{7,6},{8,9},{9,8},{10,11... | collective-permute-start | bytes 196616 | tf_op jit(solution)/shard_map/ppermute | solution.py:63
  37.1 10.1 %collective-permute-start.20 = (bf16[16,2048]{1,0:T(8,128)(2,1)S(1)}, bf16[16,2048]{1,0:T(8,128)(2,1)S(1)}, u32[]{:S(2)}, u32[]{:S(2)}) collective-permute-start(bf16[16,2048]{1,0:T(8,128)(2,1)S(1)} %broadcast_select_fusion.4), channel_id=1, source_target_pairs={{0,4},{4,12},{12,8},{8,0},{1,5},{5,13},{13,9},{9,1},{2,6},{6,14},{... | collective-permute-start | bytes 196616 | tf_op jit(solution)/shard_map/ppermute | solution.py:314
  38.5 11.8 %collective-permute-start.21 = (bf16[16,2048]{1,0:T(8,128)(2,1)S(1)}, bf16[16,2048]{1,0:T(8,128)(2,1)S(1)}, u32[]{:S(2)}, u32[]{:S(2)}) collective-permute-start(bf16[16,2048]{1,0:T(8,128)(2,1)S(1)} %broadcast_select_fusion.3), channel_id=1, source_target_pairs={{0,4},{4,12},{12,8},{8,0},{1,5},{5,13},{13,9},{9,1},{2,6},{6,14},{... | collective-permute-start | bytes 196616 | tf_op jit(solution)/shard_map/ppermute | solution.py:314
  39.5 8.5 %collective-permute-start.22 = (bf16[16,2048]{1,0:T(8,128)(2,1)S(1)}, bf16[16,2048]{1,0:T(8,128)(2,1)S(1)}, u32[]{:S(2)}, u32[]{:S(2)}) collective-permute-start(bf16[16,2048]{1,0:T(8,128)(2,1)S(1)} %broadcast_select_fusion.2), channel_id=1, source_target_pairs={{0,4},{4,12},{12,8},{8,0},{1,5},{5,13},{13,9},{9,1},{2,6},{6,14},{... | collective-permute-start | bytes 196616 | tf_op jit(solution)/shard_map/ppermute | solution.py:314
  40.9 4.3 %collective-permute-start.28 = (f32[128,128]{1,0:T(8,128)S(1)}, f32[128,128]{1,0:T(8,128)S(1)}, u32[]{:S(2)}, u32[]{:S(2)}) collective-permute-start(f32[128,128]{1,0:T(8,128)S(1)} %add.208), channel_id=1, source_target_pairs={{0,2},{1,3},{2,0},{3,1},{4,6},{5,7},{6,4},{7,5},{8,10},{9,11},{10,... | collective-permute-start | bytes 196616 | tf_op jit(solution)/shard_map/ppermute | solution.py:63
  42.5 9.5 %collective-permute-start.23 = (bf16[16,2048]{1,0:T(8,128)(2,1)S(1)}, bf16[16,2048]{1,0:T(8,128)(2,1)S(1)}, u32[]{:S(2)}, u32[]{:S(2)}) collective-permute-start(bf16[16,2048]{1,0:T(8,128)(2,1)S(1)} %broadcast_select_fusion.1), channel_id=1, source_target_pairs={{0,4},{4,12},{12,8},{8,0},{1,5},{5,13},{13,9},{9,1},{2,6},{6,14},{... | collective-permute-start | bytes 196616 | tf_op jit(solution)/shard_map/ppermute | solution.py:314
  45.6 10.9 %collective-permute-start.30 = (bf16[128,512]{1,0:T(8,128)(2,1)S(1)}, bf16[128,512]{1,0:T(8,128)(2,1)S(1)}, u32[]{:S(2)}, u32[]{:S(2)}) collective-permute-start(bf16[128,512]{1,0:T(8,128)(2,1)S(1)} %shard_map.135), channel_id=1, source_target_pairs={{4,0},{12,4},{8,12},{0,8},{5,1},{13,5},{9,13},{1,9},{6,2},{14,6},{... | collective-permute-start | bytes 393224 | tf_op jit(solution)/shard_map/ppermute | solution.py:376
  47.2 12.0 %collective-permute-start.29 = (bf16[128,512]{1,0:T(8,128)(2,1)S(1)}, bf16[128,512]{1,0:T(8,128)(2,1)S(1)}, u32[]{:S(2)}, u32[]{:S(2)}) collective-permute-start(bf16[128,512]{1,0:T(8,128)(2,1)S(1)} %shard_map.135), channel_id=1, source_target_pairs={{0,4},{4,12},{12,8},{8,0},{1,5},{5,13},{13,9},{9,1},{2,6},{6,14},{... | collective-permute-start | bytes 393224 | tf_op jit(solution)/shard_map/ppermute | solution.py:375
  48.0 8.2 %collective-permute-start.24 = (bf16[16,2048]{1,0:T(8,128)(2,1)S(1)}, bf16[16,2048]{1,0:T(8,128)(2,1)S(1)}, u32[]{:S(2)}, u32[]{:S(2)}) collective-permute-start(bf16[16,2048]{1,0:T(8,128)(2,1)S(1)} %broadcast_select_fusion), channel_id=1, source_target_pairs={{0,4},{4,12},{12,8},{8,0},{1,5},{5,13},{13,9},{9,1},{2,6},{6,14},{... | collective-permute-start | bytes 196616 | tf_op jit(solution)/shard_map/ppermute | solution.py:314
  50.3 1.3 %collective-permute-start.25 = (f32[128,64]{1,0:T(8,128)S(1)}, f32[128,64]{1,0:T(8,128)S(1)}, u32[]{:S(2)}, u32[]{:S(2)}) collective-permute-start(f32[128,64]{1,0:T(8,128)S(1)} %shard_map.132), channel_id=1, source_target_pairs={{0,1},{1,0},{2,3},{3,2},{4,5},{5,4},{6,7},{7,6},{8,9},{9,8},{10,11... | collective-permute-start | bytes 98312 | tf_op jit(solution)/shard_map/ppermute | solution.py:63
  51.6 15.1 %collective-permute-start.33 = (bf16[32,2048]{1,0:T(8,128)(2,1)S(1)}, bf16[32,2048]{1,0:T(8,128)(2,1)S(1)}, u32[]{:S(2)}, u32[]{:S(2)}) collective-permute-start(bf16[32,2048]{1,0:T(8,128)(2,1)S(1)} %pad_maximum_fusion.1), channel_id=1, source_target_pairs={{0,4},{4,12},{12,8},{8,0},{1,5},{5,13},{13,9},{9,1},{2,6},{6,14},{... | collective-permute-start | bytes 393224 | tf_op jit(solution)/shard_map/ppermute | solution.py:322
  52.0 7.3 %collective-permute-start.26 = (f32[128,64]{1,0:T(8,128)S(1)}, f32[128,64]{1,0:T(8,128)S(1)}, u32[]{:S(2)}, u32[]{:S(2)}) collective-permute-start(f32[128,64]{1,0:T(8,128)S(1)} %add.179), channel_id=1, source_target_pairs={{0,2},{1,3},{2,0},{3,1},{4,6},{5,7},{6,4},{7,5},{8,10},{9,11},{10,... | collective-permute-start | bytes 98312 | tf_op jit(solution)/shard_map/ppermute | solution.py:63
  56.2 10.5 %collective-permute-start.34 = (bf16[32,2048]{1,0:T(8,128)(2,1)S(1)}, bf16[32,2048]{1,0:T(8,128)(2,1)S(1)}, u32[]{:S(2)}, u32[]{:S(2)}) collective-permute-start(bf16[32,2048]{1,0:T(8,128)(2,1)S(1)} %pad_maximum_fusion.2), channel_id=1, source_target_pairs={{0,4},{4,12},{12,8},{8,0},{1,5},{5,13},{13,9},{9,1},{2,6},{6,14},{... | collective-permute-start | bytes 393224 | tf_op jit(solution)/shard_map/ppermute | solution.py:322
  56.5 6.9 %collective-permute-start.32 = (bf16[128,256]{1,0:T(8,128)(2,1)S(1)}, bf16[128,256]{1,0:T(8,128)(2,1)S(1)}, u32[]{:S(2)}, u32[]{:S(2)}) collective-permute-start(bf16[128,256]{1,0:T(8,128)(2,1)S(1)} %get-tuple-element.105.refs_6_), channel_id=1, source_target_pairs={{4,0},{12,4},{8,12},{0,8},{5,1},{13,5},{9,13},{1,9},{6,2},{14,6},{... | collective-permute-start | bytes 196616 | tf_op jit(solution)/shard_map/ppermute | solution.py:383
  59.3 5.2 %collective-permute-start.31 = (bf16[128,256]{1,0:T(8,128)(2,1)S(1)}, bf16[128,256]{1,0:T(8,128)(2,1)S(1)}, u32[]{:S(2)}, u32[]{:S(2)}) collective-permute-start(bf16[128,256]{1,0:T(8,128)(2,1)S(1)} %get-tuple-element.110.refs_0_), channel_id=1, source_target_pairs={{0,4},{4,12},{12,8},{8,0},{1,5},{5,13},{13,9},{9,1},{2,6},{6,14},{... | collective-permute-start | bytes 196616 | tf_op jit(solution)/shard_map/ppermute | solution.py:381
  67.1 1.2 %collective-permute-start.37 = (bf16[64,128]{1,0:T(8,128)(2,1)S(1)}, bf16[64,128]{1,0:T(8,128)(2,1)S(1)}, u32[]{:S(2)}, u32[]{:S(2)}) collective-permute-start(bf16[64,128]{1,0:T(8,128)(2,1)S(1)} %convert_element_type.26), channel_id=1, source_target_pairs={{0,1},{1,0},{2,3},{3,2},{4,5},{5,4},{6,7},{7,6},{8,9},{9,8},{10,11... | collective-permute-start | bytes 49160 | tf_op jit(solution)/shard_map/ppermute | solution.py:63
  68.3 4.7 %collective-permute-start.38 = (bf16[64,128]{1,0:T(8,128)(2,1)S(1)}, bf16[64,128]{1,0:T(8,128)(2,1)S(1)}, u32[]{:S(2)}, u32[]{:S(2)}) collective-permute-start(bf16[64,128]{1,0:T(8,128)(2,1)S(1)} %add_convert_fusion), channel_id=1, source_target_pairs={{0,2},{1,3},{2,0},{3,1},{4,6},{5,7},{6,4},{7,5},{8,10},{9,11},{10,... | collective-permute-start | bytes 49160 | tf_op jit(solution)/shard_map/ppermute | solution.py:63
  69.9 7.3 %collective-permute-start.35 = (bf16[32,2048]{1,0:T(8,128)(2,1)S(1)}, bf16[32,2048]{1,0:T(8,128)(2,1)S(1)}, u32[]{:S(2)}, u32[]{:S(2)}) collective-permute-start(bf16[32,2048]{1,0:T(8,128)(2,1)S(1)} %collective-permute-done.33.refs_0_), channel_id=1, source_target_pairs={{0,4},{4,12},{12,8},{8,0},{1,5},{5,13},{13,9},{9,1},{2,6},{6,14},{... | collective-permute-start | bytes 393224 | tf_op jit(solution)/shard_map/ppermute | solution.py:322
  70.7 8.2 %collective-permute-start.36 = (bf16[32,2048]{1,0:T(8,128)(2,1)S(1)}, bf16[32,2048]{1,0:T(8,128)(2,1)S(1)}, u32[]{:S(2)}, u32[]{:S(2)}) collective-permute-start(bf16[32,2048]{1,0:T(8,128)(2,1)S(1)} %collective-permute-done.34.refs_1_), channel_id=1, source_target_pairs={{0,4},{4,12},{12,8},{8,0},{1,5},{5,13},{13,9},{9,1},{2,6},{6,14},{... | collective-permute-start | bytes 393224 | tf_op jit(solution)/shard_map/ppermute | solution.py:322
